TPU v7x, 128 devices: a whole 4x4x4 slice. The times are simulated.
128 devices in a mesh: band: 32 (over z, x, core), lev: 4 (over y).
Axes of the slice: x: 4, y: 4, z: 4, core: 2. Of those that a mesh axis runs over, the one named last changes fastest.
Arguments:
- air_fourier_coefficients: float32 [4, 16, 1280, 256], P('lev', None, 'band'), may hold values from -6 to 6
- quadrature_factor: float32 [1280], P('band'), may hold values from 0.5 to 1.5
- associated_polynomial_table: bfloat16 [128, 1280, 1280], P('band'), may hold values from -6 to 6
- east_west_harmonic: int32 [128], replicated, may hold values from 0 to 1279, as said below
- boundary_diffusion: float32 [4, 16, 16, 1280], P('lev', None, None, 'band'), may hold values from -0.25 to 0.25
- bulk_transfer_coefficient: float32 [4, 1280], P('lev', 'band'), may hold values from 0.1 to 1
- skin_heat_earlier: float32 [12, 4, 1280, 256], P(None, 'lev', 'band'), may hold values from -6 to 6
- sea_boundary_values: float32 [4, 1024, 1440], P('lev', 'band'), may hold values from -6 to 6
- sea_damping_speed: float32 [4, 1024, 1440], P('lev', 'band'), may hold values from 0.02 to 2
- sea_coupling_matrix: float32 [4, 4], replicated, may hold values from -1.75 to 1.75
- patch_active_entries: int32 [32], P('band'), may hold values from 8 to 32, as said below
- sea_southern_parallel: int32 [1024], P('band'), may hold values from 0 to 1278, as said below
- sea_northern_share: float32 [1024], P('band'), may hold values from 0 to 1
- air_paired_cells: int32 [2, 1280], P(None, 'band'), may hold values from 0 to 1023, as said below
- air_second_share: float32 [1280], P('band'), may hold values from 0 to 1
Outputs:
- air_coefficients_end: float32 [4, 16, 1280, 256], P('lev', None, 'band')
- sea_values_end: float32 [4, 1024, 1440], P('lev', 'band')
- skin_heat_newest: float32 [12, 4, 1280, 256], P(None, 'lev', 'band')
Inputs may be any that keep to these rules, and one draw needn't show every extreme that they name: `east_west_harmonic`: Distinct; positions 2 j and 2 j + 1 hold m and 1279 - m for some m below 640; 0 is among them. `patch_active_entries`: the live slots of a tile come first; the last tile is full. For a slot of tile t, sea_southern_parallel and sea_southern_parallel + 1 lie in t * 40 - 8 to (t + 1) * 40 + 7; they do not decrease along a tile's live slots. `air_paired_cells`: for a latitude of band t both taps are live slots of tiles t - 1, t or t + 1, the first one of tile t, and the two differ.
All inputs are finite; a program needn't handle non-finite values.
Results may differ from a plain program's by a relative error of at most 0.014.
Values may be sent and summed in bfloat16 or wider, within the bound.
No kernel may reach another device: no remote copies, remote signals or barrier semaphores. Data moves between devices by JAX's collectives and lax.ppermute only.
A program may use at most 64 MiB of HBM per device.

v0:
```python
import math

import jax
import jax.numpy as jnp
from jax import lax
from jax.sharding import PartitionSpec as P

PARALLEL_NUMBER = 1280
MARG = 8


degree_damping = 2e-06
ocean_step = 0.5
mixing_diagonal = 0.95
synth_divisor = 4.0


def with_halo(shard, sides, width):
    for axis, dim in sides:
        size, length = (lax.axis_size(axis), shard.shape[dim])
        up = [(i, (i + 1) % size) for i in range(size - 1)]
        down = [(j, i) for i, j in up]
        last = lax.slice_in_dim(shard, length - width, length, axis=dim)
        first = lax.slice_in_dim(shard, 0, width, axis=dim)
        before = lax.ppermute(last, axis, up)
        after = lax.ppermute(first, axis, down)
        shard = jnp.concatenate([before, shard, after], axis=dim)
    return shard


def damping_table(wave_values, degree_count):
    degrees = wave_values[:, None] + jnp.arange(degree_count, dtype=jnp.int32)[None, :]
    degree_float = degrees.astype(jnp.float32)
    factor = 1.0 / (1.0 + degree_damping * degree_float * (degree_float + 1.0))
    return jnp.where(degrees < degree_count, factor, jnp.zeros_like(factor))


def zonal_table(wave_values, lon_count):
    longitude = jnp.arange(lon_count, dtype=jnp.int32)
    phases = wave_values[:, None] * longitude[None, :] % lon_count
    angles = phases.astype(jnp.float32) * (2.0 * math.pi / lon_count)
    stacked = jnp.stack([jnp.cos(angles), -jnp.sin(angles)], axis=1)
    return stacked.reshape(2 * wave_values.shape[0], lon_count).astype(jnp.bfloat16)


def padded_transform(values, tables, damping):
    row_count = values.shape[0]
    lat_count = values.shape[1]
    wave_count = tables.shape[0]
    shaped = values.reshape(row_count, lat_count, wave_count, 2)
    spectral = jnp.einsum("rlmc,mln->rmnc", shaped, tables, preferred_element_type=jnp.float32)
    damped = (spectral * damping[None, :, :, None]).astype(jnp.bfloat16)
    synthesis = jnp.einsum("rmnc,mln->rlmc", damped, tables, preferred_element_type=jnp.float32)
    synthesis = synthesis * (1.0 / (synth_divisor * math.sqrt(tables.shape[2])))
    return synthesis.astype(jnp.bfloat16).reshape(row_count, lat_count, wave_count * 2)


def per_device(
    air_fourier_coefficients,
    quadrature_factor,
    associated_polynomial_table,
    east_west_harmonic,
    boundary_diffusion,
    bulk_transfer_coefficient,
    skin_heat_earlier,
    sea_boundary_values,
    sea_damping_speed,
    sea_coupling_matrix,
    patch_active_entries,
    sea_southern_parallel,
    sea_northern_share,
    air_paired_cells,
    air_second_share,
):
    band_index = lax.axis_index("band")
    lev_index = lax.axis_index("lev")
    field_local = air_fourier_coefficients.shape[0]
    height_pile = air_fourier_coefficients.shape[1]
    lat_local = air_fourier_coefficients.shape[2]
    column_count = air_fourier_coefficients.shape[3]
    row_count = field_local * height_pile
    owned = associated_polynomial_table.shape[0]
    degree_count = associated_polynomial_table.shape[2]
    wave_values = lax.dynamic_slice_in_dim(east_west_harmonic, band_index * owned, owned, 0)
    damping = damping_table(wave_values, degree_count)

    def transform(values):
        return padded_transform(values, associated_polynomial_table, damping)

    identity_block = jnp.eye(height_pile, dtype=jnp.float32)[None, :, :, None]
    mixing = (
        mixing_diagonal * identity_block
        + boundary_diffusion
        - jnp.transpose(boundary_diffusion, (0, 2, 1, 3))
    )
    weight = quadrature_factor * (1.0 / math.sqrt(PARALLEL_NUMBER))

    def march_air_model(air_model_present, skin_heat_present):
        scaled = (air_model_present * weight[None, None, :, None]).astype(jnp.bfloat16)
        scaled = scaled.reshape(row_count, lat_local, column_count)
        by_wave = lax.all_to_all(scaled, "band", split_axis=2, concat_axis=1, tiled=True)
        synthesis = transform(by_wave)
        returned = lax.all_to_all(synthesis, "band", split_axis=1, concat_axis=2, tiled=True)
        synthesis_field = returned.reshape(
            field_local, height_pile, lat_local, column_count
        ).astype(jnp.float32)
        halfway_point = air_model_present - synthesis_field
        bottom_sheet = bulk_transfer_coefficient[:, :, None] * (
            skin_heat_present - halfway_point[:, height_pile - 1]
        )
        mixed_state = jnp.einsum(
            "flpa,fpac->flac", mixing, halfway_point, precision=lax.Precision.HIGHEST
        )
        mixed_state = mixed_state.at[:, height_pile - 1].add(bottom_sheet)
        return (mixed_state, bottom_sheet.astype(jnp.bfloat16))

    air_coefficients_end, forcing_series = lax.scan(
        march_air_model, air_fourier_coefficients, skin_heat_earlier
    )
    slot_rows = sea_boundary_values.shape[1]
    extended = with_halo(forcing_series, (("band", 2),), MARG)
    rim_rows = lat_local + 2 * MARG
    lowest = band_index * lat_local - MARG
    live_slot = jnp.arange(slot_rows, dtype=jnp.int32) < patch_active_entries[0]
    offsets = (sea_southern_parallel - lowest)[:, None]
    rim_index = jnp.arange(rim_rows, dtype=jnp.int32)[None, :]
    low_weight = jnp.where(live_slot, 1.0 - sea_northern_share, jnp.zeros_like(sea_northern_share))[
        :, None
    ]
    high_weight = jnp.where(live_slot, sea_northern_share, jnp.zeros_like(sea_northern_share))[
        :, None
    ]
    flux_taps = jnp.where(rim_index == offsets, low_weight, 0.0) + jnp.where(
        rim_index == offsets + 1, high_weight, 0.0
    )
    flux_taps = flux_taps.astype(jnp.bfloat16)
    ocean_flux = jnp.einsum(
        "sa,kfac->kfsc", flux_taps, extended, preferred_element_type=jnp.float32
    ).astype(jnp.bfloat16)
    lon_count = sea_boundary_values.shape[2]
    zonal_basis = zonal_table(east_west_harmonic, lon_count)
    synth_scale = 1.0 / math.sqrt(zonal_basis.shape[0])
    skew_full = sea_coupling_matrix - sea_coupling_matrix.T
    skew_mine = lax.dynamic_slice_in_dim(skew_full, lev_index * field_local, field_local, 0)

    def ocean_advance(ocean_now, flux_now):
        forcing = (
            jnp.einsum("fsc,cx->fsx", flux_now, zonal_basis, preferred_element_type=jnp.float32)
            * synth_scale
        )
        gathered = lax.all_gather(ocean_now.astype(jnp.bfloat16), "lev", axis=0, tiled=True)
        coupled = jnp.zeros_like(ocean_now)
        for field_index in range(gathered.shape[0]):
            coupled = (
                coupled
                + skew_mine[:, field_index][:, None, None]
                * gathered[field_index].astype(jnp.float32)[None]
            )
        updated = (ocean_now + ocean_step * (coupled - forcing)) / (
            1.0 + ocean_step * sea_damping_speed
        )
        return (updated, updated.astype(jnp.bfloat16))

    sea_values_end, ocean_wave = lax.scan(ocean_advance, sea_boundary_values, ocean_flux)
    ocean_coef = jnp.einsum(
        "kfsx,cx->kfsc", ocean_wave, zonal_basis, preferred_element_type=jnp.float32
    )
    ocean_coef = (ocean_coef * (1.0 / math.sqrt(lon_count))).astype(jnp.bfloat16)
    neighbours = with_halo(ocean_coef, (("band", 2),), slot_rows)
    base_slot = (band_index - 1) * slot_rows
    slot_index = jnp.arange(3 * slot_rows, dtype=jnp.int32)[None, :]
    first_local = (air_paired_cells[0] - base_slot)[:, None]
    second_local = (air_paired_cells[1] - base_slot)[:, None]
    return_taps = jnp.where(
        slot_index == first_local, (1.0 - air_second_share)[:, None], 0.0
    ) + jnp.where(slot_index == second_local, air_second_share[:, None], 0.0)
    return_taps = return_taps.astype(jnp.bfloat16)
    skin_heat_newest = jnp.einsum(
        "ga,kfac->kfgc", return_taps, neighbours, preferred_element_type=jnp.float32
    )
    return (air_coefficients_end, sea_values_end, skin_heat_newest)


def solution(mesh):
    return jax.shard_map(
        per_device,
        mesh=mesh,
        in_specs=(
            P("lev", None, "band", None),
            P("band"),
            P("band", None, None),
            P(),
            P("lev", None, None, "band"),
            P("lev", "band"),
            P(None, "lev", "band", None),
            P("lev", "band", None),
            P("lev", "band", None),
            P(),
            P("band"),
            P("band"),
            P("band"),
            P(None, "band"),
            P("band"),
        ),
        out_specs=(
            P("lev", None, "band", None),
            P("lev", "band", None),
            P(None, "lev", "band", None),
        ),
        check_vma=False,
    )
```

profile of v0, /device:TPU:32, one launch (start us, length us, event | category | flops | bytes accessed | tf_op | source)
XLA Modules:
  0.0 1151.3 jit_solution(6040955849517082085)
XLA Ops:
  4.1 916.1 %while.29 = (s32[]{:T(128)}, f32[1,16,40,256]{3,1,2,0:T(8,128)S(1)}, bf16[12,1,40,256]{3,2,1,0:T(8,128)(2,1)S(1)}, f32[40]{0:T(128)S(1)}, bf16[4,1280,1280]{2,1,...) while((s32[]{:T(128)}, ...), condition=%wide.region_1.2_spmd.clone, body=%wide.region_0.1_spmd.clone.sunk | while | flops 871552000 | bytes 31130164 | solution.py:117
  7.8 8.0 all-to-all-start
  16.0 7.9 all-to-all-done
  28.1 15.2 %fusion.110 = bf16[4,16,2,1280]{3,1,2,0:T(8,128)(2,1)} fusion(bf16[4,1280,1280]{2,1,0:T(8,128)(2,1)} %get-tuple-element.499, bf16[16,1280,4,2]{1,0,3,2:T(8,128)(2,1)S(1)} %reshape.391, f32[4,1280]{1,0:T(4,128)S(1)} %divide_select_fusion.2), kind=kOutput, calls=%fused_computation.17.clone.1 | convolution fusion | flops 839516160 | bytes 13783040 | tf_op jit(solution)/shard_map/while/body/eval_jaxpr/rmnc,mln->rlmc/dot_general | solution.py:53
  57.3 6.1 all-to-all-done.1
  92.0 8.0 all-to-all-done
  104.2 15.2 %fusion.110 = bf16[4,16,2,1280]{3,1,2,0:T(8,128)(2,1)} fusion(bf16[4,1280,1280]{2,1,0:T(8,128)(2,1)} %get-tuple-element.499, bf16[16,1280,4,2]{1,0,3,2:T(8,128)(2,1)S(1)} %reshape.391, f32[4,1280]{1,0:T(4,128)S(1)} %divide_select_fusion.2), kind=kOutput, calls=%fused_computation.17.clone.1 | convolution fusion | flops 839516160 | bytes 13783040 | tf_op jit(solution)/shard_map/while/body/eval_jaxpr/rmnc,mln->rlmc/dot_general | solution.py:53
  133.4 6.1 all-to-all-done.1
  168.1 8.0 all-to-all-done
  180.3 15.2 %fusion.110 = bf16[4,16,2,1280]{3,1,2,0:T(8,128)(2,1)} fusion(bf16[4,1280,1280]{2,1,0:T(8,128)(2,1)} %get-tuple-element.499, bf16[16,1280,4,2]{1,0,3,2:T(8,128)(2,1)S(1)} %reshape.391, f32[4,1280]{1,0:T(4,128)S(1)} %divide_select_fusion.2), kind=kOutput, calls=%fused_computation.17.clone.1 | convolution fusion | flops 839516160 | bytes 13783040 | tf_op jit(solution)/shard_map/while/body/eval_jaxpr/rmnc,mln->rlmc/dot_general | solution.py:53
  209.5 6.1 all-to-all-done.1
  244.2 8.0 all-to-all-done
  256.4 15.2 %fusion.110 = bf16[4,16,2,1280]{3,1,2,0:T(8,128)(2,1)} fusion(bf16[4,1280,1280]{2,1,0:T(8,128)(2,1)} %get-tuple-element.499, bf16[16,1280,4,2]{1,0,3,2:T(8,128)(2,1)S(1)} %reshape.391, f32[4,1280]{1,0:T(4,128)S(1)} %divide_select_fusion.2), kind=kOutput, calls=%fused_computation.17.clone.1 | convolution fusion | flops 839516160 | bytes 13783040 | tf_op jit(solution)/shard_map/while/body/eval_jaxpr/rmnc,mln->rlmc/dot_general | solution.py:53
  285.6 6.1 all-to-all-done.1
  320.3 8.0 all-to-all-done
  332.5 15.2 %fusion.110 = bf16[4,16,2,1280]{3,1,2,0:T(8,128)(2,1)} fusion(bf16[4,1280,1280]{2,1,0:T(8,128)(2,1)} %get-tuple-element.499, bf16[16,1280,4,2]{1,0,3,2:T(8,128)(2,1)S(1)} %reshape.391, f32[4,1280]{1,0:T(4,128)S(1)} %divide_select_fusion.2), kind=kOutput, calls=%fused_computation.17.clone.1 | convolution fusion | flops 839516160 | bytes 13783040 | tf_op jit(solution)/shard_map/while/body/eval_jaxpr/rmnc,mln->rlmc/dot_general | solution.py:53
  361.8 6.1 all-to-all-done.1
  396.4 8.0 all-to-all-done
  408.6 15.2 %fusion.110 = bf16[4,16,2,1280]{3,1,2,0:T(8,128)(2,1)} fusion(bf16[4,1280,1280]{2,1,0:T(8,128)(2,1)} %get-tuple-element.499, bf16[16,1280,4,2]{1,0,3,2:T(8,128)(2,1)S(1)} %reshape.391, f32[4,1280]{1,0:T(4,128)S(1)} %divide_select_fusion.2), kind=kOutput, calls=%fused_computation.17.clone.1 | convolution fusion | flops 839516160 | bytes 13783040 | tf_op jit(solution)/shard_map/while/body/eval_jaxpr/rmnc,mln->rlmc/dot_general | solution.py:53
  437.9 6.1 all-to-all-done.1
  472.5 8.0 all-to-all-done
  484.7 15.2 %fusion.110 = bf16[4,16,2,1280]{3,1,2,0:T(8,128)(2,1)} fusion(bf16[4,1280,1280]{2,1,0:T(8,128)(2,1)} %get-tuple-element.499, bf16[16,1280,4,2]{1,0,3,2:T(8,128)(2,1)S(1)} %reshape.391, f32[4,1280]{1,0:T(4,128)S(1)} %divide_select_fusion.2), kind=kOutput, calls=%fused_computation.17.clone.1 | convolution fusion | flops 839516160 | bytes 13783040 | tf_op jit(solution)/shard_map/while/body/eval_jaxpr/rmnc,mln->rlmc/dot_general | solution.py:53
  514.0 6.1 all-to-all-done.1
  548.6 8.0 all-to-all-done
  560.8 15.2 %fusion.110 = bf16[4,16,2,1280]{3,1,2,0:T(8,128)(2,1)} fusion(bf16[4,1280,1280]{2,1,0:T(8,128)(2,1)} %get-tuple-element.499, bf16[16,1280,4,2]{1,0,3,2:T(8,128)(2,1)S(1)} %reshape.391, f32[4,1280]{1,0:T(4,128)S(1)} %divide_select_fusion.2), kind=kOutput, calls=%fused_computation.17.clone.1 | convolution fusion | flops 839516160 | bytes 13783040 | tf_op jit(solution)/shard_map/while/body/eval_jaxpr/rmnc,mln->rlmc/dot_general | solution.py:53
  624.7 8.0 all-to-all-done
  636.9 15.2 %fusion.110 = bf16[4,16,2,1280]{3,1,2,0:T(8,128)(2,1)} fusion(bf16[4,1280,1280]{2,1,0:T(8,128)(2,1)} %get-tuple-element.499, bf16[16,1280,4,2]{1,0,3,2:T(8,128)(2,1)S(1)} %reshape.391, f32[4,1280]{1,0:T(4,128)S(1)} %divide_select_fusion.2), kind=kOutput, calls=%fused_computation.17.clone.1 | convolution fusion | flops 839516160 | bytes 13783040 | tf_op jit(solution)/shard_map/while/body/eval_jaxpr/rmnc,mln->rlmc/dot_general | solution.py:53
  666.2 6.1 all-to-all-done.1
  700.8 8.0 all-to-all-done
  713.0 15.2 %fusion.110 = bf16[4,16,2,1280]{3,1,2,0:T(8,128)(2,1)} fusion(bf16[4,1280,1280]{2,1,0:T(8,128)(2,1)} %get-tuple-element.499, bf16[16,1280,4,2]{1,0,3,2:T(8,128)(2,1)S(1)} %reshape.391, f32[4,1280]{1,0:T(4,128)S(1)} %divide_select_fusion.2), kind=kOutput, calls=%fused_computation.17.clone.1 | convolution fusion | flops 839516160 | bytes 13783040 | tf_op jit(solution)/shard_map/while/body/eval_jaxpr/rmnc,mln->rlmc/dot_general | solution.py:53
  742.3 6.1 all-to-all-done.1
  776.9 8.0 all-to-all-done
  789.1 15.2 %fusion.110 = bf16[4,16,2,1280]{3,1,2,0:T(8,128)(2,1)} fusion(bf16[4,1280,1280]{2,1,0:T(8,128)(2,1)} %get-tuple-element.499, bf16[16,1280,4,2]{1,0,3,2:T(8,128)(2,1)S(1)} %reshape.391, f32[4,1280]{1,0:T(4,128)S(1)} %divide_select_fusion.2), kind=kOutput, calls=%fused_computation.17.clone.1 | convolution fusion | flops 839516160 | bytes 13783040 | tf_op jit(solution)/shard_map/while/body/eval_jaxpr/rmnc,mln->rlmc/dot_general | solution.py:53
  853.1 8.0 all-to-all-done
  865.2 15.2 %fusion.110 = bf16[4,16,2,1280]{3,1,2,0:T(8,128)(2,1)} fusion(bf16[4,1280,1280]{2,1,0:T(8,128)(2,1)} %get-tuple-element.499, bf16[16,1280,4,2]{1,0,3,2:T(8,128)(2,1)S(1)} %reshape.391, f32[4,1280]{1,0:T(4,128)S(1)} %divide_select_fusion.2), kind=kOutput, calls=%fused_computation.17.clone.1 | convolution fusion | flops 839516160 | bytes 13783040 | tf_op jit(solution)/shard_map/while/body/eval_jaxpr/rmnc,mln->rlmc/dot_general | solution.py:53
  935.9 202.9 %while.28 = (s32[]{:T(128)}, f32[1,32,1440]{2,1,0:T(8,128)S(1)}, bf16[12,1,32,1440]{3,2,1,0:T(8,128)(2,1)S(1)}, f32[1,4]{1,0:T(1,128)S(1)}, bf16[12,1,32,256]{3,...) while((s32[]{:T(128)}, f32[1,32,1440]{2,1,0:T(8,128)S(1)}, ...), condition=%wide.region_3.4_spmd, body=%wide.region_2.3_spmd.sunk | while | flops 24514560 | bytes 2624629 | solution.py:164
  936.6 13.2 %all_gather.4 = bf16[4,32,1440]{2,1,0:T(8,128)(2,1)S(1)} all-gather(bf16[1,32,1440]{2,1,0:T(8,128)(2,1)S(1)} %convert_element_type.206), channel_id=1, replica_groups=mesh['band'=32,'lev'=4] {'lev'}, dimensions={0}, use_global_device_ids=true | all-gather | bytes 460800 | tf_op jit(solution)/shard_map/while/body/eval_jaxpr/all_gather | solution.py:151
  954.0 12.5 %all_gather.4 = bf16[4,32,1440]{2,1,0:T(8,128)(2,1)S(1)} all-gather(bf16[1,32,1440]{2,1,0:T(8,128)(2,1)S(1)} %convert_element_type.206), channel_id=1, replica_groups=mesh['band'=32,'lev'=4] {'lev'}, dimensions={0}, use_global_device_ids=true | all-gather | bytes 460800 | tf_op jit(solution)/shard_map/while/body/eval_jaxpr/all_gather | solution.py:151
  970.8 12.5 %all_gather.4 = bf16[4,32,1440]{2,1,0:T(8,128)(2,1)S(1)} all-gather(bf16[1,32,1440]{2,1,0:T(8,128)(2,1)S(1)} %convert_element_type.206), channel_id=1, replica_groups=mesh['band'=32,'lev'=4] {'lev'}, dimensions={0}, use_global_device_ids=true | all-gather | bytes 460800 | tf_op jit(solution)/shard_map/while/body/eval_jaxpr/all_gather | solution.py:151
  987.5 12.5 %all_gather.4 = bf16[4,32,1440]{2,1,0:T(8,128)(2,1)S(1)} all-gather(bf16[1,32,1440]{2,1,0:T(8,128)(2,1)S(1)} %convert_element_type.206), channel_id=1, replica_groups=mesh['band'=32,'lev'=4] {'lev'}, dimensions={0}, use_global_device_ids=true | all-gather | bytes 460800 | tf_op jit(solution)/shard_map/while/body/eval_jaxpr/all_gather | solution.py:151
  1004.3 12.8 %all_gather.4 = bf16[4,32,1440]{2,1,0:T(8,128)(2,1)S(1)} all-gather(bf16[1,32,1440]{2,1,0:T(8,128)(2,1)S(1)} %convert_element_type.206), channel_id=1, replica_groups=mesh['band'=32,'lev'=4] {'lev'}, dimensions={0}, use_global_device_ids=true | all-gather | bytes 460800 | tf_op jit(solution)/shard_map/while/body/eval_jaxpr/all_gather | solution.py:151
  1021.3 12.8 %all_gather.4 = bf16[4,32,1440]{2,1,0:T(8,128)(2,1)S(1)} all-gather(bf16[1,32,1440]{2,1,0:T(8,128)(2,1)S(1)} %convert_element_type.206), channel_id=1, replica_groups=mesh['band'=32,'lev'=4] {'lev'}, dimensions={0}, use_global_device_ids=true | all-gather | bytes 460800 | tf_op jit(solution)/shard_map/while/body/eval_jaxpr/all_gather | solution.py:151
  1038.3 12.5 %all_gather.4 = bf16[4,32,1440]{2,1,0:T(8,128)(2,1)S(1)} all-gather(bf16[1,32,1440]{2,1,0:T(8,128)(2,1)S(1)} %convert_element_type.206), channel_id=1, replica_groups=mesh['band'=32,'lev'=4] {'lev'}, dimensions={0}, use_global_device_ids=true | all-gather | bytes 460800 | tf_op jit(solution)/shard_map/while/body/eval_jaxpr/all_gather | solution.py:151
  1055.0 12.5 %all_gather.4 = bf16[4,32,1440]{2,1,0:T(8,128)(2,1)S(1)} all-gather(bf16[1,32,1440]{2,1,0:T(8,128)(2,1)S(1)} %convert_element_type.206), channel_id=1, replica_groups=mesh['band'=32,'lev'=4] {'lev'}, dimensions={0}, use_global_device_ids=true | all-gather | bytes 460800 | tf_op jit(solution)/shard_map/while/body/eval_jaxpr/all_gather | solution.py:151
  1071.8 12.5 %all_gather.4 = bf16[4,32,1440]{2,1,0:T(8,128)(2,1)S(1)} all-gather(bf16[1,32,1440]{2,1,0:T(8,128)(2,1)S(1)} %convert_element_type.206), channel_id=1, replica_groups=mesh['band'=32,'lev'=4] {'lev'}, dimensions={0}, use_global_device_ids=true | all-gather | bytes 460800 | tf_op jit(solution)/shard_map/while/body/eval_jaxpr/all_gather | solution.py:151
  1088.5 13.1 %all_gather.4 = bf16[4,32,1440]{2,1,0:T(8,128)(2,1)S(1)} all-gather(bf16[1,32,1440]{2,1,0:T(8,128)(2,1)S(1)} %convert_element_type.206), channel_id=1, replica_groups=mesh['band'=32,'lev'=4] {'lev'}, dimensions={0}, use_global_device_ids=true | all-gather | bytes 460800 | tf_op jit(solution)/shard_map/while/body/eval_jaxpr/all_gather | solution.py:151
  1105.9 12.6 %all_gather.4 = bf16[4,32,1440]{2,1,0:T(8,128)(2,1)S(1)} all-gather(bf16[1,32,1440]{2,1,0:T(8,128)(2,1)S(1)} %convert_element_type.206), channel_id=1, replica_groups=mesh['band'=32,'lev'=4] {'lev'}, dimensions={0}, use_global_device_ids=true | all-gather | bytes 460800 | tf_op jit(solution)/shard_map/while/body/eval_jaxpr/all_gather | solution.py:151
  1122.8 12.5 %all_gather.4 = bf16[4,32,1440]{2,1,0:T(8,128)(2,1)S(1)} all-gather(bf16[1,32,1440]{2,1,0:T(8,128)(2,1)S(1)} %convert_element_type.206), channel_id=1, replica_groups=mesh['band'=32,'lev'=4] {'lev'}, dimensions={0}, use_global_device_ids=true | all-gather | bytes 460800 | tf_op jit(solution)/shard_map/while/body/eval_jaxpr/all_gather | solution.py:151
  (397 shorter events, 654.7 us)
Async XLA Ops:
  0.6 2.4 copy-start.4
  0.6 2.6 copy-start.12
  0.7 2.6 copy-start.8
  3.0 1.1 copy-start.5
  4.1 927.8 %copy-start.6 = (f32[4,4]{1,0:T(4,128)S(1)}, f32[4,4]{1,0:T(4,128)}, u32[]{:S(2)}) copy-start(f32[4,4]{1,0:T(4,128)} %param.30) | copy-start | bytes 196
  4.1 927.9 %copy-start.9 = (s32[32]{0:T(128)S(1)}, s32[32]{0:T(128)}, u32[]{:S(2)}) copy-start(s32[32]{0:T(128)} %param.32) | copy-start | bytes 388
  4.1 927.9 %copy-start.10 = (f32[32]{0:T(128)S(1)}, f32[32]{0:T(128)}, u32[]{:S(2)}) copy-start(f32[32]{0:T(128)} %param.33) | copy-start | bytes 388
  7.8 16.0 %all-to-all-start = ((bf16[32,2,2560]{2,1,0:T(2,128)(2,1)}), bf16[32,2,2560]{2,1,0:T(2,128)(2,1)S(1)}, u32[]{:S(2)}, u32[]{:S(2)}) async-start(bf16[32,2,2560]{2,1,0:T(2,128)(2,1)} %reshape.389), calls=%async_computation | async-start | bytes 655360 | tf_op jit(solution)/shard_map/while/body/eval_jaxpr/all_to_all | solution.py:101
  49.3 14.1 %all-to-all-start.1 = ((bf16[32,2,2560]{2,1,0:T(2,128)(2,1)}), bf16[32,2,2560]{2,1,0:T(2,128)(2,1)}, u32[]{:S(2)}, u32[]{:S(2)}) async-start(bf16[32,2,2560]{2,1,0:T(2,128)(2,1)} %reshape.392), calls=%async_computation.1 | async-start | bytes 655360 | tf_op jit(solution)/shard_map/while/body/eval_jaxpr/all_to_all | solution.py:103
  78.0 1.0 copy-start
  86.6 13.4 %all-to-all-start = ((bf16[32,2,2560]{2,1,0:T(2,128)(2,1)}), bf16[32,2,2560]{2,1,0:T(2,128)(2,1)S(1)}, u32[]{:S(2)}, u32[]{:S(2)}) async-start(bf16[32,2,2560]{2,1,0:T(2,128)(2,1)} %reshape.389), calls=%async_computation | async-start | bytes 655360 | tf_op jit(solution)/shard_map/while/body/eval_jaxpr/all_to_all | solution.py:101
  125.4 14.1 %all-to-all-start.1 = ((bf16[32,2,2560]{2,1,0:T(2,128)(2,1)}), bf16[32,2,2560]{2,1,0:T(2,128)(2,1)}, u32[]{:S(2)}, u32[]{:S(2)}) async-start(bf16[32,2,2560]{2,1,0:T(2,128)(2,1)} %reshape.392), calls=%async_computation.1 | async-start | bytes 655360 | tf_op jit(solution)/shard_map/while/body/eval_jaxpr/all_to_all | solution.py:103
  162.7 13.4 %all-to-all-start = ((bf16[32,2,2560]{2,1,0:T(2,128)(2,1)}), bf16[32,2,2560]{2,1,0:T(2,128)(2,1)S(1)}, u32[]{:S(2)}, u32[]{:S(2)}) async-start(bf16[32,2,2560]{2,1,0:T(2,128)(2,1)} %reshape.389), calls=%async_computation | async-start | bytes 655360 | tf_op jit(solution)/shard_map/while/body/eval_jaxpr/all_to_all | solution.py:101
  201.6 14.1 %all-to-all-start.1 = ((bf16[32,2,2560]{2,1,0:T(2,128)(2,1)}), bf16[32,2,2560]{2,1,0:T(2,128)(2,1)}, u32[]{:S(2)}, u32[]{:S(2)}) async-start(bf16[32,2,2560]{2,1,0:T(2,128)(2,1)} %reshape.392), calls=%async_computation.1 | async-start | bytes 655360 | tf_op jit(solution)/shard_map/while/body/eval_jaxpr/all_to_all | solution.py:103
  230.2 1.0 copy-start
  238.8 13.4 %all-to-all-start = ((bf16[32,2,2560]{2,1,0:T(2,128)(2,1)}), bf16[32,2,2560]{2,1,0:T(2,128)(2,1)S(1)}, u32[]{:S(2)}, u32[]{:S(2)}) async-start(bf16[32,2,2560]{2,1,0:T(2,128)(2,1)} %reshape.389), calls=%async_computation | async-start | bytes 655360 | tf_op jit(solution)/shard_map/while/body/eval_jaxpr/all_to_all | solution.py:101
  277.7 14.1 %all-to-all-start.1 = ((bf16[32,2,2560]{2,1,0:T(2,128)(2,1)}), bf16[32,2,2560]{2,1,0:T(2,128)(2,1)}, u32[]{:S(2)}, u32[]{:S(2)}) async-start(bf16[32,2,2560]{2,1,0:T(2,128)(2,1)} %reshape.392), calls=%async_computation.1 | async-start | bytes 655360 | tf_op jit(solution)/shard_map/while/body/eval_jaxpr/all_to_all | solution.py:103
  306.3 1.0 copy-start
  314.9 13.4 %all-to-all-start = ((bf16[32,2,2560]{2,1,0:T(2,128)(2,1)}), bf16[32,2,2560]{2,1,0:T(2,128)(2,1)S(1)}, u32[]{:S(2)}, u32[]{:S(2)}) async-start(bf16[32,2,2560]{2,1,0:T(2,128)(2,1)} %reshape.389), calls=%async_computation | async-start | bytes 655360 | tf_op jit(solution)/shard_map/while/body/eval_jaxpr/all_to_all | solution.py:101
  353.8 14.1 %all-to-all-start.1 = ((bf16[32,2,2560]{2,1,0:T(2,128)(2,1)}), bf16[32,2,2560]{2,1,0:T(2,128)(2,1)}, u32[]{:S(2)}, u32[]{:S(2)}) async-start(bf16[32,2,2560]{2,1,0:T(2,128)(2,1)} %reshape.392), calls=%async_computation.1 | async-start | bytes 655360 | tf_op jit(solution)/shard_map/while/body/eval_jaxpr/all_to_all | solution.py:103
  382.4 1.0 copy-start
  391.0 13.4 %all-to-all-start = ((bf16[32,2,2560]{2,1,0:T(2,128)(2,1)}), bf16[32,2,2560]{2,1,0:T(2,128)(2,1)S(1)}, u32[]{:S(2)}, u32[]{:S(2)}) async-start(bf16[32,2,2560]{2,1,0:T(2,128)(2,1)} %reshape.389), calls=%async_computation | async-start | bytes 655360 | tf_op jit(solution)/shard_map/while/body/eval_jaxpr/all_to_all | solution.py:101
  429.9 14.1 %all-to-all-start.1 = ((bf16[32,2,2560]{2,1,0:T(2,128)(2,1)}), bf16[32,2,2560]{2,1,0:T(2,128)(2,1)}, u32[]{:S(2)}, u32[]{:S(2)}) async-start(bf16[32,2,2560]{2,1,0:T(2,128)(2,1)} %reshape.392), calls=%async_computation.1 | async-start | bytes 655360 | tf_op jit(solution)/shard_map/while/body/eval_jaxpr/all_to_all | solution.py:103
  458.5 1.0 copy-start
  467.1 13.4 %all-to-all-start = ((bf16[32,2,2560]{2,1,0:T(2,128)(2,1)}), bf16[32,2,2560]{2,1,0:T(2,128)(2,1)S(1)}, u32[]{:S(2)}, u32[]{:S(2)}) async-start(bf16[32,2,2560]{2,1,0:T(2,128)(2,1)} %reshape.389), calls=%async_computation | async-start | bytes 655360 | tf_op jit(solution)/shard_map/while/body/eval_jaxpr/all_to_all | solution.py:101
  506.0 14.1 %all-to-all-start.1 = ((bf16[32,2,2560]{2,1,0:T(2,128)(2,1)}), bf16[32,2,2560]{2,1,0:T(2,128)(2,1)}, u32[]{:S(2)}, u32[]{:S(2)}) async-start(bf16[32,2,2560]{2,1,0:T(2,128)(2,1)} %reshape.392), calls=%async_computation.1 | async-start | bytes 655360 | tf_op jit(solution)/shard_map/while/body/eval_jaxpr/all_to_all | solution.py:103
  543.2 13.4 %all-to-all-start = ((bf16[32,2,2560]{2,1,0:T(2,128)(2,1)}), bf16[32,2,2560]{2,1,0:T(2,128)(2,1)S(1)}, u32[]{:S(2)}, u32[]{:S(2)}) async-start(bf16[32,2,2560]{2,1,0:T(2,128)(2,1)} %reshape.389), calls=%async_computation | async-start | bytes 655360 | tf_op jit(solution)/shard_map/while/body/eval_jaxpr/all_to_all | solution.py:101
  582.1 14.1 %all-to-all-start.1 = ((bf16[32,2,2560]{2,1,0:T(2,128)(2,1)}), bf16[32,2,2560]{2,1,0:T(2,128)(2,1)}, u32[]{:S(2)}, u32[]{:S(2)}) async-start(bf16[32,2,2560]{2,1,0:T(2,128)(2,1)} %reshape.392), calls=%async_computation.1 | async-start | bytes 655360 | tf_op jit(solution)/shard_map/while/body/eval_jaxpr/all_to_all | solution.py:103
  619.3 13.4 %all-to-all-start = ((bf16[32,2,2560]{2,1,0:T(2,128)(2,1)}), bf16[32,2,2560]{2,1,0:T(2,128)(2,1)S(1)}, u32[]{:S(2)}, u32[]{:S(2)}) async-start(bf16[32,2,2560]{2,1,0:T(2,128)(2,1)} %reshape.389), calls=%async_computation | async-start | bytes 655360 | tf_op jit(solution)/shard_map/while/body/eval_jaxpr/all_to_all | solution.py:101
  658.2 14.1 %all-to-all-start.1 = ((bf16[32,2,2560]{2,1,0:T(2,128)(2,1)}), bf16[32,2,2560]{2,1,0:T(2,128)(2,1)}, u32[]{:S(2)}, u32[]{:S(2)}) async-start(bf16[32,2,2560]{2,1,0:T(2,128)(2,1)} %reshape.392), calls=%async_computation.1 | async-start | bytes 655360 | tf_op jit(solution)/shard_map/while/body/eval_jaxpr/all_to_all | solution.py:103
  686.8 1.0 copy-start
  695.4 13.4 %all-to-all-start = ((bf16[32,2,2560]{2,1,0:T(2,128)(2,1)}), bf16[32,2,2560]{2,1,0:T(2,128)(2,1)S(1)}, u32[]{:S(2)}, u32[]{:S(2)}) async-start(bf16[32,2,2560]{2,1,0:T(2,128)(2,1)} %reshape.389), calls=%async_computation | async-start | bytes 655360 | tf_op jit(solution)/shard_map/while/body/eval_jaxpr/all_to_all | solution.py:101
  734.3 14.1 %all-to-all-start.1 = ((bf16[32,2,2560]{2,1,0:T(2,128)(2,1)}), bf16[32,2,2560]{2,1,0:T(2,128)(2,1)}, u32[]{:S(2)}, u32[]{:S(2)}) async-start(bf16[32,2,2560]{2,1,0:T(2,128)(2,1)} %reshape.392), calls=%async_computation.1 | async-start | bytes 655360 | tf_op jit(solution)/shard_map/while/body/eval_jaxpr/all_to_all | solution.py:103
  771.5 13.4 %all-to-all-start = ((bf16[32,2,2560]{2,1,0:T(2,128)(2,1)}), bf16[32,2,2560]{2,1,0:T(2,128)(2,1)S(1)}, u32[]{:S(2)}, u32[]{:S(2)}) async-start(bf16[32,2,2560]{2,1,0:T(2,128)(2,1)} %reshape.389), calls=%async_computation | async-start | bytes 655360 | tf_op jit(solution)/shard_map/while/body/eval_jaxpr/all_to_all | solution.py:101
  810.4 14.1 %all-to-all-start.1 = ((bf16[32,2,2560]{2,1,0:T(2,128)(2,1)}), bf16[32,2,2560]{2,1,0:T(2,128)(2,1)}, u32[]{:S(2)}, u32[]{:S(2)}) async-start(bf16[32,2,2560]{2,1,0:T(2,128)(2,1)} %reshape.392), calls=%async_computation.1 | async-start | bytes 655360 | tf_op jit(solution)/shard_map/while/body/eval_jaxpr/all_to_all | solution.py:103
  839.1 1.0 copy-start
  847.7 13.4 %all-to-all-start = ((bf16[32,2,2560]{2,1,0:T(2,128)(2,1)}), bf16[32,2,2560]{2,1,0:T(2,128)(2,1)S(1)}, u32[]{:S(2)}, u32[]{:S(2)}) async-start(bf16[32,2,2560]{2,1,0:T(2,128)(2,1)} %reshape.389), calls=%async_computation | async-start | bytes 655360 | tf_op jit(solution)/shard_map/while/body/eval_jaxpr/all_to_all | solution.py:101
  886.5 14.1 %all-to-all-start.1 = ((bf16[32,2,2560]{2,1,0:T(2,128)(2,1)}), bf16[32,2,2560]{2,1,0:T(2,128)(2,1)}, u32[]{:S(2)}, u32[]{:S(2)}) async-start(bf16[32,2,2560]{2,1,0:T(2,128)(2,1)} %reshape.392), calls=%async_computation.1 | async-start | bytes 655360 | tf_op jit(solution)/shard_map/while/body/eval_jaxpr/all_to_all | solution.py:103
  920.2 11.9 %copy-start.7 = (s32[2,40]{1,0:T(2,128)S(1)}, s32[2,40]{1,0:T(2,128)}, u32[]{:S(2)}) copy-start(s32[2,40]{1,0:T(2,128)} %param.34) | copy-start | bytes 964
  920.3 14.7 %collective-permute-start = (bf16[12,1,8,256]{3,2,0,1:T(8,128)(2,1)S(1)}, bf16[12,1,8,256]{3,2,0,1:T(8,128)(2,1)S(1)}, u32[]{:S(2)}, u32[]{:S(2)}) collective-permute-start(bf16[12,1,8,256]{3,2,0,1:T(8,128)(2,1)S(1)} %get-tuple-element.349), channel_id=1, source_target_pairs={{0,4},{4,8},{8,12},{12,16},{16,20},{20,24},{24,28},{28,32},{32,36}... | collective-permute-start | bytes 147464 | tf_op jit(solution)/shard_map/ppermute | solution.py:25
  922.8 12.2 %collective-permute-start.1 = (bf16[12,1,8,256]{3,2,0,1:T(8,128)(2,1)S(1)}, bf16[12,1,8,256]{3,2,0,1:T(8,128)(2,1)S(1)}, u32[]{:S(2)}, u32[]{:S(2)}) collective-permute-start(bf16[12,1,8,256]{3,2,0,1:T(8,128)(2,1)S(1)} %get-tuple-element.350), channel_id=1, source_target_pairs={{4,0},{8,4},{12,8},{16,12},{20,16},{24,20},{28,24},{32,28},{36,32}... | collective-permute-start | bytes 147464 | tf_op jit(solution)/shard_map/ppermute | solution.py:26
  933.7 2.2 copy-start.2
  933.8 2.2 copy-start.3
  933.8 2.2 copy-start.11
  1138.8 12.4 %copy-start.1 = (f32[1,32,1440]{2,1,0:T(8,128)}, f32[1,32,1440]{2,1,0:T(8,128)S(1)}, u32[]{:S(2)}) copy-start(f32[1,32,1440]{2,1,0:T(8,128)S(1)} %get-tuple-element.305) | copy-start | bytes 552964
  1138.8 8.2 copy-start.13
  1139.4 9.1 collective-permute-start.2
  1141.3 8.9 collective-permute-start.3
  (5 other events, 4.9 us)
where the time goes:
time: 1160 us; the launch traced here: 1150 us
  local copies, waits for them, and re-layouts  398 us (34%)
  matrix products  238 us (21%)
  waiting for transfers between devices  172 us (15%)
  starting transfers between devices  153 us (13%)
  blocking collectives  152 us (13%)
  other arithmetic  34.7 us (3%)
    dot_general x12, matrix products, padded_transform(): jnp.einsum('rmnc,mln->rlmc', damped, tables, preferred_element_type=jnp.f...  182 us
    while x84, local copies, waits for them, and re-layouts  153 us
    all_gather x12, blocking collectives, ocean_advance(): lax.all_gather(ocean_now.astype(jnp.bfloat16), 'lev', axis=0, tiled=True)  152 us
    convert_element_type x36, local copies, waits for them, and re-layouts, march_air_model(): synthesis_field = returned.reshape(field_local, height_pile, lat_local, c...  108 us
    all_to_all x12, waiting for transfers between devices, march_air_model(): lax.all_to_all(scaled, 'band', split_axis=2, concat_axis=1, tiled=True)  95.5 us
    all_to_all x12, waiting for transfers between devices, march_air_model(): lax.all_to_all(synthesis, 'band', split_axis=1, concat_axis=2, tiled=True)  72.9 us
    all_to_all x12, starting transfers between devices, march_air_model(): lax.all_to_all(synthesis, 'band', split_axis=1, concat_axis=2, tiled=True)  71.3 us
    all_to_all x12, starting transfers between devices, march_air_model(): lax.all_to_all(scaled, 'band', split_axis=2, concat_axis=1, tiled=True)  66.4 us
  transfers between devices with their start and end apart: 28, of which 26 were waited for; matrix products, arithmetic and copies ran while one was open for 3% of the time, Pallas kernels for 0%

commit v1 on v0

v1 whole, which is shorter than its diff:
```python
import math

import jax
import jax.numpy as jnp
import numpy as np
from jax import lax
from jax.experimental import pallas as pl
from jax.experimental.pallas import tpu as pltpu
from jax.sharding import PartitionSpec as P

MARG = 8
AXES = ("band", "lev")
degree_damping = 2e-06
ocean_step = 0.5
mixing_diagonal = 0.95
synth_divisor = 4.0

BANDS, FIELDS = 32, 4
LEVELS, LAT, COLS = 16, 40, 256
NLAT = BANDS * LAT
WAVES = COLS // 2
STEPS = 12
SLOTS = 32
HALF = LAT // 2
ITEMS = 32
PAIRS = [(l, p) for l in range(LEVELS) for p in range(l + 1, LEVELS)]
NPAIR = len(PAIRS)
XROWS = 24
CHUNK = XROWS + LAT
BF = jnp.bfloat16
F32 = jnp.float32
NT = (((1,), (1,)), ((), ()))


def pair_matrix():
    q = np.zeros((LEVELS * LEVELS, 128), np.float32)
    for i, (l, p) in enumerate(PAIRS):
        q[l * LEVELS + p, i] = 1.0
        q[p * LEVELS + l, i] = -1.0
    return q


def damping_table(wave_values, degree_count):
    degrees = wave_values[:, None] + jnp.arange(degree_count, dtype=jnp.int32)[None, :]
    degree_float = degrees.astype(F32)
    factor = 1.0 / (1.0 + degree_damping * degree_float * (degree_float + 1.0))
    return jnp.where(degrees < degree_count, factor, jnp.zeros_like(factor))


def hi_lo(v):
    hi = lax.reduce_precision(v, 8, 7)
    return hi, v - hi


def pack_kernel(x_ref, s_ref, e_ref, m_ref, o_ref, d_ref, t_ref):
    row = lax.broadcasted_iota(jnp.int32, (COLS, COLS), 0)
    col = lax.broadcasted_iota(jnp.int32, (COLS, COLS), 1)
    spread = jnp.where(row == 2 * (col % WAVES) + col // WAVES, 1.0, 0.0).astype(BF)
    base = 0
    for ref in (x_ref, s_ref, e_ref):
        n = ref.shape[0]
        d = jnp.dot(ref[...].astype(BF), spread, preferred_element_type=F32)
        d_ref[0, base : base + n, :] = d[:, :WAVES]
        d_ref[1, base : base + n, :] = d[:, WAVES:]
        base += n
    for h in range(HALF):
        parts = [
            d_ref[c, pl.ds(lo * HALF + h, ITEMS, stride=LAT), :] for c in range(2) for lo in range(2)
        ]
        t_ref[pl.ds(h, WAVES, stride=XROWS), :] = jnp.concatenate(parts, axis=0).T
    mix = m_ref[...]

    def put(m, _):
        o_ref[m, 0:XROWS, :] = t_ref[pl.ds(pl.multiple_of(m * XROWS, 8), XROWS), :].astype(BF)
        o_ref[m, XROWS:CHUNK, :] = mix
        return 0

    for h in range(HALF, XROWS):
        t_ref[pl.ds(h, WAVES, stride=XROWS), :] = jnp.zeros((WAVES, 128), F32)
    lax.fori_loop(0, WAVES, put, 0)


def atmosphere_kernel(rm_ref, rx_ref, sm_ref, sx_ref, p_ref, g_ref, xo_ref, fo_ref, a_ref, x_ref, y_ref, f_ref):
    for n in range(NLAT // 256):
        a_ref[:, n * 256 : (n + 1) * 256] = lax.dot_general(
            sm_ref[...], rm_ref[n * 256 : (n + 1) * 256, :], NT, preferred_element_type=F32
        )
    for lo in range(2):
        x_ref[:, lo * 640 : (lo + 1) * 640] = lax.dot_general(
            sx_ref[lo], rx_ref[...], NT, preferred_element_type=F32
        )

    def step(k, _):
        weight = x_ref[28 * 8 : 29 * 8, :]
        state = x_ref[0:128, :].reshape(LEVELS, 8, NLAT) * weight[None]
        y_ref[...] = jnp.dot(
            state.reshape(128, NLAT).astype(BF), p_ref[...], preferred_element_type=F32
        )

        def block(n, _):
            lanes = pl.ds(pl.multiple_of(n * 128, 128), 128)
            mid = [
                x_ref[8 * l : 8 * l + 8, lanes] - y_ref[8 * l : 8 * l + 8, lanes]
                for l in range(LEVELS)
            ]
            skin = x_ref[pl.ds(pl.multiple_of(128 + 8 * k, 8), 8), lanes]
            flux = x_ref[29 * 8 : 30 * 8, lanes] * (skin - mid[LEVELS - 1])
            f_ref[pl.ds(pl.multiple_of(8 * k, 8), 8), lanes] = flux
            acc = [mixing_diagonal * v for v in mid]
            acc[LEVELS - 1] = acc[LEVELS - 1] + flux
            for i, (l, p) in enumerate(PAIRS):
                a = a_ref[8 * i : 8 * i + 8, lanes]
                acc[l] = acc[l] + a * mid[p]
                acc[p] = acc[p] - a * mid[l]
            for l in range(LEVELS):
                x_ref[8 * l : 8 * l + 8, lanes] = acc[l]
            return 0

        lax.fori_loop(0, NLAT // 128, block, 0)
        return 0

    lax.fori_loop(0, STEPS, step, 0)
    xo_ref[...] = x_ref[0:128, :].astype(BF)
    fo_ref[...] = jnp.dot(f_ref[...].astype(BF), g_ref[...], preferred_element_type=F32).astype(BF)


def ocean_kernel(lev_ref, f_ref, zt_ref, z_ref, c_ref, o0_ref, r_ref, so_ref, co_ref, o_ref, t_ref):
    o_ref[...] = o0_ref[...]
    start = pl.multiple_of(lev_ref[0] * SLOTS, SLOTS)
    scale = 1.0 / math.sqrt(z_ref.shape[1])

    def step(k, _):
        ocean = o_ref[...]
        coarse = ocean.astype(BF)
        push = jnp.dot(zt_ref[...], f_ref[k], preferred_element_type=F32)
        pull = jnp.dot(coarse, c_ref[0], preferred_element_type=F32)
        pull = pull + jnp.dot(coarse, c_ref[1], preferred_element_type=F32)
        updated = (ocean + (pull + push)) * r_ref[...]
        o_ref[...] = updated
        coef = jnp.dot(z_ref[...], updated.astype(BF), preferred_element_type=F32) * scale
        t_ref[...] = coef.T
        co_ref[k] = t_ref[pl.ds(start, SLOTS), :].astype(BF)
        return 0

    lax.fori_loop(0, STEPS, step, 0)
    lon = o_ref.shape[0]
    for x in range(0, lon, 128):
        w = min(128, lon - x)
        t_ref[:, 0:w] = o_ref[x : x + w, :].T
        so_ref[:, x : x + w] = t_ref[pl.ds(start, SLOTS), 0:w]


def vmem(n):
    return [pl.BlockSpec(memory_space=pltpu.VMEM)] * n


def per_device(
    air_fourier_coefficients,
    quadrature_factor,
    associated_polynomial_table,
    east_west_harmonic,
    boundary_diffusion,
    bulk_transfer_coefficient,
    skin_heat_earlier,
    sea_boundary_values,
    sea_damping_speed,
    sea_coupling_matrix,
    patch_active_entries,
    sea_southern_parallel,
    sea_northern_share,
    air_paired_cells,
    air_second_share,
):
    band = lax.axis_index("band")
    lev = lax.axis_index("lev")
    lon = sea_boundary_values.shape[2]
    degree_count = associated_polynomial_table.shape[2]

    w_hi, w_lo = hi_lo(quadrature_factor)
    b_hi, b_lo = hi_lo(bulk_transfer_coefficient[0])
    live = jnp.arange(SLOTS, dtype=jnp.int32) < patch_active_entries[0]
    offset = (sea_southern_parallel - (band * LAT - MARG)).astype(F32)
    low = jnp.where(live, 1.0 - sea_northern_share, 0.0)
    high = jnp.where(live, sea_northern_share, 0.0)
    taps = jnp.where(lev == 0, offset, jnp.where(lev == 1, low, high))
    taps = jnp.pad(taps, (0, LAT - SLOTS))
    even = (jnp.arange(COLS) % 2 == 0)[None, :]
    extra = jnp.concatenate(
        [
            jnp.where(even, w_hi[:, None], w_lo[:, None]),
            jnp.where(even, b_hi[:, None], b_lo[:, None]),
            jnp.broadcast_to(taps[:, None], (LAT, COLS)),
            jnp.zeros((LAT, COLS), F32),
        ],
        axis=0,
    )
    mix = jnp.einsum(
        "rg,ri->gi",
        boundary_diffusion.reshape(LEVELS * LEVELS, LAT),
        jnp.asarray(pair_matrix()),
        precision=lax.Precision.HIGHEST,
    ).astype(BF)
    chunks = pl.pallas_call(
        pack_kernel,
        out_shape=jax.ShapeDtypeStruct((WAVES, CHUNK, 128), BF),
        in_specs=vmem(4),
        out_specs=pl.BlockSpec(memory_space=pltpu.VMEM),
        scratch_shapes=[
            pltpu.VMEM((2, ITEMS * LAT, 128), F32),
            pltpu.VMEM((WAVES * XROWS, 128), F32),
        ],
        name="pack_in",
    )(
        air_fourier_coefficients.reshape(LEVELS * LAT, COLS),
        skin_heat_earlier.reshape(STEPS * LAT, COLS),
        extra,
        mix,
    )
    got = lax.all_to_all(chunks, AXES, 0, 0, tiled=True)

    table = lax.dynamic_index_in_dim(associated_polynomial_table, lev, 0, keepdims=False)
    table = table.reshape(BANDS, 2, HALF, degree_count).transpose(1, 0, 2, 3).reshape(NLAT, degree_count)
    wave = lax.dynamic_slice_in_dim(east_west_harmonic, band * FIELDS + lev, 1, 0)
    damping = damping_table(wave, degree_count)
    damped = (table * damping).astype(BF)
    operator = lax.dot_general(table, damped, NT, preferred_element_type=F32)
    operator = (operator * (1.0 / (synth_divisor * math.sqrt(degree_count) * math.sqrt(NLAT)))).astype(BF)

    row = jnp.arange(NPAIR * 8, dtype=jnp.int32)[:, None]
    col = jnp.arange(FIELDS * 128, dtype=jnp.int32)[None, :]
    select_mix = ((row // 8 == col % 128) & (row % 8 // 2 == col // 128)).astype(BF)
    row = jnp.arange(ITEMS * 8, dtype=jnp.int32)[:, None]
    item = row // 8
    same = (col % ITEMS == item) & (col // 128 == row % 8 // 2)
    same_c = (col % 128 // 64 == row % 2) | (item == 28) | (item == 29)
    select_x = jnp.stack([same & same_c & (col % 64 // ITEMS == lo) for lo in range(2)]).astype(BF)

    longitude = jnp.arange(lon, dtype=jnp.int32)
    phases = east_west_harmonic[:, None] * longitude[None, :] % lon
    angles = phases.astype(F32) * (2.0 * math.pi / lon)
    cosine, sine = jnp.cos(angles).astype(BF), (-jnp.sin(angles)).astype(BF)
    zonal = jnp.stack([cosine, sine], axis=1).reshape(COLS, lon)
    push_scale = -ocean_step / math.sqrt(COLS)
    zonal_t = (jnp.concatenate([cosine, sine], axis=0).astype(F32) * push_scale).astype(BF).T
    own = jnp.concatenate([sea_boundary_values[0], sea_damping_speed[0]], axis=0)
    sent = own.astype(BF)
    shifted = [sent]
    for d in range(1, FIELDS):
        shifted.append(lax.ppermute(sent, "lev", [(i, (i + d) % FIELDS) for i in range(FIELDS)]))
    shifted = jnp.stack(shifted)
    fields = []
    for f in range(FIELDS):
        other = lax.dynamic_index_in_dim(shifted, (lev - f) % FIELDS, 0, keepdims=False)
        fields.append(jnp.where(lev == f, own, other.astype(F32)))
    fields = jnp.stack(fields).reshape(FIELDS, 2, SLOTS, lon)
    ocean0 = fields[:, 0].reshape(FIELDS * SLOTS, lon).T
    shrink = 1.0 / (1.0 + ocean_step * fields[:, 1].reshape(FIELDS * SLOTS, lon).T)
    skew = ocean_step * (sea_coupling_matrix - sea_coupling_matrix.T)
    couple = jnp.kron(skew.T, jnp.eye(SLOTS, dtype=F32))
    couple = jnp.stack(hi_lo(couple)).astype(BF)

    gotx = got[:, :HALF].reshape(BANDS, FIELDS, HALF, 128)
    recv_x = gotx.transpose(0, 2, 1, 3).reshape(BANDS * HALF, FIELDS * 128)
    recv_m = (
        got[:, XROWS:].reshape(BANDS, FIELDS, 2, HALF, 128).transpose(2, 0, 3, 1, 4).reshape(NLAT, FIELDS * 128)
    )
    tap = gotx.reshape(BANDS, FIELDS, HALF, 2, 2, ITEMS)[:, :3, :, 0, :, 30]
    tap = tap.transpose(1, 0, 3, 2).reshape(3, BANDS, LAT)[:, :, :SLOTS].astype(F32).reshape(3, 1, BANDS * SLOTS)
    south = tap[0] + (jnp.arange(BANDS * SLOTS, dtype=jnp.int32) // SLOTS * LAT - MARG).astype(F32)[None]
    place = jnp.arange(NLAT, dtype=jnp.int32)
    place = place % 640 // HALF * LAT + place // 640 * HALF + place % HALF
    place = place.astype(F32)[:, None]
    to_slots = (jnp.where(place == south, tap[1], 0.0) + jnp.where(place == south + 1.0, tap[2], 0.0)).astype(BF)

    air_end, slot_flux = pl.pallas_call(
        atmosphere_kernel,
        out_shape=(
            jax.ShapeDtypeStruct((128, NLAT), BF),
            jax.ShapeDtypeStruct((STEPS * 8, BANDS * SLOTS), BF),
        ),
        in_specs=vmem(6),
        out_specs=tuple(vmem(2)),
        scratch_shapes=[
            pltpu.VMEM((NPAIR * 8, NLAT), F32),
            pltpu.VMEM((ITEMS * 8, NLAT), F32),
            pltpu.VMEM((128, NLAT), F32),
            pltpu.VMEM((STEPS * 8, NLAT), F32),
        ],
        name="atmosphere",
    )(recv_m, recv_x, select_mix, select_x, operator, to_slots)

    flux_out = slot_flux.reshape(STEPS, FIELDS, 2, BANDS, SLOTS).transpose(3, 2, 0, 1, 4)
    flux_out = jnp.broadcast_to(
        flux_out.reshape(BANDS, 1, 2 * STEPS, 128), (BANDS, FIELDS, 2 * STEPS, 128)
    ).reshape(WAVES, 2 * STEPS, 128)
    air_out = air_end.reshape(LEVELS, FIELDS, 2, 2, BANDS, HALF).transpose(4, 1, 2, 0, 3, 5)
    air_out = air_out.reshape(WAVES, 10, 128)
    out = jnp.concatenate([flux_out, air_out, jnp.zeros((WAVES, 6, 128), BF)], axis=1)
    back = lax.all_to_all(out, AXES, 0, 0, tiled=True)
    air_coefficients_end = (
        back[:, 24:34].reshape(COLS, LEVELS * LAT).T.astype(F32).reshape(1, LEVELS, LAT, COLS)
    )
    flux_in = back[:, :24].reshape(WAVES, 2, STEPS, 128).transpose(2, 1, 0, 3).reshape(STEPS, COLS, 128)

    sea_end, ocean_coef = pl.pallas_call(
        ocean_kernel,
        out_shape=(
            jax.ShapeDtypeStruct((SLOTS, lon), F32),
            jax.ShapeDtypeStruct((STEPS, SLOTS, COLS), BF),
        ),
        in_specs=[pl.BlockSpec(memory_space=pltpu.SMEM)] + vmem(6),
        out_specs=tuple(vmem(2)),
        scratch_shapes=[pltpu.VMEM((lon, 128), F32), pltpu.VMEM((128, COLS), F32)],
        name="ocean",
    )(lev.astype(jnp.int32)[None], flux_in, zonal_t, zonal, couple, ocean0, shrink)

    up = [(i, i + 1) for i in range(BANDS - 1)]
    down = [(j, i) for i, j in up]
    before = lax.ppermute(ocean_coef, "band", up)
    after = lax.ppermute(ocean_coef, "band", down)
    neighbours = jnp.concatenate([before, ocean_coef, after], axis=1)
    slot_index = jnp.arange(3 * SLOTS, dtype=jnp.int32)[None, :]
    first = (air_paired_cells[0] - (band - 1) * SLOTS)[:, None]
    second = (air_paired_cells[1] - (band - 1) * SLOTS)[:, None]
    return_taps = jnp.where(slot_index == first, (1.0 - air_second_share)[:, None], 0.0) + jnp.where(
        slot_index == second, air_second_share[:, None], 0.0
    )
    skin_heat_newest = jnp.einsum(
        "ga,kac->kgc", return_taps.astype(BF), neighbours, preferred_element_type=F32
    )[:, None]
    return (air_coefficients_end, sea_end[None], skin_heat_newest)


def solution(mesh):
    return jax.shard_map(
        per_device,
        mesh=mesh,
        in_specs=(
            P("lev", None, "band", None),
            P("band"),
            P("band", None, None),
            P(),
            P("lev", None, None, "band"),
            P("lev", "band"),
            P(None, "lev", "band", None),
            P("lev", "band", None),
            P("lev", "band", None),
            P(),
            P("band"),
            P("band"),
            P("band"),
            P(None, "band"),
            P("band"),
        ),
        out_specs=(
            P("lev", None, "band", None),
            P("lev", "band", None),
            P(None, "lev", "band", None),
        ),
        check_vma=False,
    )
```

time: 1160 us -> 215 us (0.19)
  local copies, waits for them, and re-layouts: 398 us -> 72.9 us
  matrix products: 238 us -> 10.7 us
  blocking collectives: 152 us -> 0 us
  waiting for transfers between devices: 172 us -> 23.4 us
  starting transfers between devices: 153 us -> 29.8 us
  Pallas kernels: 0 us -> 41.3 us
    dot_general x39 -> x3, matrix products: 238 us -> 10.7 us  [the longest x1 7.79 us: per_device(): operator = lax.dot_general(table, damped, NT, preferred_element_type=F32)]
    while x84 -> x0, local copies, waits for them, and re-layouts: 153 us -> none
    all_gather x12 -> x0, blocking collectives: 152 us -> none  [ocean_advance(): lax.all_gather(ocean_now.astype(jnp.bfloat16), 'lev', axis=0, tiled=True)]
    all_to_all x24 -> x2, waiting for transfers between devices: 168 us -> 17.4 us  [the longest x1 17.4 us: per_device(): back = lax.all_to_all(out, AXES, 0, 0, tiled=True)]
    all_to_all x24 -> x2, starting transfers between devices: 138 us -> 19.5 us  [the longest x1 9.77 us: per_device(): got = lax.all_to_all(chunks, AXES, 0, 0, tiled=True)]
    convert_element_type x38 -> x2, local copies, waits for them, and re-layouts: 109 us -> 9.94 us  [per_device(): damped = (table * damping).astype(BF)]
    pallas_call x0 -> x3, Pallas kernels: none -> 41.3 us  [the longest x1 24.3 us: per_device(): pl.pallas_call(atmosphere_kernel, out_shape=(jax.ShapeDtypeStruct((128, N...]
    reshape x36 -> x11, local copies, waits for them, and re-layouts: 65.5 us -> 25.5 us  [the longest x2 7.32 us: per_device(): table.reshape(BANDS, 2, HALF, degree_count).transpose(1, 0, 2, 3)]
  transfers between devices with their start and end apart: 28 -> 7, of which waited for: 26 -> 3; matrix products, arithmetic and copies ran while one was open for 3% -> 33% of each run, Pallas kernels for 0% -> 2%
where the time goes in v1:
time: 215 us; the launch traced here: 214 us
  local copies, waits for them, and re-layouts  72.9 us (34%)
  Pallas kernels  41.3 us (19%)
  other arithmetic  34 us (16%)
  starting transfers between devices  29.8 us (14%)
  waiting for transfers between devices  23.4 us (11%)
  matrix products  10.7 us (5%)
    pallas_call x1, Pallas kernels, per_device(): pl.pallas_call(atmosphere_kernel, out_shape=(jax.ShapeDtypeStruct((128, N...  24.3 us
    all_to_all x1, waiting for transfers between devices, per_device(): back = lax.all_to_all(out, AXES, 0, 0, tiled=True)  17.4 us
    pallas_call x1, Pallas kernels, per_device(): pl.pallas_call(ocean_kernel, out_shape=(jax.ShapeDtypeStruct((SLOTS, lon)...  12.8 us
    convert_element_type x2, local copies, waits for them, and re-layouts, per_device(): damped = (table * damping).astype(BF)  9.94 us
    all_to_all x1, starting transfers between devices, per_device(): got = lax.all_to_all(chunks, AXES, 0, 0, tiled=True)  9.77 us
    all_to_all x1, starting transfers between devices, per_device(): back = lax.all_to_all(out, AXES, 0, 0, tiled=True)  9.76 us
    dot_general x1, matrix products, per_device(): operator = lax.dot_general(table, damped, NT, preferred_element_type=F32)  7.79 us
    convert_element_type x2, other arithmetic, per_device(): cosine, sine = (jnp.cos(angles).astype(BF), (-jnp.sin(angles)).astype(BF))  7.43 us
  transfers between devices with their start and end apart: 7, of which 3 were waited for; matrix products, arithmetic and copies ran while one was open for 33% of the time, Pallas kernels for 2%

profile of v1, /device:TPU:32, one launch (start us, length us, event | category | flops | bytes accessed | tf_op | source)
XLA Modules:
  0.0 213.8 jit_solution(2822793526801164339)
XLA Ops:
  0.6 1.8 convert_bitcast_fusion.1
  2.4 1.7 convert_bitcast_fusion
  4.8 3.0 %collective-permute-start.2 = (bf16[64,1440]{1,0:T(8,128)(2,1)}, bf16[64,1440]{1,0:T(8,128)(2,1)}, u32[]{:S(2)}, u32[]{:S(2)}) collective-permute-start(bf16[64,1440]{1,0:T(8,128)(2,1)} %pad_maximum_fusion.3), channel_id=1, source_target_pairs={{0,3},{1,0},{2,1},{3,2},{4,7},{5,4},{6,5},{7,6},{8,11},{9,8},{10,9... | collective-permute-start | bytes 552968 | tf_op jit(solution)/shard_map/ppermute | solution.py:249
  11.6 1.9 fusion.1.m_ref
  14.4 4.2 %pack_in.1 = bf16[128,64,128]{2,1,0:T(8,128)(2,1)} custom-call(f32[640,256]{1,0:T(8,128)} %bitcast.124, f32[480,256]{1,0:T(8,128)} %bitcast.125, f32[160,256]{1,0:T(8,128)} %maximum_maximum_fusion.1.e_ref, bf16[40,128]{1,0:T(8,128)(2,1)} %fusion.1.m_ref), custom_call_target="tpu_custom_call" | custom-call | tf_op jit(solution)/shard_map/pack_in/pallas_call | solution.py:203
  18.6 9.8 %all-to-all-start = ((bf16[128,64,128]{2,1,0:T(8,128)(2,1)}), bf16[128,64,128]{2,1,0:T(8,128)(2,1)}, u32[]{:S(2)}, u32[]{:S(2)}) async-start(bf16[128,64,128]{2,1,0:T(8,128)(2,1)} %pack_in.1), calls=%async_computation | async-start | bytes 4194304 | tf_op jit(solution)/shard_map/all_to_all | solution.py:219
  28.6 2.1 %constant_dynamic-slice_fusion = bf16[1,1280,1280]{2,1,0:T(8,128)(2,1)S(1)} fusion(bf16[4,1280,1280]{2,1,0:T(8,128)(2,1)} %param.18, s32[]{:T(128)S(6)} %select_n.393), kind=kLoop, calls=%fused_computation.192 | loop fusion | bytes 6553604 | tf_op jit(solution)/shard_map/jit(dynamic_index_in_dim)/dynamic_slice | solution.py:221
  30.7 2.7 %reshape.1134 = bf16[32,2,20,1280]{3,2,1,0:T(8,128)(2,1)} reshape(bf16[1,1280,1280]{2,1,0:T(8,128)(2,1)S(1)} %constant_dynamic-slice_fusion) | data formatting | bytes 6553600 | tf_op jit(solution)/shard_map/reshape | solution.py:222
  33.4 4.3 %copy.108 = bf16[2,32,20,1280]{3,2,1,0:T(8,128)(2,1)} copy(bf16[2,32,20,1280]{3,2,0,1:T(8,128)(2,1)} %bitcast.102) | data formatting | bytes 6553600 | tf_op jit(solution)/shard_map/transpose | solution.py:222
  37.7 4.7 %reshape.1135 = bf16[1280,1280]{1,0:T(8,128)(2,1)S(1)} reshape(bf16[2,32,20,1280]{3,2,1,0:T(8,128)(2,1)} %copy.108) | data formatting | bytes 6553600 | tf_op jit(solution)/shard_map/reshape | solution.py:222
  42.4 4.1 %cosine_convert_fusion = (bf16[128,1,1440]{0,2,1:T(8,128)(2,1)}, bf16[128,1,1440]{0,2,1:T(8,128)(2,1)}) fusion(s32[128]{0:T(128)S(1)} %copy-done.4), kind=kLoop, calls=%fused_computation.27 | loop fusion | flops 2211840 | bytes 737792 | tf_op jit(solution)/shard_map/convert_element_type | solution.py:241
  47.9 3.2 %multiply_convert_fusion = bf16[2,32,20,1280]{3,1,2,0:T(8,128)(2,1)S(1)} fusion(bf16[32,2,20,1280]{3,2,1,0:T(8,128)(2,1)} %reshape.1134, f32[1280]{0:T(1024)S(1)} %divide_select_fusion), kind=kLoop, calls=%fused_computation.2 | loop fusion | flops 4915200 | bytes 6558720 | tf_op jit(solution)/shard_map/convert_element_type | solution.py:225
  51.1 3.8 %copy.109 = bf16[2,32,20,1280]{3,2,1,0:T(8,128)(2,1)} copy(bf16[2,32,20,1280]{3,1,2,0:T(8,128)(2,1)S(1)} %multiply_convert_fusion) | data formatting | bytes 6553600 | tf_op jit(solution)/shard_map/convert_element_type | solution.py:225
  54.9 6.1 %convert_element_type.157 = bf16[1280,1280]{1,0:T(8,128)(2,1)} reshape(bf16[2,32,20,1280]{3,2,1,0:T(8,128)(2,1)} %copy.109) | data formatting | bytes 6553600 | tf_op jit(solution)/shard_map/convert_element_type | solution.py:225
  61.1 2.0 pad_maximum_fusion.2
  63.1 3.1 %copy.121 = bf16[128,2,1440]{2,1,0:T(2,128)(2,1)} copy(bf16[128,2,1440]{0,2,1:T(8,128)(2,1)} %pad_maximum_fusion.2) | data formatting | bytes 1474560 | tf_op jit(solution)/shard_map/stack | solution.py:242
  66.2 3.0 %reshape.1145.z_ref = bf16[256,1440]{1,0:T(8,128)(2,1)} reshape(bf16[128,2,1440]{2,1,0:T(2,128)(2,1)} %copy.121) | data formatting | bytes 1474560 | tf_op jit(solution)/shard_map/reshape | solution.py:242
  70.2 1.1 mul.212
  71.3 1.7 convert_element_type.174
  75.0 1.4 and_convert_fusion.sm_ref
  76.4 3.3 %cosine_convert_fusion.1 = (bf16[128,1440]{0,1:T(8,128)(2,1)S(1)}, bf16[128,1440]{0,1:T(8,128)(2,1)S(1)}) fusion(s32[128]{0:T(128)S(1)} %copy-done.4), kind=kLoop, calls=%fused_computation.32 | loop fusion | flops 2211840 | bytes 737792 | tf_op jit(solution)/shard_map/convert_element_type | solution.py:241
  79.7 1.1 fusion.8.zt_ref
  80.7 7.8 %fusion.p_ref = bf16[1280,1280]{1,0:T(8,128)(2,1)} fusion(bf16[1280,1280]{1,0:T(8,128)(2,1)S(1)} %reshape.1135, bf16[1280,1280]{1,0:T(8,128)(2,1)} %convert_element_type.157), kind=kOutput, calls=%fused_computation.1 | convolution fusion | flops 4197580800 | bytes 9830400 | tf_op jit(solution)/shard_map/dot_general | solution.py:226
  89.1 1.2 pad_maximum_fusion.1
  90.3 1.5 slice.55
  92.5 1.3 copy.139
  93.8 1.2 slice.56
  97.3 5.9 %reshape_reshape.3 = bf16[32,4,20,2,2,32]{5,4,3,1,0,2:T(2,128)(2,1)S(1)} reshape(bf16[128,20,128]{2,0,1:T(8,128)(2,1)} %copy.110) | data formatting | bytes 1310720 | tf_op jit(solution)/shard_map/reshape;reshape | solution.py:267
  103.2 2.1 slice.57
  105.3 2.6 %copy.111 = bf16[32,3,20,1,2,1]{0,4,2,1,5,3:T(2,128)(2,1)S(1)} copy(bf16[32,3,20,1,2,1]{5,4,3,1,0,2:T(2,128)(2,1)} %slice.57) | data formatting | bytes 15360 | tf_op jit(solution)/shard_map/slice | solution.py:267
  108.4 2.5 %add_convert_fusion.g_ref = bf16[1280,1024]{1,0:T(8,128)(2,1)} fusion(f32[1024]{0:T(1024)S(1)} %broadcast_in_dim.150, f32[1024]{0:T(1024)S(1)} %get-tuple-element.44, f32[1024]{0:T(1024)S(1)} %broadcast_in_dim.147, f32[1024]{0:T(1024)S(1)} %get-tuple-element.43, f32[1280]{0:T(1024)S(1)} %fusion.42), kind=kLoop, calls=%fused_computation.3 | loop fusion | flops 7864320 | bytes 2642944 | tf_op jit(solution)/shard_map/convert_element_type | solution.py:273
  110.9 24.3 %atmosphere.1 = (bf16[128,1280]{1,0:T(8,128)(2,1)}, bf16[96,1024]{1,0:T(8,128)(2,1)}) custom-call(bf16[1280,512]{1,0:T(8,128)(2,1)} %bitcast.105, bf16[640,512]{1,0:T(8,128)(2,1)} %bitcast.116, bf16[960,512]{1,0:T(8,128)(2,1)} %and_convert_fusion.sm_ref, bf16[2,256,512]{2,1,0:T(8,128)(2,1)} %add_convert_fusion.1.sx_ref, bf16[1280,1280]{1,0:T(8,128)(2,1)} %fusion.p_ref, ...), custom_call_target="tpu_custom_call" | custom-call | tf_op jit(solution)/shard_map/atmosphere/pallas_call | solution.py:275
  135.2 6.8 %reshape.1139 = bf16[16,4,2,2,32,20]{5,4,3,2,1,0:T(8,128)(2,1)} reshape(bf16[128,1280]{1,0:T(8,128)(2,1)} %get-tuple-element.8) | data formatting | bytes 655360 | tf_op jit(solution)/shard_map/reshape | solution.py:296
  141.9 4.0 %copy.117 = bf16[32,4,2,16,2,20]{5,4,3,2,1,0:T(2,128)(2,1)S(1)} copy(bf16[32,4,2,16,2,20]{5,0,4,2,1,3:T(8,128)(2,1)} %bitcast.103) | data formatting | bytes 655360 | tf_op jit(solution)/shard_map/transpose | solution.py:296
  145.9 4.8 %reshape.1140 = bf16[128,10,128]{2,1,0:T(8,128)(2,1)S(1)} reshape(bf16[32,4,2,16,2,20]{5,4,3,2,1,0:T(2,128)(2,1)S(1)} %copy.117) | data formatting | bytes 655360 | tf_op jit(solution)/shard_map/reshape | solution.py:297
  150.7 1.5 reshape.1137
  153.4 1.4 maximum_maximum_fusion
  154.8 9.8 %all-to-all-start.1 = ((bf16[128,40,128]{2,1,0:T(8,128)(2,1)}), bf16[128,40,128]{2,1,0:T(8,128)(2,1)S(1)}, u32[]{:S(2)}, u32[]{:S(2)}) async-start(bf16[128,40,128]{2,1,0:T(8,128)(2,1)} %maximum_maximum_fusion), calls=%async_computation.1 | async-start | bytes 2621440 | tf_op jit(solution)/shard_map/all_to_all | solution.py:299
  164.5 1.2 convert_select_fusion.3
  166.0 1.1 copy.128
  167.2 1.1 copy.129
  168.3 17.4 %all-to-all-done.1 = bf16[128,40,128]{2,1,0:T(8,128)(2,1)S(1)} async-done(((bf16[128,40,128]{2,1,0:T(8,128)(2,1)}), bf16[128,40,128]{2,1,0:T(8,128)(2,1)S(1)}, u32[]{:S(2)}, u32[]{:S(2)}) %all-to-all-start.1) | async-done | bytes 1310752 | tf_op jit(solution)/shard_map/all_to_all | solution.py:299
  186.9 12.8 %ocean.1 = (f32[32,1440]{1,0:T(8,128)}, bf16[12,32,256]{2,1,0:T(8,128)(2,1)}) custom-call(s32[1]{0:T(128)} %bitcast.20.lev_ref, bf16[12,256,128]{2,1,0:T(8,128)(2,1)} %bitcast.113, bf16[1440,256]{1,0:T(8,128)(2,1)} %fusion.8.zt_ref, bf16[256,1440]{1,0:T(8,128)(2,1)} %reshape.1145.z_ref, bf16[2,128,128]{2,1,0:T(8,128)(2,1)} %pad_maximum_fusion.4.c_ref, ...), custom_call_target="tpu_custom_call" | custom-call | tf_op jit(solution)/shard_map/ocean/pallas_call | solution.py:305
  199.7 3.7 %collective-permute-start.4 = (bf16[12,32,256]{2,1,0:T(8,128)(2,1)}, bf16[12,32,256]{2,1,0:T(8,128)(2,1)S(1)}, u32[]{:S(2)}, u32[]{:S(2)}) collective-permute-start(bf16[12,32,256]{2,1,0:T(8,128)(2,1)} %get-tuple-element.10), channel_id=1, source_target_pairs={{4,0},{8,4},{12,8},{16,12},{20,16},{24,20},{28,24},{32,28},{36,32}... | collective-permute-start | bytes 589832 | tf_op jit(solution)/shard_map/ppermute | solution.py:320
  203.4 1.9 collective-permute-start.3
  205.6 1.1 copy.118
  206.9 5.8 %collective-permute-done.3 = bf16[12,32,256]{2,1,0:T(8,128)(2,1)S(1)} collective-permute-done((bf16[12,32,256]{2,1,0:T(8,128)(2,1)}, bf16[12,32,256]{2,1,0:T(8,128)(2,1)S(1)}, u32[]{:S(2)}, u32[]{:S(2)}) %collective-permute-start.3) | collective-permute-done | bytes 196640 | tf_op jit(solution)/shard_map/ppermute | solution.py:319
  212.7 1.1 convolution_bitcast_fusion
  (85 shorter events, 16.2 us)
Async XLA Ops:
  0.6 11.0 %copy-start = (f32[1,16,16,40]{3,2,1,0:T(8,128)S(1)}, f32[1,16,16,40]{3,2,1,0:T(8,128)}, u32[]{:S(2)}) copy-start(f32[1,16,16,40]{3,2,1,0:T(8,128)} %param.20) | copy-start | bytes 122884
  4.8 84.2 %collective-permute-start.2 = (bf16[64,1440]{1,0:T(8,128)(2,1)}, bf16[64,1440]{1,0:T(8,128)(2,1)}, u32[]{:S(2)}, u32[]{:S(2)}) collective-permute-start(bf16[64,1440]{1,0:T(8,128)(2,1)} %pad_maximum_fusion.3), channel_id=1, source_target_pairs={{0,3},{1,0},{2,1},{3,2},{4,7},{5,4},{6,5},{7,6},{8,11},{9,8},{10,9... | collective-permute-start | bytes 552968 | tf_op jit(solution)/shard_map/ppermute | solution.py:249
  7.8 81.2 %collective-permute-start.1 = (bf16[64,1440]{1,0:T(8,128)(2,1)}, bf16[64,1440]{1,0:T(8,128)(2,1)}, u32[]{:S(2)}, u32[]{:S(2)}) collective-permute-start(bf16[64,1440]{1,0:T(8,128)(2,1)} %pad_maximum_fusion.3), channel_id=1, source_target_pairs={{0,2},{1,3},{2,0},{3,1},{4,6},{5,7},{6,4},{7,5},{8,10},{9,11},{10,... | collective-permute-start | bytes 552968 | tf_op jit(solution)/shard_map/ppermute | solution.py:249
  8.5 80.6 %collective-permute-start = (bf16[64,1440]{1,0:T(8,128)(2,1)}, bf16[64,1440]{1,0:T(8,128)(2,1)}, u32[]{:S(2)}, u32[]{:S(2)}) collective-permute-start(bf16[64,1440]{1,0:T(8,128)(2,1)} %pad_maximum_fusion.3), channel_id=1, source_target_pairs={{0,1},{1,2},{2,3},{3,0},{4,5},{5,6},{6,7},{7,4},{8,9},{9,10},{10,1... | collective-permute-start | bytes 552968 | tf_op jit(solution)/shard_map/ppermute | solution.py:249
  18.6 71.7 %all-to-all-start = ((bf16[128,64,128]{2,1,0:T(8,128)(2,1)}), bf16[128,64,128]{2,1,0:T(8,128)(2,1)}, u32[]{:S(2)}, u32[]{:S(2)}) async-start(bf16[128,64,128]{2,1,0:T(8,128)(2,1)} %pack_in.1), calls=%async_computation | async-start | bytes 4194304 | tf_op jit(solution)/shard_map/all_to_all | solution.py:219
  37.7 4.7 %copy-start.4 = (s32[128]{0:T(128)S(1)}, s32[128]{0:T(128)}, u32[]{:S(2)}) copy-start(s32[128]{0:T(128)} %param.19) | copy-start | bytes 1540
  61.1 8.1 %copy-start.3 = (f32[4,4]{1,0:T(4,128)S(1)}, f32[4,4]{1,0:T(4,128)}, u32[]{:S(2)}) copy-start(f32[4,4]{1,0:T(4,128)} %param.25) | copy-start | bytes 196
  63.1 11.9 %copy-start.5 = (s32[2,40]{1,0:T(2,128)S(1)}, s32[2,40]{1,0:T(2,128)}, u32[]{:S(2)}) copy-start(s32[2,40]{1,0:T(2,128)} %param.29) | copy-start | bytes 964
  80.7 7.8 %copy-start.7 = (f32[40]{0:T(128)S(1)}, f32[40]{0:T(128)}, u32[]{:S(2)}) copy-start(f32[40]{0:T(128)} %param.30) | copy-start | bytes 484
  80.7 8.3 %copy-start.2 = (bf16[1,64,1440]{2,1,0:T(8,128)(2,1)S(1)}, bf16[1,64,1440]{2,1,0:T(8,128)(2,1)}, u32[]{:S(2)}) copy-start(bf16[1,64,1440]{2,1,0:T(8,128)(2,1)} %convert_element_type.174) | copy-start | bytes 552964
  154.8 30.9 %all-to-all-start.1 = ((bf16[128,40,128]{2,1,0:T(8,128)(2,1)}), bf16[128,40,128]{2,1,0:T(8,128)(2,1)S(1)}, u32[]{:S(2)}, u32[]{:S(2)}) async-start(bf16[128,40,128]{2,1,0:T(8,128)(2,1)} %maximum_maximum_fusion), calls=%async_computation.1 | async-start | bytes 2621440 | tf_op jit(solution)/shard_map/all_to_all | solution.py:299
  199.7 13.0 %copy-start.6 = (bf16[12,32,256]{2,1,0:T(8,128)(2,1)S(1)}, bf16[12,32,256]{2,1,0:T(8,128)(2,1)}, u32[]{:S(2)}) copy-start(bf16[12,32,256]{2,1,0:T(8,128)(2,1)} %get-tuple-element.10) | copy-start | bytes 589828
  199.7 13.0 %copy-start.8 = (f32[40]{0:T(128)S(1)}, f32[40]{0:T(128)}, u32[]{:S(2)}) copy-start(f32[40]{0:T(128)} %param.30) | copy-start | bytes 484
  199.7 13.0 %copy-start.9 = (f32[40]{0:T(128)S(1)}, f32[40]{0:T(128)}, u32[]{:S(2)}) copy-start(f32[40]{0:T(128)} %broadcast_subtract_fusion) | copy-start | bytes 484
  199.7 7.2 %collective-permute-start.4 = (bf16[12,32,256]{2,1,0:T(8,128)(2,1)}, bf16[12,32,256]{2,1,0:T(8,128)(2,1)S(1)}, u32[]{:S(2)}, u32[]{:S(2)}) collective-permute-start(bf16[12,32,256]{2,1,0:T(8,128)(2,1)} %get-tuple-element.10), channel_id=1, source_target_pairs={{4,0},{8,4},{12,8},{16,12},{20,16},{24,20},{28,24},{32,28},{36,32}... | collective-permute-start | bytes 589832 | tf_op jit(solution)/shard_map/ppermute | solution.py:320
  203.4 9.3 %collective-permute-start.3 = (bf16[12,32,256]{2,1,0:T(8,128)(2,1)}, bf16[12,32,256]{2,1,0:T(8,128)(2,1)S(1)}, u32[]{:S(2)}, u32[]{:S(2)}) collective-permute-start(bf16[12,32,256]{2,1,0:T(8,128)(2,1)} %get-tuple-element.10), channel_id=1, source_target_pairs={{0,4},{4,8},{8,12},{12,16},{16,20},{20,24},{24,28},{28,32},{32,36}... | collective-permute-start | bytes 589832 | tf_op jit(solution)/shard_map/ppermute | solution.py:319
  205.3 8.4 %copy-start.1 = (f32[1,16,16,40]{3,2,1,0:T(8,128)S(1)}, f32[1,16,16,40]{3,2,1,0:T(8,128)}, u32[]{:S(2)}) copy-start(f32[1,16,16,40]{3,2,1,0:T(8,128)} %param.20) | copy-start | bytes 122884

commit v2 on v1

v2 whole, which is shorter than its diff:
```python
import math

import jax
import jax.numpy as jnp
import numpy as np
from jax import lax
from jax.experimental import pallas as pl
from jax.experimental.pallas import tpu as pltpu
from jax.sharding import PartitionSpec as P


MARG = 8
AXES = ("band", "lev")
degree_damping = 2e-06
ocean_step = 0.5
mixing_diagonal = 0.95
synth_divisor = 4.0

BANDS, FIELDS = 32, 4
LEVELS, LAT, COLS = 16, 40, 256
NLAT = BANDS * LAT
WAVES = COLS // 2
STEPS = 12
SLOTS = 32
LO = LAT // 8
ITEMS = 32
PAIRS = [(l, p) for l in range(LEVELS) for p in range(l + 1, LEVELS)]
NPAIR = len(PAIRS)
XROWS = 24
OUT_ROWS = 40
CHUNK = XROWS + LAT
BF = jnp.bfloat16
F32 = jnp.float32
NT = (((1,), (1,)), ((), ()))


def pair_matrix():
    q = np.zeros((LEVELS * LEVELS, 128), np.float32)
    for i, (l, p) in enumerate(PAIRS):
        q[l * LEVELS + p, i] = 1.0
        q[p * LEVELS + l, i] = -1.0
    return q


def hi_lo(v):
    hi = v.astype(BF)
    return hi, (v - hi.astype(F32)).astype(BF)


def split_columns():
    row = lax.broadcasted_iota(jnp.int32, (COLS, COLS), 0)
    col = lax.broadcasted_iota(jnp.int32, (COLS, COLS), 1)
    return jnp.where(row == 2 * (col % WAVES) + col // WAVES, 1.0, 0.0).astype(BF)


def join_columns():
    row = lax.broadcasted_iota(jnp.int32, (COLS, COLS), 0)
    col = lax.broadcasted_iota(jnp.int32, (COLS, COLS), 1)
    return jnp.where(col == 2 * (row % WAVES) + row // WAVES, 1.0, 0.0).astype(BF)


def block_transpose(arrays, width):
    arrays = list(arrays)
    block = lax.broadcasted_iota(jnp.int32, arrays[0].shape, 1) // width
    s = 1
    while s < len(arrays):
        upper = (block & s) != 0
        for i in range(len(arrays)):
            if not i & s:
                a, b = arrays[i], arrays[i | s]
                arrays[i] = jnp.where(upper, pltpu.roll(b, s * width, 1), a)
                arrays[i | s] = jnp.where(upper, b, pltpu.roll(a, 128 - s * width, 1))
        s *= 2
    return arrays


def pack_kernel(ids, live_ref, x_ref, s_ref, b_ref, w_ref, k_ref, south_ref, north_ref, q_ref, o_ref, d_ref, t_ref):
    spread = split_columns()
    base = 0
    for ref in (x_ref, s_ref):
        n = ref.shape[0]
        d = jnp.dot(ref[...].astype(BF), spread, preferred_element_type=F32)
        d_ref[0, base : base + n, :] = d[:, :WAVES]
        d_ref[1, base : base + n, :] = d[:, WAVES:]
        base += n
    slot = lax.broadcasted_iota(jnp.int32, (1, SLOTS), 1)
    live = slot < live_ref[0]
    offset = (south_ref[...] - (ids[0] * LAT - MARG)).astype(F32)
    low = jnp.where(live, 1.0 - north_ref[...], 0.0)
    high = jnp.where(live, north_ref[...], 0.0)
    kind = jnp.full((1, SLOTS), ids[1], jnp.int32)
    taps = jnp.where(kind == 0, offset, jnp.where(kind == 1, low, high))
    taps = jnp.concatenate([taps, jnp.zeros((1, LAT - SLOTS), F32)], axis=1)
    w_hi, w_lo = hi_lo(w_ref[...])
    k_hi, k_lo = hi_lo(k_ref[...])
    rows = [w_hi.astype(F32), w_lo.astype(F32), k_hi.astype(F32), k_lo.astype(F32), taps]
    small = jnp.concatenate(rows + [jnp.zeros((3, LAT), F32)], axis=0).T
    for c in range(2):
        for i, pick in enumerate((c, 2 + c, 4)):
            d_ref[c, (28 + i) * LAT : (29 + i) * LAT, :] = jnp.broadcast_to(
                small[:, pick : pick + 1], (LAT, WAVES)
            )
        d_ref[c, 31 * LAT : 32 * LAT, :] = jnp.zeros((LAT, WAVES), F32)
    m_hi, m_lo = hi_lo(b_ref[...].T)
    mix = jnp.dot(m_hi, q_ref[...], preferred_element_type=F32)
    mix = (mix + jnp.dot(m_lo, q_ref[...], preferred_element_type=F32)).astype(BF)
    for j in range(XROWS // 8):
        for h in range(8):
            parts = []
            for q in range(2):
                for c in range(2):
                    lo = 2 * j + q
                    if lo < LO:
                        parts.append(d_ref[c, pl.ds(lo * 8 + h, ITEMS, stride=LAT), :])
                    else:
                        parts.append(jnp.zeros((ITEMS, WAVES), F32))
            t_ref[pl.ds(j * 8 + h, WAVES, stride=XROWS), :] = jnp.concatenate(parts, axis=0).T

    def put(m, _):
        o_ref[m, 0:XROWS, :] = t_ref[pl.ds(pl.multiple_of(m * XROWS, 8), XROWS), :].astype(BF)
        o_ref[m, XROWS:CHUNK, :] = mix
        return 0

    lax.fori_loop(0, WAVES, put, 0)


def operator_kernel(ids, wave_ref, table_ref, p_ref, t_ref, d_ref, sem):
    def copy(lo):
        return pltpu.make_async_copy(table_ref.at[ids[1], :, lo], t_ref.at[lo], sem.at[lo])

    for lo in range(LO):
        copy(lo).start()
    degree_count = p_ref.shape[1]
    wave = wave_ref[ids[0] * FIELDS + ids[1]]
    degrees = wave + lax.broadcasted_iota(jnp.int32, (1, degree_count), 1)
    degree_float = degrees.astype(F32)
    damping = 1.0 / (1.0 + degree_damping * degree_float * (degree_float + 1.0))
    damping = jnp.where(degrees < degree_count, damping, 0.0)
    scale = 1.0 / (synth_divisor * math.sqrt(degree_count) * math.sqrt(NLAT))
    for lo in range(LO):
        copy(lo).wait()
        part = t_ref[lo].reshape(BANDS * 8, degree_count)
        d_ref[lo * 256 : (lo + 1) * 256, :] = (part.astype(F32) * damping).astype(BF)
    for lo in range(LO):
        part = t_ref[lo].reshape(BANDS * 8, degree_count)
        p = lax.dot_general(part, d_ref[...], NT, preferred_element_type=F32)
        p_ref[lo * 256 : (lo + 1) * 256, :] = (p * scale).astype(BF)


def tables_kernel(ids, c_ref, a_ref, own_s, own_d, o1, o2, o3, zt_ref, z_ref, so_ref, sr_ref, cp_ref, w_ref, h_ref):
    lon = own_s.shape[1]
    fine = a_ref[0:80, :]
    for q in range(lon // 40):
        ca = a_ref[80 + q : 81 + q, :]
        sa = a_ref[120 + q : 121 + q, :]
        cos = ca * fine[0:40] - sa * fine[40:80]
        sin = sa * fine[0:40] + ca * fine[40:80]
        w_ref[40 * q : 40 * q + 40, 0:WAVES] = cos
        w_ref[40 * q : 40 * q + 40, WAVES:COLS] = -sin
    zt_ref[...] = w_ref[...].astype(BF)
    for x in range(0, lon, 128):
        w = min(128, lon - x)
        for c in range(2):
            z_ref[c * WAVES : (c + 1) * WAVES, x : x + w] = (
                w_ref[x : x + w, c * WAVES : (c + 1) * WAVES].T.astype(BF)
            )
    for j, (sea, damp) in enumerate(
        [(own_s[...], own_d[...])] + [(o[0:SLOTS, :], o[SLOTS:, :]) for o in (o1, o2, o3)]
    ):
        field = (ids[1] + FIELDS - j) % FIELDS
        at = pl.multiple_of(field * SLOTS, SLOTS)
        h_ref[0, pl.ds(at, SLOTS), :] = sea.astype(F32)
        h_ref[1, pl.ds(at, SLOTS), :] = damp.astype(F32)
    for x in range(0, lon, 128):
        w = min(128, lon - x)
        so_ref[x : x + w, :] = h_ref[0, :, x : x + w].T
        sr_ref[x : x + w, :] = 1.0 / (1.0 + ocean_step * h_ref[1, :, x : x + w].T)
    row = lax.broadcasted_iota(jnp.int32, (128, 128), 0)
    col = lax.broadcasted_iota(jnp.int32, (128, 128), 1)
    same = row % SLOTS == col % SLOTS
    couple = jnp.zeros((128, 128), F32)
    for e in range(FIELDS):
        for f in range(FIELDS):
            v = ocean_step * (c_ref[f, e] - c_ref[e, f])
            couple = jnp.where(same & (row // SLOTS == e) & (col // SLOTS == f), v, couple)
    hi, lo = hi_lo(couple)
    cp_ref[0:128, :] = hi
    cp_ref[128:256, :] = lo


def atmosphere_kernel(
    g_ref, sm_ref, sx_ref, se_ref, p_ref, o_ref, a_ref, x_ref, y_ref, f_ref, t_ref
):
    for lo in range(LO):
        lanes = slice(lo * 256, (lo + 1) * 256)
        mix = jnp.concatenate([g_ref[f, 3 + lo] for f in range(FIELDS)], axis=1)
        a_ref[:, lanes] = lax.dot_general(sm_ref[...], mix, NT, preferred_element_type=F32)
        rows = jnp.concatenate([g_ref[f, lo // 2] for f in range(FIELDS)], axis=1)
        x_ref[:, lanes] = lax.dot_general(sx_ref[lo % 2], rows, NT, preferred_element_type=F32)

    def step(k, _):
        weight = x_ref[28 * 8 : 29 * 8, :]
        state = x_ref[0:128, :].reshape(LEVELS, 8, NLAT) * weight[None]
        y_ref[...] = jnp.dot(
            state.reshape(128, NLAT).astype(BF), p_ref[...], preferred_element_type=F32
        )

        def block(n, _):
            lanes = pl.ds(pl.multiple_of(n * 128, 128), 128)
            mid = [
                x_ref[8 * l : 8 * l + 8, lanes] - y_ref[8 * l : 8 * l + 8, lanes]
                for l in range(LEVELS)
            ]
            skin = x_ref[pl.ds(pl.multiple_of(128 + 8 * k, 8), 8), lanes]
            flux = x_ref[29 * 8 : 30 * 8, lanes] * (skin - mid[LEVELS - 1])
            f_ref[n, pl.ds(k, 8, stride=STEPS), :] = flux
            acc = [mixing_diagonal * v for v in mid]
            acc[LEVELS - 1] = acc[LEVELS - 1] + flux
            for i, (l, p) in enumerate(PAIRS):
                a = a_ref[8 * i : 8 * i + 8, lanes]
                acc[l] = acc[l] + a * mid[p]
                acc[p] = acc[p] - a * mid[l]
            for l in range(LEVELS):
                x_ref[8 * l : 8 * l + 8, lanes] = acc[l]
            return 0

        lax.fori_loop(0, NLAT // 128, block, 0)
        return 0

    lax.fori_loop(0, STEPS, step, 0)

    nslot = BANDS * SLOTS
    slot = lax.broadcasted_iota(jnp.int32, (1, nslot), 1)
    south = x_ref[240:241, 0:nslot] + (slot % 256 // 8 * LAT - MARG).astype(F32)
    low = x_ref[242:243, 0:nslot]
    high = x_ref[244:245, 0:nslot]
    for lo in range(LO):
        r = lax.broadcasted_iota(jnp.int32, (256, 1), 0)
        place = (r // 8 * LAT + lo * 8 + r % 8).astype(F32)
        t_ref[lo * 256 : (lo + 1) * 256, :] = jnp.where(
            place == south, low, jnp.where(place == south + 1.0, high, 0.0)
        ).astype(BF)
    flux = jnp.concatenate([f_ref[n].astype(BF) for n in range(NLAT // 128)], axis=1)
    at_slots = jnp.dot(flux, t_ref[...], preferred_element_type=F32) * (-ocean_step / math.sqrt(COLS))
    ends = jnp.concatenate(
        [x_ref[0:128, n * 128 : (n + 1) * 128].T.astype(BF) for n in range(NLAT // 128)], axis=0
    )
    ends = jnp.concatenate([ends[lo * 256 : (lo + 1) * 256] for lo in range(LO)], axis=1)
    ends = jnp.dot(ends, se_ref[...], preferred_element_type=F32)
    for u in range(2):
        pieces = []
        for f in range(FIELDS):
            for s in range(4):
                at = s * 256 + u * 128
                pieces.append(at_slots[f * 24 : f * 24 + 24, at : at + 128])
        for i, v in enumerate(block_transpose(pieces, 8)):
            tile = u * 16 + i
            for f in range(FIELDS):
                o_ref[tile * FIELDS + f, 0:24, :] = v.astype(BF)
    for b in range(BANDS):
        for f in range(FIELDS):
            pair = [ends[8 * b : 8 * b + 8, (q * FIELDS + f) * 128 : (q * FIELDS + f + 1) * 128] for q in range(2)]
            o_ref[b * FIELDS + f, 24:40, :] = jnp.concatenate(pair, axis=0).astype(BF)


def ocean_kernel(
    ids, f_ref, zt_ref, z_ref, c_ref, o0_ref, r_ref, so_ref, co_ref, o_ref, w_ref, p_ref, t_ref, h_ref
):
    lon = o_ref.shape[0]
    start = pl.multiple_of(ids[1] * SLOTS, SLOTS)
    o_ref[...] = o0_ref[...]
    scale = 1.0 / math.sqrt(lon)

    def two_steps(j, _):
        pair = jnp.concatenate([f_ref[2 * j], f_ref[2 * j + 1]], axis=1)
        p_ref[...] = jnp.dot(zt_ref[...], pair, preferred_element_type=F32)
        for i in range(2):
            coarse = o_ref[...].astype(BF)
            pull = jnp.dot(
                jnp.concatenate([coarse, coarse], axis=1), c_ref[...], preferred_element_type=F32
            )
            updated = (o_ref[...] + (pull + p_ref[:, i * 128 : (i + 1) * 128])) * r_ref[...]
            o_ref[...] = updated
            w_ref[:, i * 128 : (i + 1) * 128] = updated.astype(BF)
        coef = jnp.dot(z_ref[...], w_ref[...], preferred_element_type=F32) * scale
        for i in range(2):
            h_ref[i] = coef[:, i * 128 : (i + 1) * 128].T
            at = pl.multiple_of((2 * j + i) * SLOTS, SLOTS)
            t_ref[pl.ds(at, SLOTS), :] = h_ref[i, pl.ds(start, SLOTS), :]
        return 0

    lax.fori_loop(0, STEPS // 2, two_steps, 0)
    co_ref[...] = jnp.dot(t_ref[...].astype(BF), join_columns(), preferred_element_type=F32).astype(BF)
    for x in range(0, lon, 128):
        w = min(128, lon - x)
        h_ref[0, :, 0:w] = o_ref[x : x + w, :].T
        so_ref[:, x : x + w] = h_ref[0, pl.ds(start, SLOTS), 0:w]


def unpack_kernel(b_ref, o_ref, t_ref, v_ref):
    def take(m, _):
        t_ref[pl.ds(pl.multiple_of(m * 16, 16), 16), :] = b_ref[m, 24:40, :].astype(F32)
        return 0

    lax.fori_loop(0, WAVES, take, 0)
    for q in range(2):
        for h in range(8):
            v = t_ref[pl.ds(q * 8 + h, WAVES, stride=16), :].T
            for i in range(4 if q == 0 else 1):
                for c in range(2):
                    at = i * 32 + c * LEVELS
                    v_ref[c, pl.ds((4 * q + i) * 8 + h, LEVELS, stride=LAT), :] = v[at : at + LEVELS]
    both = jnp.concatenate([v_ref[0], v_ref[1]], axis=1).astype(BF)
    o_ref[...] = jnp.dot(both, join_columns(), preferred_element_type=F32)


def vmem(n):
    return [pl.BlockSpec(memory_space=pltpu.VMEM)] * n


def smem(n):
    return [pl.BlockSpec(memory_space=pltpu.SMEM)] * n


def call(kernel, in_specs, out_shape, scratch):
    return pl.pallas_call(
        kernel,
        out_shape=out_shape,
        in_specs=in_specs,
        out_specs=jax.tree.map(lambda _: pl.BlockSpec(memory_space=pltpu.VMEM), out_shape),
        scratch_shapes=scratch,
    )


def shape(dims, kind):
    return jax.ShapeDtypeStruct(dims, kind)


def per_device(
    air_fourier_coefficients,
    quadrature_factor,
    associated_polynomial_table,
    east_west_harmonic,
    boundary_diffusion,
    bulk_transfer_coefficient,
    skin_heat_earlier,
    sea_boundary_values,
    sea_damping_speed,
    sea_coupling_matrix,
    patch_active_entries,
    sea_southern_parallel,
    sea_northern_share,
    air_paired_cells,
    air_second_share,
):
    band = lax.axis_index("band")
    lev = lax.axis_index("lev")
    ids = jnp.stack([band, lev]).astype(jnp.int32)
    lon = sea_boundary_values.shape[2]
    degree_count = associated_polynomial_table.shape[2]

    chunks = call(
        pack_kernel,
        smem(2) + vmem(8),
        shape((WAVES, CHUNK, 128), BF),
        [pltpu.VMEM((2, ITEMS * LAT, 128), F32), pltpu.VMEM((WAVES * XROWS, 128), F32)],
    )(
        ids,
        patch_active_entries,
        air_fourier_coefficients.reshape(LEVELS * LAT, COLS),
        skin_heat_earlier.reshape(STEPS * LAT, COLS),
        boundary_diffusion.reshape(LEVELS * LEVELS, LAT),
        quadrature_factor[None],
        bulk_transfer_coefficient,
        sea_southern_parallel[None],
        sea_northern_share[None],
        jnp.asarray(pair_matrix(), BF),
    )
    got = lax.all_to_all(chunks, AXES, 0, 0, tiled=True)

    operator = call(
        operator_kernel,
        smem(2) + [pl.BlockSpec(memory_space=pl.ANY)],
        shape((NLAT, NLAT), BF),
        [
            pltpu.VMEM((LO, BANDS, 8, degree_count), BF),
            pltpu.VMEM((NLAT, degree_count), BF),
            pltpu.SemaphoreType.DMA((LO,)),
        ],
    )(ids, east_west_harmonic, associated_polynomial_table.reshape(FIELDS, BANDS, LO, 8, degree_count))

    row = jnp.arange(NPAIR * 8, dtype=jnp.int32)[:, None]
    col = jnp.arange(FIELDS * 128, dtype=jnp.int32)[None, :]
    select_mix = ((row // 8 == col % 128) & (row % 8 // 2 == col // 128)).astype(BF)
    row = jnp.arange(ITEMS * 8, dtype=jnp.int32)[:, None]
    item = row // 8
    same = (col % ITEMS == item) & (col // 128 == row % 8 // 2)
    same_c = (col % 64 // ITEMS == row % 2) | (item == 28) | (item == 29)
    select_x = jnp.stack([same & same_c & (col % 128 // 64 == q) for q in range(2)]).astype(BF)
    row = jnp.arange(LO * 128, dtype=jnp.int32)[:, None]
    col = jnp.arange(2 * FIELDS * 128, dtype=jnp.int32)[None, :]
    lo = col // 512 * 4 + col % 128 // 32
    at = lo * 128 + col % LEVELS * 8 + col % 512 // 128 * 2 + col % 32 // LEVELS
    select_end = (row == at).astype(BF)

    part = jnp.arange(160, dtype=jnp.int32)[:, None]
    longitude = jnp.where(part < 80, part % 40, part % 40 * 40)
    phases = longitude * east_west_harmonic[None, :] % lon
    angles = phases.astype(F32) * (2.0 * math.pi / lon)
    angle_parts = jnp.where(part // 40 % 2 == 0, jnp.cos(angles), jnp.sin(angles))
    own_sea, own_damp, operator = lax.optimization_barrier((sea_boundary_values[0], sea_damping_speed[0], operator))
    sent = jnp.concatenate([own_sea.astype(BF), own_damp.astype(BF)], axis=0)
    others = []
    for d in range(1, FIELDS):
        others.append(lax.ppermute(sent, "lev", [(i, (i + d) % FIELDS) for i in range(FIELDS)]))
    zonal_t, zonal, ocean0, shrink, couple = call(
        tables_kernel,
        smem(2) + vmem(6),
        (
            shape((lon, COLS), BF),
            shape((COLS, lon), BF),
            shape((lon, 128), F32),
            shape((lon, 128), F32),
            shape((256, 128), BF),
        ),
        [pltpu.VMEM((lon, COLS), F32), pltpu.VMEM((2, 128, lon), F32)],
    )(ids, sea_coupling_matrix, angle_parts, own_sea, own_damp, *others)

    got, zonal_t, zonal, ocean0, shrink, couple = lax.optimization_barrier(
        (got, zonal_t, zonal, ocean0, shrink, couple)
    )
    got = got.reshape(BANDS, FIELDS, 8, 8, 128).transpose(1, 2, 0, 3, 4).reshape(FIELDS, 8, 256, 128)
    out = call(
        atmosphere_kernel,
        vmem(5),
        shape((WAVES, OUT_ROWS, 128), BF),
        [
            pltpu.VMEM((NPAIR * 8, NLAT), F32),
            pltpu.VMEM((ITEMS * 8, NLAT), F32),
            pltpu.VMEM((128, NLAT), F32),
            pltpu.VMEM((NLAT // 128, STEPS * 8, 128), F32),
            pltpu.VMEM((NLAT, BANDS * SLOTS), BF),
        ],
    )(got, select_mix, select_x, select_end, operator)

    back = lax.all_to_all(out, AXES, 0, 0, tiled=True)
    flux_in = back[:, :24].reshape(WAVES, 2, STEPS, 128).transpose(2, 1, 0, 3).reshape(STEPS, COLS, 128)
    sea_end, ocean_coef = call(
        ocean_kernel,
        smem(1) + vmem(6),
        (shape((SLOTS, lon), F32), shape((STEPS * SLOTS, COLS), BF)),
        [
            pltpu.VMEM((lon, 128), F32),
            pltpu.VMEM((lon, COLS), BF),
            pltpu.VMEM((lon, COLS), F32),
            pltpu.VMEM((STEPS * SLOTS, COLS), F32),
            pltpu.VMEM((2, 128, COLS), F32),
        ],
    )(ids, flux_in, zonal_t, zonal, couple, ocean0, shrink)
    ocean_coef = ocean_coef.reshape(STEPS, SLOTS, COLS)
    air_coefficients_end = call(
        unpack_kernel,
        vmem(1),
        shape((LEVELS * LAT, COLS), F32),
        [pltpu.VMEM((WAVES * 16, 128), F32), pltpu.VMEM((2, LEVELS * LAT, 128), F32)],
    )(back).reshape(1, LEVELS, LAT, COLS)

    up = [(i, i + 1) for i in range(BANDS - 1)]
    down = [(j, i) for i, j in up]
    before = lax.ppermute(ocean_coef, "band", up)
    after = lax.ppermute(ocean_coef, "band", down)
    neighbours = jnp.concatenate([before, ocean_coef, after], axis=1)
    slot_index = jnp.arange(3 * SLOTS, dtype=jnp.int32)[None, :]
    first = (air_paired_cells[0] - (band - 1) * SLOTS)[:, None]
    second = (air_paired_cells[1] - (band - 1) * SLOTS)[:, None]
    return_taps = jnp.where(slot_index == first, (1.0 - air_second_share)[:, None], 0.0) + jnp.where(
        slot_index == second, air_second_share[:, None], 0.0
    )
    skin_heat_newest = jnp.einsum(
        "ga,kac->kgc", return_taps.astype(BF), neighbours, preferred_element_type=F32
    )[:, None]
    return (air_coefficients_end, sea_end[None], skin_heat_newest)


def solution(mesh):
    return jax.shard_map(
        per_device,
        mesh=mesh,
        in_specs=(
            P("lev", None, "band", None),
            P("band"),
            P("band", None, None),
            P(),
            P("lev", None, None, "band"),
            P("lev", "band"),
            P(None, "lev", "band", None),
            P("lev", "band", None),
            P("lev", "band", None),
            P(),
            P("band"),
            P("band"),
            P("band"),
            P(None, "band"),
            P("band"),
        ),
        out_specs=(
            P("lev", None, "band", None),
            P("lev", "band", None),
            P(None, "lev", "band", None),
        ),
        check_vma=False,
    )
```

time: 215 us -> 139 us (0.65)
  local copies, waits for them, and re-layouts: 72.9 us -> 4.66 us
  other arithmetic: 34 us -> 5.92 us
  waiting for transfers between devices: 23.4 us -> 40.1 us
  Pallas kernels: 41.3 us -> 57.3 us
  matrix products: 10.7 us -> 1.05 us
  starting transfers between devices: 29.8 us -> 26.4 us
    reshape x11 -> x1, local copies, waits for them, and re-layouts: 25.5 us -> 1.9 us  [per_device(): got.reshape(BANDS, FIELDS, 8, 8, 128).transpose(1, 2, 0, 3, 4)]
    all_to_all x1, waiting for transfers between devices: 0.01 us -> 19 us  [per_device(): got = lax.all_to_all(chunks, AXES, 0, 0, tiled=True)]
    pallas_call x3 -> x6, Pallas kernels: 41.3 us -> 57.3 us  [the longest x1 25.6 us: per_device(): call(atmosphere_kernel, vmem(5), shape((WAVES, OUT_ROWS, 128), BF), [pltp...]
    convert_element_type x9 -> x4, other arithmetic: 15.7 us -> 2.37 us  [the longest x1 1.49 us: per_device(): select_end = (row == at).astype(BF)]
    another operation x3 -> x0, local copies, waits for them, and re-layouts: 10.1 us -> none  [the longest x1 5.91 us: per_device(): tap = gotx.reshape(BANDS, FIELDS, HALF, 2, 2, ITEMS)[:, :3, :, 0, :, 30]]
    convert_element_type x2 -> x0, local copies, waits for them, and re-layouts: 9.94 us -> none  [per_device(): damped = (table * damping).astype(BF)]
    dot_general x2 -> x0, matrix products: 9.65 us -> none  [the longest x1 7.79 us: per_device(): operator = lax.dot_general(table, damped, NT, preferred_element_type=F32)]
    slice x10 -> x0, local copies, waits for them, and re-layouts: 8.88 us -> none  [the longest x2 4.68 us: per_device(): tap = gotx.reshape(BANDS, FIELDS, HALF, 2, 2, ITEMS)[:, :3, :, 0, :, 30]]
  transfers between devices with their start and end apart: 7 -> 7, of which waited for: 3 -> 2; matrix products, arithmetic and copies ran while one was open for 33% -> 4% of each run, Pallas kernels for 2% -> 8%
where the time goes in v2:
time: 139 us; the launch traced here: 137 us
  Pallas kernels  57.3 us (41%)
  waiting for transfers between devices  40.1 us (29%)
  starting transfers between devices  26.4 us (19%)
  other arithmetic  5.92 us (4%)
  local copies, waits for them, and re-layouts  4.66 us (3%)
  between operations  1.52 us (1%)
    pallas_call x1, Pallas kernels, per_device(): call(atmosphere_kernel, vmem(5), shape((WAVES, OUT_ROWS, 128), BF), [pltp...  25.6 us
    all_to_all x1, waiting for transfers between devices, per_device(): back = lax.all_to_all(out, AXES, 0, 0, tiled=True)  21.1 us
    all_to_all x1, waiting for transfers between devices, per_device(): got = lax.all_to_all(chunks, AXES, 0, 0, tiled=True)  19 us
    pallas_call x1, Pallas kernels, per_device(): call(ocean_kernel, smem(1) + vmem(6), (shape((SLOTS, lon), F32), shape((S...  11.4 us
    pallas_call x1, Pallas kernels, per_device(): call(operator_kernel, smem(2) + [pl.BlockSpec(memory_space=pl.ANY)], shap...  8.86 us
    all_to_all x1, starting transfers between devices, per_device(): got = lax.all_to_all(chunks, AXES, 0, 0, tiled=True)  7.7 us
    ppermute x3, starting transfers between devices, per_device(): lax.ppermute(sent, 'lev', [(i, (i + d) % FIELDS) for i in range(FIELDS)])  5.9 us
    ppermute x1, starting transfers between devices, per_device(): after = lax.ppermute(ocean_coef, 'band', down)  5.65 us
  transfers between devices with their start and end apart: 7, of which 2 were waited for; matrix products, arithmetic and copies ran while one was open for 4% of the time, Pallas kernels for 8%

profile of v2, /device:TPU:32, one launch (start us, length us, event | category | flops | bytes accessed | tf_op | source)
XLA Modules:
  0.0 137.0 jit_solution(4827747404274094970)
XLA Ops:
  0.6 0.6 pad_add_fusion.ids
  1.2 0.0 copy-start.1
  1.2 0.0 copy-start.2
  1.2 8.9 %shard_map.176.p_ref = bf16[1280,1280]{1,0:T(8,128)(2,1)} custom-call(s32[2]{0:T(128)} %pad_add_fusion.ids, s32[128]{0:T(128)} %wave_ref.1, bf16[4,32,5,8,1280]{4,3,2,1,0:T(8,128)(2,1)} %bitcast.37), custom_call_target="tpu_custom_call" | custom-call | tf_op jit(solution)/shard_map/pallas_call | solution.py:381
  10.1 0.0 copy-done.1
  10.1 0.0 copy-done.2
  10.2 1.6 %collective-permute-start = (bf16[64,1440]{1,0:T(8,128)(2,1)S(1)}, bf16[64,1440]{1,0:T(8,128)(2,1)S(1)}, u32[]{:S(2)}, u32[]{:S(2)}) collective-permute-start(bf16[64,1440]{1,0:T(8,128)(2,1)S(1)} %pad_maximum_fusion), channel_id=1, source_target_pairs={{0,1},{1,2},{2,3},{3,0},{4,5},{5,6},{6,7},{7,4},{8,9},{9,10},{10,1... | collective-permute-start | bytes 552968 | tf_op jit(solution)/shard_map/ppermute | solution.py:415
  11.8 2.9 %collective-permute-start.1 = (bf16[64,1440]{1,0:T(8,128)(2,1)S(1)}, bf16[64,1440]{1,0:T(8,128)(2,1)S(1)}, u32[]{:S(2)}, u32[]{:S(2)}) collective-permute-start(bf16[64,1440]{1,0:T(8,128)(2,1)S(1)} %pad_maximum_fusion), channel_id=1, source_target_pairs={{0,2},{1,3},{2,0},{3,1},{4,6},{5,7},{6,4},{7,5},{8,10},{9,11},{10,... | collective-permute-start | bytes 552968 | tf_op jit(solution)/shard_map/ppermute | solution.py:415
  14.7 1.3 collective-permute-start.2
  16.7 4.3 %shard_map.175 = bf16[128,64,128]{2,1,0:T(8,128)(2,1)} custom-call(s32[2]{0:T(128)} %pad_add_fusion.ids, s32[1]{0:T(128)S(6)} %copy.28.live_ref, f32[640,256]{1,0:T(8,128)} %bitcast.46, f32[480,256]{1,0:T(8,128)} %bitcast.48, f32[256,40]{1,0:T(8,128)} %bitcast.49, f32[1,40]{1,0:T(1,128)} %bitcast.50, f32[1,40]{1,0:T(1,128)} %k_ref.1, s32[1,32]{1,0:T(1,128)} %bitcast.51, ...), custom_call_target="tpu_custom_call" | custom-call | tf_op jit(solution)/shard_map/pallas_call | solution.py:362
  21.0 7.7 %all-to-all-start = ((bf16[128,64,128]{2,1,0:T(8,128)(2,1)}), bf16[128,64,128]{2,1,0:T(8,128)(2,1)S(1)}, u32[]{:S(2)}, u32[]{:S(2)}) async-start(bf16[128,64,128]{2,1,0:T(8,128)(2,1)} %shard_map.175), calls=%async_computation | async-start | bytes 4194304 | tf_op jit(solution)/shard_map/all_to_all | solution.py:379
  28.7 0.0 copy-start.6
  28.9 0.4 broadcast_and_fusion.1
  29.3 0.9 add_convert_fusion.sx_ref
  30.2 1.4 %and_convert_fusion.sm_ref = bf16[960,512]{1,0:T(8,128)(2,1)} fusion(s32[512]{0:T(512)S(1)} %get-tuple-element.47, s32[512]{0:T(512)S(1)} %get-tuple-element.48, s32[960]{0:T(1024)S(1)} %get-tuple-element.45, s32[960]{0:T(1024)S(1)} %get-tuple-element.46), kind=kLoop, calls=%fused_computation.3 | loop fusion | flops 1966080 | bytes 994816 | tf_op jit(solution)/shard_map/convert_element_type | solution.py:394
  31.5 1.5 %fusion.se_ref = bf16[640,1024]{1,0:T(8,128)(2,1)} fusion(s32[1024]{0:T(1024)S(1)} %fusion.48), kind=kLoop, calls=%fused_computation.1 | loop fusion | flops 1310720 | bytes 1314816 | tf_op jit(solution)/shard_map/convert_element_type | solution.py:404
  33.0 0.0 copy-done.6
  33.0 1.1 sine_select_fusion.a_ref
  34.1 0.0 collective-permute-done.o1
  34.1 0.0 copy-start.3
  34.1 0.0 collective-permute-done.1.o2
  34.1 0.0 copy-start.4
  34.1 0.0 collective-permute-done.2.o3
  34.1 0.6 copy-done.3
  34.8 0.1 copy-done.4
  34.8 0.0 copy-start.5
  34.8 0.7 copy-done.5
  35.5 3.7 %shard_map.177 = (bf16[1440,256]{1,0:T(8,128)(2,1)}, bf16[256,1440]{1,0:T(8,128)(2,1)}, f32[1440,128]{1,0:T(8,128)}, f32[1440,128]{1,0:T(8,128)}, bf16[256,128]{1,0:T(8,128)(2,1)}) custom-call(s32[2]{0:T(128)} %pad_add_fusion.ids, f32[4,4]{1,0:T(4,128)} %c_ref.1, f32[160,128]{1,0:T(8,128)} %sine_select_fusion.a_ref, f32[32,1440]{1,0:T(8,128)} %bitcast.42, ...), custom_call_target="tpu_custom_call" | custom-call | tf_op jit(solution)/shard_map/pallas_call | solution.py:416
  39.2 19.0 %all-to-all-done = bf16[128,64,128]{2,1,0:T(8,128)(2,1)S(1)} async-done(((bf16[128,64,128]{2,1,0:T(8,128)(2,1)}), bf16[128,64,128]{2,1,0:T(8,128)(2,1)S(1)}, u32[]{:S(2)}, u32[]{:S(2)}) %all-to-all-start) | async-done | bytes 2097184 | tf_op jit(solution)/shard_map/all_to_all | solution.py:379
  58.2 1.9 %copy.27 = bf16[32,4,8,8,128]{4,3,0,2,1:T(8,128)(2,1)} copy(bf16[32,4,8,8,128]{4,3,2,1,0:T(8,128)(2,1)S(1)} %bitcast.38) | data formatting | bytes 4194304 | tf_op jit(solution)/shard_map/reshape | solution.py:432
  60.1 25.6 %shard_map.178 = bf16[128,40,128]{2,1,0:T(8,128)(2,1)} custom-call(bf16[4,8,256,128]{3,2,1,0:T(8,128)(2,1)} %bitcast.39, bf16[960,512]{1,0:T(8,128)(2,1)} %and_convert_fusion.sm_ref, bf16[2,256,512]{2,1,0:T(8,128)(2,1)} %add_convert_fusion.sx_ref, bf16[640,1024]{1,0:T(8,128)(2,1)} %fusion.se_ref, bf16[1280,1280]{1,0:T(8,128)(2,1)} %shard_map.176.p_ref), custom_call_target="tpu_custom_call" | custom-call | tf_op jit(solution)/shard_map/pallas_call | solution.py:433
  85.6 0.0 copy-start.7
  85.6 5.0 %all-to-all-start.1 = ((bf16[128,40,128]{2,1,0:T(8,128)(2,1)}), bf16[128,40,128]{2,1,0:T(8,128)(2,1)S(1)}, u32[]{:S(2)}, u32[]{:S(2)}) async-start(bf16[128,40,128]{2,1,0:T(8,128)(2,1)} %shard_map.178), calls=%async_computation.1 | async-start | bytes 2621440 | tf_op jit(solution)/shard_map/all_to_all | solution.py:446
  90.7 0.0 copy-done.7
  90.7 21.1 %all-to-all-done.1.b_ref = bf16[128,40,128]{2,1,0:T(8,128)(2,1)S(1)} async-done(((bf16[128,40,128]{2,1,0:T(8,128)(2,1)}), bf16[128,40,128]{2,1,0:T(8,128)(2,1)S(1)}, u32[]{:S(2)}, u32[]{:S(2)}) %all-to-all-start.1) | async-done | bytes 1310752 | tf_op jit(solution)/shard_map/all_to_all | solution.py:446
  111.8 0.1 slice.12
  111.9 0.2 copy.23
  112.1 1.1 copy.24
  113.1 0.0 copy-done
  113.2 11.4 %shard_map.180 = (f32[32,1440]{1,0:T(8,128)}, bf16[384,256]{1,0:T(8,128)(2,1)}) custom-call(s32[2]{0:T(128)} %pad_add_fusion.ids, bf16[12,256,128]{2,1,0:T(8,128)(2,1)} %bitcast.41, bf16[1440,256]{1,0:T(8,128)(2,1)} %get-tuple-element.28.zt_ref, bf16[256,1440]{1,0:T(8,128)(2,1)} %get-tuple-element.29.z_ref, bf16[256,128]{1,0:T(8,128)(2,1)} %get-tuple-element.30.c_ref, ...), custom_call_target="tpu_custom_call" | custom-call | tf_op jit(solution)/shard_map/pallas_call | solution.py:448
  124.5 2.1 %collective-permute-start.3 = (bf16[12,32,256]{2,1,0:T(8,128)(2,1)}, bf16[12,32,256]{2,1,0:T(8,128)(2,1)S(1)}, u32[]{:S(2)}, u32[]{:S(2)}) collective-permute-start(bf16[12,32,256]{2,1,0:T(8,128)(2,1)} %bitcast.54), channel_id=1, source_target_pairs={{0,4},{4,8},{8,12},{12,16},{16,20},{20,24},{24,28},{28,32},{32,36}... | collective-permute-start | bytes 589832 | tf_op jit(solution)/shard_map/ppermute | solution.py:470
  126.7 5.7 %collective-permute-start.4 = (bf16[12,32,256]{2,1,0:T(8,128)(2,1)}, bf16[12,32,256]{2,1,0:T(8,128)(2,1)S(1)}, u32[]{:S(2)}, u32[]{:S(2)}) collective-permute-start(bf16[12,32,256]{2,1,0:T(8,128)(2,1)} %bitcast.55), channel_id=1, source_target_pairs={{4,0},{8,4},{12,8},{16,12},{20,16},{24,20},{28,24},{32,28},{36,32}... | collective-permute-start | bytes 589832 | tf_op jit(solution)/shard_map/ppermute | solution.py:471
  132.4 0.0 copy-done.9
  132.4 3.6 %shard_map.179 = f32[640,256]{1,0:T(8,128)} custom-call(bf16[128,40,128]{2,1,0:T(8,128)(2,1)} %copy-done), custom_call_target="tpu_custom_call" | custom-call | tf_op jit(solution)/shard_map/pallas_call | solution.py:461
  136.0 0.0 collective-permute-done.3
  136.0 0.0 collective-permute-done.4
  136.0 0.0 copy-done.8
  136.0 1.1 convolution_bitcast_fusion
  (18 shorter events, 0.2 us)
Async XLA Ops:
  1.2 8.9 %copy-start.1 = (f32[1,32,1440]{2,1,0:T(8,128)S(1)}, f32[1,32,1440]{2,1,0:T(8,128)}, u32[]{:S(2)}) copy-start(f32[1,32,1440]{2,1,0:T(8,128)} %param.23) | copy-start | bytes 552964
  1.2 8.9 %copy-start.2 = (f32[1,32,1440]{2,1,0:T(8,128)S(1)}, f32[1,32,1440]{2,1,0:T(8,128)}, u32[]{:S(2)}) copy-start(f32[1,32,1440]{2,1,0:T(8,128)} %param.24) | copy-start | bytes 552964
  10.2 23.9 %collective-permute-start = (bf16[64,1440]{1,0:T(8,128)(2,1)S(1)}, bf16[64,1440]{1,0:T(8,128)(2,1)S(1)}, u32[]{:S(2)}, u32[]{:S(2)}) collective-permute-start(bf16[64,1440]{1,0:T(8,128)(2,1)S(1)} %pad_maximum_fusion), channel_id=1, source_target_pairs={{0,1},{1,2},{2,3},{3,0},{4,5},{5,6},{6,7},{7,4},{8,9},{9,10},{10,1... | collective-permute-start | bytes 552968 | tf_op jit(solution)/shard_map/ppermute | solution.py:415
  11.8 22.3 %collective-permute-start.1 = (bf16[64,1440]{1,0:T(8,128)(2,1)S(1)}, bf16[64,1440]{1,0:T(8,128)(2,1)S(1)}, u32[]{:S(2)}, u32[]{:S(2)}) collective-permute-start(bf16[64,1440]{1,0:T(8,128)(2,1)S(1)} %pad_maximum_fusion), channel_id=1, source_target_pairs={{0,2},{1,3},{2,0},{3,1},{4,6},{5,7},{6,4},{7,5},{8,10},{9,11},{10,... | collective-permute-start | bytes 552968 | tf_op jit(solution)/shard_map/ppermute | solution.py:415
  14.7 19.4 %collective-permute-start.2 = (bf16[64,1440]{1,0:T(8,128)(2,1)S(1)}, bf16[64,1440]{1,0:T(8,128)(2,1)S(1)}, u32[]{:S(2)}, u32[]{:S(2)}) collective-permute-start(bf16[64,1440]{1,0:T(8,128)(2,1)S(1)} %pad_maximum_fusion), channel_id=1, source_target_pairs={{0,3},{1,0},{2,1},{3,2},{4,7},{5,4},{6,5},{7,6},{8,11},{9,8},{10,9... | collective-permute-start | bytes 552968 | tf_op jit(solution)/shard_map/ppermute | solution.py:415
  21.0 37.1 %all-to-all-start = ((bf16[128,64,128]{2,1,0:T(8,128)(2,1)}), bf16[128,64,128]{2,1,0:T(8,128)(2,1)S(1)}, u32[]{:S(2)}, u32[]{:S(2)}) async-start(bf16[128,64,128]{2,1,0:T(8,128)(2,1)} %shard_map.175), calls=%async_computation | async-start | bytes 4194304 | tf_op jit(solution)/shard_map/all_to_all | solution.py:379
  28.7 4.3 %copy-start.6 = (s32[128]{0:T(128)S(1)}, s32[128]{0:T(128)}, u32[]{:S(2)}) copy-start(s32[128]{0:T(128)} %wave_ref.1) | copy-start | bytes 1540
  34.1 0.7 copy-start.3
  34.1 0.7 copy-start.4
  34.8 0.7 copy-start.5
  85.6 5.0 %copy-start.7 = (s32[2,40]{1,0:T(2,128)S(1)}, s32[2,40]{1,0:T(2,128)}, u32[]{:S(2)}) copy-start(s32[2,40]{1,0:T(2,128)} %param.29) | copy-start | bytes 964
  85.6 26.2 %all-to-all-start.1 = ((bf16[128,40,128]{2,1,0:T(8,128)(2,1)}), bf16[128,40,128]{2,1,0:T(8,128)(2,1)S(1)}, u32[]{:S(2)}, u32[]{:S(2)}) async-start(bf16[128,40,128]{2,1,0:T(8,128)(2,1)} %shard_map.178), calls=%async_computation.1 | async-start | bytes 2621440 | tf_op jit(solution)/shard_map/all_to_all | solution.py:446
  111.8 1.3 copy-start
  113.2 19.2 %copy-start.9 = (f32[40]{0:T(128)S(1)}, f32[40]{0:T(128)}, u32[]{:S(2)}) copy-start(f32[40]{0:T(128)} %param.30) | copy-start | bytes 484
  124.5 11.4 %copy-start.8 = (bf16[384,256]{1,0:T(8,128)(2,1)S(1)}, bf16[384,256]{1,0:T(8,128)(2,1)}, u32[]{:S(2)}) copy-start(bf16[384,256]{1,0:T(8,128)(2,1)} %get-tuple-element.34) | copy-start | bytes 589828
  124.5 11.4 %collective-permute-start.3 = (bf16[12,32,256]{2,1,0:T(8,128)(2,1)}, bf16[12,32,256]{2,1,0:T(8,128)(2,1)S(1)}, u32[]{:S(2)}, u32[]{:S(2)}) collective-permute-start(bf16[12,32,256]{2,1,0:T(8,128)(2,1)} %bitcast.54), channel_id=1, source_target_pairs={{0,4},{4,8},{8,12},{12,16},{16,20},{20,24},{24,28},{28,32},{32,36}... | collective-permute-start | bytes 589832 | tf_op jit(solution)/shard_map/ppermute | solution.py:470
  126.7 9.3 %collective-permute-start.4 = (bf16[12,32,256]{2,1,0:T(8,128)(2,1)}, bf16[12,32,256]{2,1,0:T(8,128)(2,1)S(1)}, u32[]{:S(2)}, u32[]{:S(2)}) collective-permute-start(bf16[12,32,256]{2,1,0:T(8,128)(2,1)} %bitcast.55), channel_id=1, source_target_pairs={{4,0},{8,4},{12,8},{16,12},{20,16},{24,20},{28,24},{32,28},{36,32}... | collective-permute-start | bytes 589832 | tf_op jit(solution)/shard_map/ppermute | solution.py:471

commit v3 on v2

--- a/solution.py
+++ b/solution.py
@@ -189,7 +189,7 @@
 
 
 def atmosphere_kernel(
-    g_ref, sm_ref, sx_ref, se_ref, p_ref, o_ref, a_ref, x_ref, y_ref, f_ref, t_ref
+    g_ref, sm_ref, sx_ref, se_ref, p_ref, o_ref, a_ref, x_ref, y_ref, s_ref, f_ref, t_ref
 ):
     for lo in range(LO):
         lanes = slice(lo * 256, (lo + 1) * 256)
@@ -198,33 +198,42 @@
         rows = jnp.concatenate([g_ref[f, lo // 2] for f in range(FIELDS)], axis=1)
         x_ref[:, lanes] = lax.dot_general(sx_ref[lo % 2], rows, NT, preferred_element_type=F32)
 
+    weight = x_ref[28 * 8 : 29 * 8, :]
+    for l in range(0, LEVELS, 2):
+        pair = x_ref[8 * l : 8 * l + 16, :].reshape(2, 8, NLAT) * weight[None]
+        s_ref[0, 8 * l : 8 * l + 16, :] = pair.reshape(16, NLAT).astype(BF)
+
+    def mix_block(k, n, half):
+        lanes = slice(n * 256 + half * 128, n * 256 + half * 128 + 128)
+        mid = [
+            x_ref[8 * l : 8 * l + 8, lanes] - y_ref[n, 8 * l : 8 * l + 8, half * 128 : half * 128 + 128]
+            for l in range(LEVELS)
+        ]
+        skin = x_ref[pl.ds(pl.multiple_of(128 + 8 * k, 8), 8), lanes]
+        flux = x_ref[29 * 8 : 30 * 8, lanes] * (skin - mid[LEVELS - 1])
+        f_ref[2 * n + half, pl.ds(k, 8, stride=STEPS), :] = flux
+        acc = [mixing_diagonal * v for v in mid]
+        acc[LEVELS - 1] = acc[LEVELS - 1] + flux
+        for i, (l, p) in enumerate(PAIRS):
+            a = a_ref[8 * i : 8 * i + 8, lanes]
+            acc[l] = acc[l] + a * mid[p]
+            acc[p] = acc[p] - a * mid[l]
+        scale = x_ref[28 * 8 : 29 * 8, lanes]
+        for l in range(LEVELS):
+            x_ref[8 * l : 8 * l + 8, lanes] = acc[l]
+        for l in range(0, LEVELS, 2):
+            pair = jnp.concatenate([acc[l] * scale, acc[l + 1] * scale], axis=0)
+            s_ref[1 - k % 2, 8 * l : 8 * l + 16, lanes] = pair.astype(BF)
+
     def step(k, _):
-        weight = x_ref[28 * 8 : 29 * 8, :]
-        state = x_ref[0:128, :].reshape(LEVELS, 8, NLAT) * weight[None]
-        y_ref[...] = jnp.dot(
-            state.reshape(128, NLAT).astype(BF), p_ref[...], preferred_element_type=F32
-        )
-
-        def block(n, _):
-            lanes = pl.ds(pl.multiple_of(n * 128, 128), 128)
-            mid = [
-                x_ref[8 * l : 8 * l + 8, lanes] - y_ref[8 * l : 8 * l + 8, lanes]
-                for l in range(LEVELS)
-            ]
-            skin = x_ref[pl.ds(pl.multiple_of(128 + 8 * k, 8), 8), lanes]
-            flux = x_ref[29 * 8 : 30 * 8, lanes] * (skin - mid[LEVELS - 1])
-            f_ref[n, pl.ds(k, 8, stride=STEPS), :] = flux
-            acc = [mixing_diagonal * v for v in mid]
-            acc[LEVELS - 1] = acc[LEVELS - 1] + flux
-            for i, (l, p) in enumerate(PAIRS):
-                a = a_ref[8 * i : 8 * i + 8, lanes]
-                acc[l] = acc[l] + a * mid[p]
-                acc[p] = acc[p] - a * mid[l]
-            for l in range(LEVELS):
-                x_ref[8 * l : 8 * l + 8, lanes] = acc[l]
-            return 0
-
-        lax.fori_loop(0, NLAT // 128, block, 0)
+        for n in range(LO + 1):
+            if n < LO:
+                y_ref[n] = jnp.dot(
+                    s_ref[k % 2], p_ref[:, n * 256 : (n + 1) * 256], preferred_element_type=F32
+                )
+            if n > 0:
+                mix_block(k, n - 1, 0)
+                mix_block(k, n - 1, 1)
         return 0
 
     lax.fori_loop(0, STEPS, step, 0)
@@ -408,7 +417,7 @@
     phases = longitude * east_west_harmonic[None, :] % lon
     angles = phases.astype(F32) * (2.0 * math.pi / lon)
     angle_parts = jnp.where(part // 40 % 2 == 0, jnp.cos(angles), jnp.sin(angles))
-    own_sea, own_damp, operator = lax.optimization_barrier((sea_boundary_values[0], sea_damping_speed[0], operator))
+    own_sea, own_damp = sea_boundary_values[0], sea_damping_speed[0]
     sent = jnp.concatenate([own_sea.astype(BF), own_damp.astype(BF)], axis=0)
     others = []
     for d in range(1, FIELDS):
@@ -426,9 +435,6 @@
         [pltpu.VMEM((lon, COLS), F32), pltpu.VMEM((2, 128, lon), F32)],
     )(ids, sea_coupling_matrix, angle_parts, own_sea, own_damp, *others)
 
-    got, zonal_t, zonal, ocean0, shrink, couple = lax.optimization_barrier(
-        (got, zonal_t, zonal, ocean0, shrink, couple)
-    )
     got = got.reshape(BANDS, FIELDS, 8, 8, 128).transpose(1, 2, 0, 3, 4).reshape(FIELDS, 8, 256, 128)
     out = call(
         atmosphere_kernel,
@@ -437,7 +443,8 @@
         [
             pltpu.VMEM((NPAIR * 8, NLAT), F32),
             pltpu.VMEM((ITEMS * 8, NLAT), F32),
-            pltpu.VMEM((128, NLAT), F32),
+            pltpu.VMEM((LO, 128, 256), F32),
+            pltpu.VMEM((2, 128, NLAT), BF),
             pltpu.VMEM((NLAT // 128, STEPS * 8, 128), F32),
             pltpu.VMEM((NLAT, BANDS * SLOTS), BF),
         ],

time: 139 us -> 134 us (0.964)
  waiting for transfers between devices: 40.1 us -> 35.3 us
  Pallas kernels: 57.3 us -> 54.4 us
  starting transfers between devices: 26.4 us -> 29 us
    all_to_all x1, waiting for transfers between devices: 21.1 us -> 0.01 us  [per_device(): back = lax.all_to_all(out, AXES, 0, 0, tiled=True)]
    ppermute x3, waiting for transfers between devices: 0.01 us -> 18.9 us  [per_device(): lax.ppermute(sent, 'lev', [(i, (i + d) % FIELDS) for i in range(FIELDS)])]
    pallas_call x1, Pallas kernels: 25.6 us -> 22.7 us  [per_device(): call(atmosphere_kernel, vmem(5), shape((WAVES, OUT_ROWS, 128), BF), [pltp...]
    all_to_all x1, waiting for transfers between devices: 19 us -> 16.4 us  [per_device(): got = lax.all_to_all(chunks, AXES, 0, 0, tiled=True)]
    all_to_all x1, starting transfers between devices: 7.7 us -> 10.2 us  [per_device(): got = lax.all_to_all(chunks, AXES, 0, 0, tiled=True)]
  transfers between devices with their start and end apart: 7 -> 7, of which waited for: 2 -> 3; matrix products, arithmetic and copies ran while one was open for 4% -> 4% of each run, Pallas kernels for 8% -> 12%
where the time goes in v3:
time: 134 us; the launch traced here: 131 us
  Pallas kernels  54.4 us (41%)
  waiting for transfers between devices  35.3 us (26%)
  starting transfers between devices  29 us (22%)
  other arithmetic  6.03 us (4%)
  local copies, waits for them, and re-layouts  3.94 us (3%)
  between operations  1.49 us (1%)
    pallas_call x1, Pallas kernels, per_device(): call(atmosphere_kernel, vmem(5), shape((WAVES, OUT_ROWS, 128), BF), [pltp...  22.7 us
    ppermute x3, waiting for transfers between devices, per_device(): lax.ppermute(sent, 'lev', [(i, (i + d) % FIELDS) for i in range(FIELDS)])  18.9 us
    all_to_all x1, waiting for transfers between devices, per_device(): got = lax.all_to_all(chunks, AXES, 0, 0, tiled=True)  16.4 us
    pallas_call x1, Pallas kernels, per_device(): call(ocean_kernel, smem(1) + vmem(6), (shape((SLOTS, lon), F32), shape((S...  11.4 us
    all_to_all x1, starting transfers between devices, per_device(): got = lax.all_to_all(chunks, AXES, 0, 0, tiled=True)  10.2 us
    pallas_call x1, Pallas kernels, per_device(): call(operator_kernel, smem(2) + [pl.BlockSpec(memory_space=pl.ANY)], shap...  8.74 us
    ppermute x3, starting transfers between devices, per_device(): lax.ppermute(sent, 'lev', [(i, (i + d) % FIELDS) for i in range(FIELDS)])  5.8 us
    ppermute x1, starting transfers between devices, per_device(): after = lax.ppermute(ocean_coef, 'band', down)  5.75 us
  transfers between devices with their start and end apart: 7, of which 3 were waited for; matrix products, arithmetic and copies ran while one was open for 4% of the time, Pallas kernels for 12%

profile of v3, /device:TPU:32, one launch (start us, length us, event | category | flops | bytes accessed | tf_op | source)
XLA Modules:
  0.0 131.2 jit_solution(7880855201244261525)
XLA Ops:
  1.3 0.7 pad_add_fusion.ids
  1.9 4.3 %shard_map.175 = bf16[128,64,128]{2,1,0:T(8,128)(2,1)} custom-call(s32[2]{0:T(128)} %pad_add_fusion.ids, s32[1]{0:T(128)S(6)} %copy.28.live_ref, f32[640,256]{1,0:T(8,128)} %bitcast.46, f32[480,256]{1,0:T(8,128)} %bitcast.48, f32[256,40]{1,0:T(8,128)} %bitcast.49, f32[1,40]{1,0:T(1,128)} %bitcast.50, f32[1,40]{1,0:T(1,128)} %k_ref.1, s32[1,32]{1,0:T(1,128)} %bitcast.51, ...), custom_call_target="tpu_custom_call" | custom-call | tf_op jit(solution)/shard_map/pallas_call | solution.py:371
  6.2 10.2 %all-to-all-start = ((bf16[128,64,128]{2,1,0:T(8,128)(2,1)}), bf16[128,64,128]{2,1,0:T(8,128)(2,1)S(1)}, u32[]{:S(2)}, u32[]{:S(2)}) async-start(bf16[128,64,128]{2,1,0:T(8,128)(2,1)} %shard_map.175), calls=%async_computation | async-start | bytes 4194304 | tf_op jit(solution)/shard_map/all_to_all | solution.py:388
  16.4 8.7 %shard_map.176.p_ref = bf16[1280,1280]{1,0:T(8,128)(2,1)} custom-call(s32[2]{0:T(128)} %pad_add_fusion.ids, s32[128]{0:T(128)} %wave_ref.1, bf16[4,32,5,8,1280]{4,3,2,1,0:T(8,128)(2,1)} %bitcast.39), custom_call_target="tpu_custom_call" | custom-call | tf_op jit(solution)/shard_map/pallas_call | solution.py:390
  25.3 0.4 broadcast_and_fusion.1
  25.7 0.9 add_convert_fusion.sx_ref
  26.6 1.4 %and_convert_fusion.sm_ref = bf16[960,512]{1,0:T(8,128)(2,1)} fusion(s32[512]{0:T(512)S(1)} %get-tuple-element.29, s32[512]{0:T(512)S(1)} %get-tuple-element.30, s32[960]{0:T(1024)S(1)} %get-tuple-element.27, s32[960]{0:T(1024)S(1)} %get-tuple-element.28), kind=kLoop, calls=%fused_computation.3 | loop fusion | flops 1966080 | bytes 994816 | tf_op jit(solution)/shard_map/convert_element_type | solution.py:403
  27.9 1.5 %fusion.se_ref = bf16[640,1024]{1,0:T(8,128)(2,1)} fusion(s32[1024]{0:T(1024)S(1)} %fusion.48), kind=kLoop, calls=%fused_computation.1 | loop fusion | flops 1310720 | bytes 1314816 | tf_op jit(solution)/shard_map/convert_element_type | solution.py:413
  29.5 16.4 %all-to-all-done = bf16[128,64,128]{2,1,0:T(8,128)(2,1)S(1)} async-done(((bf16[128,64,128]{2,1,0:T(8,128)(2,1)}), bf16[128,64,128]{2,1,0:T(8,128)(2,1)S(1)}, u32[]{:S(2)}, u32[]{:S(2)}) %all-to-all-start) | async-done | bytes 2097184 | tf_op jit(solution)/shard_map/all_to_all | solution.py:388
  45.9 1.9 %copy.27 = bf16[32,4,8,8,128]{4,3,0,2,1:T(8,128)(2,1)} copy(bf16[32,4,8,8,128]{4,3,2,1,0:T(8,128)(2,1)S(1)} %bitcast.40) | data formatting | bytes 4194304 | tf_op jit(solution)/shard_map/reshape | solution.py:438
  47.8 22.7 %shard_map.177 = bf16[128,40,128]{2,1,0:T(8,128)(2,1)} custom-call(bf16[4,8,256,128]{3,2,1,0:T(8,128)(2,1)} %bitcast.41, bf16[960,512]{1,0:T(8,128)(2,1)} %and_convert_fusion.sm_ref, bf16[2,256,512]{2,1,0:T(8,128)(2,1)} %add_convert_fusion.sx_ref, bf16[640,1024]{1,0:T(8,128)(2,1)} %fusion.se_ref, bf16[1280,1280]{1,0:T(8,128)(2,1)} %shard_map.176.p_ref), custom_call_target="tpu_custom_call" | custom-call | tf_op jit(solution)/shard_map/pallas_call | solution.py:439
  70.5 0.0 copy-start.1
  70.5 0.0 copy-start.2
  70.5 0.0 copy-start.6
  70.5 0.0 copy-start.7
  70.5 5.2 %all-to-all-start.1 = ((bf16[128,40,128]{2,1,0:T(8,128)(2,1)}), bf16[128,40,128]{2,1,0:T(8,128)(2,1)S(1)}, u32[]{:S(2)}, u32[]{:S(2)}) async-start(bf16[128,40,128]{2,1,0:T(8,128)(2,1)} %shard_map.177), calls=%async_computation.1 | async-start | bytes 2621440 | tf_op jit(solution)/shard_map/all_to_all | solution.py:453
  75.7 0.0 copy-done.1
  75.7 0.0 copy-done.2
  75.8 1.6 %collective-permute-start = (bf16[64,1440]{1,0:T(8,128)(2,1)S(1)}, bf16[64,1440]{1,0:T(8,128)(2,1)S(1)}, u32[]{:S(2)}, u32[]{:S(2)}) collective-permute-start(bf16[64,1440]{1,0:T(8,128)(2,1)S(1)} %pad_maximum_fusion), channel_id=1, source_target_pairs={{0,1},{1,2},{2,3},{3,0},{4,5},{5,6},{6,7},{7,4},{8,9},{9,10},{10,1... | collective-permute-start | bytes 552968 | tf_op jit(solution)/shard_map/ppermute | solution.py:424
  77.4 2.8 %collective-permute-start.1 = (bf16[64,1440]{1,0:T(8,128)(2,1)S(1)}, bf16[64,1440]{1,0:T(8,128)(2,1)S(1)}, u32[]{:S(2)}, u32[]{:S(2)}) collective-permute-start(bf16[64,1440]{1,0:T(8,128)(2,1)S(1)} %pad_maximum_fusion), channel_id=1, source_target_pairs={{0,2},{1,3},{2,0},{3,1},{4,6},{5,7},{6,4},{7,5},{8,10},{9,11},{10,... | collective-permute-start | bytes 552968 | tf_op jit(solution)/shard_map/ppermute | solution.py:424
  80.2 1.4 %collective-permute-start.2 = (bf16[64,1440]{1,0:T(8,128)(2,1)S(1)}, bf16[64,1440]{1,0:T(8,128)(2,1)S(1)}, u32[]{:S(2)}, u32[]{:S(2)}) collective-permute-start(bf16[64,1440]{1,0:T(8,128)(2,1)S(1)} %pad_maximum_fusion), channel_id=1, source_target_pairs={{0,3},{1,0},{2,1},{3,2},{4,7},{5,4},{6,5},{7,6},{8,11},{9,8},{10,9... | collective-permute-start | bytes 552968 | tf_op jit(solution)/shard_map/ppermute | solution.py:424
  81.6 0.0 copy-done.6
  81.6 1.1 sine_select_fusion.a_ref
  82.7 0.0 copy-done.7
  82.7 14.8 %collective-permute-done.o1 = bf16[64,1440]{1,0:T(8,128)(2,1)S(1)} collective-permute-done((bf16[64,1440]{1,0:T(8,128)(2,1)S(1)}, bf16[64,1440]{1,0:T(8,128)(2,1)S(1)}, u32[]{:S(2)}, u32[]{:S(2)}) %collective-permute-start) | collective-permute-done | bytes 184352 | tf_op jit(solution)/shard_map/ppermute | solution.py:424
  97.5 0.0 copy-start.3
  97.5 4.1 %collective-permute-done.1.o2 = bf16[64,1440]{1,0:T(8,128)(2,1)S(1)} collective-permute-done((bf16[64,1440]{1,0:T(8,128)(2,1)S(1)}, bf16[64,1440]{1,0:T(8,128)(2,1)S(1)}, u32[]{:S(2)}, u32[]{:S(2)}) %collective-permute-start.1) | collective-permute-done | bytes 184352 | tf_op jit(solution)/shard_map/ppermute | solution.py:424
  101.6 0.0 copy-start.4
  101.6 0.0 collective-permute-done.2.o3
  101.6 0.0 copy-start.5
  101.6 0.0 copy-done.3
  101.6 0.7 copy-done.4
  102.3 0.1 copy-done.5
  102.3 3.7 %shard_map.179 = (bf16[1440,256]{1,0:T(8,128)(2,1)}, bf16[256,1440]{1,0:T(8,128)(2,1)}, f32[1440,128]{1,0:T(8,128)}, f32[1440,128]{1,0:T(8,128)}, bf16[256,128]{1,0:T(8,128)(2,1)}) custom-call(s32[2]{0:T(128)} %pad_add_fusion.ids, f32[4,4]{1,0:T(4,128)} %c_ref.1, f32[160,128]{1,0:T(8,128)} %sine_select_fusion.a_ref, f32[32,1440]{1,0:T(8,128)} %bitcast.44, ...), custom_call_target="tpu_custom_call" | custom-call | tf_op jit(solution)/shard_map/pallas_call | solution.py:425
  106.0 0.0 all-to-all-done.1.b_ref
  106.0 0.1 slice.12
  106.1 0.2 copy.23
  106.3 1.0 copy.24
  107.3 0.0 copy-done
  107.3 11.4 %shard_map.180 = (f32[32,1440]{1,0:T(8,128)}, bf16[384,256]{1,0:T(8,128)(2,1)}) custom-call(s32[2]{0:T(128)} %pad_add_fusion.ids, bf16[12,256,128]{2,1,0:T(8,128)(2,1)} %bitcast.43, bf16[1440,256]{1,0:T(8,128)(2,1)} %get-tuple-element.10.zt_ref, bf16[256,1440]{1,0:T(8,128)(2,1)} %get-tuple-element.11.z_ref, bf16[256,128]{1,0:T(8,128)(2,1)} %get-tuple-element.12.c_ref, ...), custom_call_target="tpu_custom_call" | custom-call | tf_op jit(solution)/shard_map/pallas_call | solution.py:455
  118.7 2.0 %collective-permute-start.3 = (bf16[12,32,256]{2,1,0:T(8,128)(2,1)}, bf16[12,32,256]{2,1,0:T(8,128)(2,1)S(1)}, u32[]{:S(2)}, u32[]{:S(2)}) collective-permute-start(bf16[12,32,256]{2,1,0:T(8,128)(2,1)} %bitcast.54), channel_id=1, source_target_pairs={{0,4},{4,8},{8,12},{12,16},{16,20},{20,24},{24,28},{28,32},{32,36}... | collective-permute-start | bytes 589832 | tf_op jit(solution)/shard_map/ppermute | solution.py:477
  120.8 5.8 %collective-permute-start.4 = (bf16[12,32,256]{2,1,0:T(8,128)(2,1)}, bf16[12,32,256]{2,1,0:T(8,128)(2,1)S(1)}, u32[]{:S(2)}, u32[]{:S(2)}) collective-permute-start(bf16[12,32,256]{2,1,0:T(8,128)(2,1)} %bitcast.55), channel_id=1, source_target_pairs={{4,0},{8,4},{12,8},{16,12},{20,16},{24,20},{28,24},{32,28},{36,32}... | collective-permute-start | bytes 589832 | tf_op jit(solution)/shard_map/ppermute | solution.py:478
  126.5 0.0 copy-done.9
  126.6 3.6 %shard_map.178 = f32[640,256]{1,0:T(8,128)} custom-call(bf16[128,40,128]{2,1,0:T(8,128)(2,1)} %copy-done), custom_call_target="tpu_custom_call" | custom-call | tf_op jit(solution)/shard_map/pallas_call | solution.py:468
  130.2 0.0 collective-permute-done.3
  130.2 0.0 collective-permute-done.4
  130.2 0.0 copy-done.8
  130.2 1.1 convolution_bitcast_fusion
  (17 shorter events, 0.1 us)
Async XLA Ops:
  6.2 39.7 %all-to-all-start = ((bf16[128,64,128]{2,1,0:T(8,128)(2,1)}), bf16[128,64,128]{2,1,0:T(8,128)(2,1)S(1)}, u32[]{:S(2)}, u32[]{:S(2)}) async-start(bf16[128,64,128]{2,1,0:T(8,128)(2,1)} %shard_map.175), calls=%async_computation | async-start | bytes 4194304 | tf_op jit(solution)/shard_map/all_to_all | solution.py:388
  70.5 5.2 %copy-start.1 = (f32[1,32,1440]{2,1,0:T(8,128)S(1)}, f32[1,32,1440]{2,1,0:T(8,128)}, u32[]{:S(2)}) copy-start(f32[1,32,1440]{2,1,0:T(8,128)} %param.23) | copy-start | bytes 552964
  70.5 5.2 %copy-start.2 = (f32[1,32,1440]{2,1,0:T(8,128)S(1)}, f32[1,32,1440]{2,1,0:T(8,128)}, u32[]{:S(2)}) copy-start(f32[1,32,1440]{2,1,0:T(8,128)} %param.24) | copy-start | bytes 552964
  70.5 11.1 %copy-start.6 = (s32[128]{0:T(128)S(1)}, s32[128]{0:T(128)}, u32[]{:S(2)}) copy-start(s32[128]{0:T(128)} %wave_ref.1) | copy-start | bytes 1540
  70.5 12.2 %copy-start.7 = (s32[2,40]{1,0:T(2,128)S(1)}, s32[2,40]{1,0:T(2,128)}, u32[]{:S(2)}) copy-start(s32[2,40]{1,0:T(2,128)} %param.29) | copy-start | bytes 964
  70.5 35.6 %all-to-all-start.1 = ((bf16[128,40,128]{2,1,0:T(8,128)(2,1)}), bf16[128,40,128]{2,1,0:T(8,128)(2,1)S(1)}, u32[]{:S(2)}, u32[]{:S(2)}) async-start(bf16[128,40,128]{2,1,0:T(8,128)(2,1)} %shard_map.177), calls=%async_computation.1 | async-start | bytes 2621440 | tf_op jit(solution)/shard_map/all_to_all | solution.py:453
  75.8 21.7 %collective-permute-start = (bf16[64,1440]{1,0:T(8,128)(2,1)S(1)}, bf16[64,1440]{1,0:T(8,128)(2,1)S(1)}, u32[]{:S(2)}, u32[]{:S(2)}) collective-permute-start(bf16[64,1440]{1,0:T(8,128)(2,1)S(1)} %pad_maximum_fusion), channel_id=1, source_target_pairs={{0,1},{1,2},{2,3},{3,0},{4,5},{5,6},{6,7},{7,4},{8,9},{9,10},{10,1... | collective-permute-start | bytes 552968 | tf_op jit(solution)/shard_map/ppermute | solution.py:424
  77.4 24.2 %collective-permute-start.1 = (bf16[64,1440]{1,0:T(8,128)(2,1)S(1)}, bf16[64,1440]{1,0:T(8,128)(2,1)S(1)}, u32[]{:S(2)}, u32[]{:S(2)}) collective-permute-start(bf16[64,1440]{1,0:T(8,128)(2,1)S(1)} %pad_maximum_fusion), channel_id=1, source_target_pairs={{0,2},{1,3},{2,0},{3,1},{4,6},{5,7},{6,4},{7,5},{8,10},{9,11},{10,... | collective-permute-start | bytes 552968 | tf_op jit(solution)/shard_map/ppermute | solution.py:424
  80.2 21.4 %collective-permute-start.2 = (bf16[64,1440]{1,0:T(8,128)(2,1)S(1)}, bf16[64,1440]{1,0:T(8,128)(2,1)S(1)}, u32[]{:S(2)}, u32[]{:S(2)}) collective-permute-start(bf16[64,1440]{1,0:T(8,128)(2,1)S(1)} %pad_maximum_fusion), channel_id=1, source_target_pairs={{0,3},{1,0},{2,1},{3,2},{4,7},{5,4},{6,5},{7,6},{8,11},{9,8},{10,9... | collective-permute-start | bytes 552968 | tf_op jit(solution)/shard_map/ppermute | solution.py:424
  97.5 4.1 %copy-start.3 = (bf16[64,1440]{1,0:T(8,128)(2,1)}, bf16[64,1440]{1,0:T(8,128)(2,1)S(1)}, u32[]{:S(2)}) copy-start(bf16[64,1440]{1,0:T(8,128)(2,1)S(1)} %collective-permute-done.o1) | copy-start | bytes 552964
  101.6 0.7 copy-start.4
  101.6 0.7 copy-start.5
  106.0 1.3 copy-start
  107.3 19.2 %copy-start.9 = (f32[40]{0:T(128)S(1)}, f32[40]{0:T(128)}, u32[]{:S(2)}) copy-start(f32[40]{0:T(128)} %param.30) | copy-start | bytes 484
  118.7 11.4 %copy-start.8 = (bf16[384,256]{1,0:T(8,128)(2,1)S(1)}, bf16[384,256]{1,0:T(8,128)(2,1)}, u32[]{:S(2)}) copy-start(bf16[384,256]{1,0:T(8,128)(2,1)} %get-tuple-element.16) | copy-start | bytes 589828
  118.7 11.4 %collective-permute-start.3 = (bf16[12,32,256]{2,1,0:T(8,128)(2,1)}, bf16[12,32,256]{2,1,0:T(8,128)(2,1)S(1)}, u32[]{:S(2)}, u32[]{:S(2)}) collective-permute-start(bf16[12,32,256]{2,1,0:T(8,128)(2,1)} %bitcast.54), channel_id=1, source_target_pairs={{0,4},{4,8},{8,12},{12,16},{16,20},{20,24},{24,28},{28,32},{32,36}... | collective-permute-start | bytes 589832 | tf_op jit(solution)/shard_map/ppermute | solution.py:477
  120.8 9.4 %collective-permute-start.4 = (bf16[12,32,256]{2,1,0:T(8,128)(2,1)}, bf16[12,32,256]{2,1,0:T(8,128)(2,1)S(1)}, u32[]{:S(2)}, u32[]{:S(2)}) collective-permute-start(bf16[12,32,256]{2,1,0:T(8,128)(2,1)} %bitcast.55), channel_id=1, source_target_pairs={{4,0},{8,4},{12,8},{16,12},{20,16},{24,20},{28,24},{32,28},{36,32}... | collective-permute-start | bytes 589832 | tf_op jit(solution)/shard_map/ppermute | solution.py:478

commit v4 on v3

--- a/solution.py
+++ b/solution.py
@@ -28,7 +28,7 @@
 NPAIR = len(PAIRS)
 XROWS = 24
 OUT_ROWS = 40
-CHUNK = XROWS + LAT
+CHUNK = XROWS + 16
 BF = jnp.bfloat16
 F32 = jnp.float32
 NT = (((1,), (1,)), ((), ()))
@@ -103,7 +103,7 @@
         d_ref[c, 31 * LAT : 32 * LAT, :] = jnp.zeros((LAT, WAVES), F32)
     m_hi, m_lo = hi_lo(b_ref[...].T)
     mix = jnp.dot(m_hi, q_ref[...], preferred_element_type=F32)
-    mix = (mix + jnp.dot(m_lo, q_ref[...], preferred_element_type=F32)).astype(BF)
+    mix = mix + jnp.dot(m_lo, q_ref[...], preferred_element_type=F32)
     for j in range(XROWS // 8):
         for h in range(8):
             parts = []
@@ -116,12 +116,20 @@
                         parts.append(jnp.zeros((ITEMS, WAVES), F32))
             t_ref[pl.ds(j * 8 + h, WAVES, stride=XROWS), :] = jnp.concatenate(parts, axis=0).T
 
-    def put(m, _):
-        o_ref[m, 0:XROWS, :] = t_ref[pl.ds(pl.multiple_of(m * XROWS, 8), XROWS), :].astype(BF)
-        o_ref[m, XROWS:CHUNK, :] = mix
-        return 0
-
-    lax.fori_loop(0, WAVES, put, 0)
+    upper = lax.broadcasted_iota(jnp.int32, (8, 128), 1) >= 64
+    for core in range(2):
+        half = mix[32:40] if core else pltpu.roll(mix[32:40], 64, 1)
+        spare = jnp.concatenate([jnp.zeros((16, 128), F32), jnp.where(upper, half, 0.0)], axis=0)
+        whole = mix[16 * core : 16 * core + 16].astype(BF)
+
+        def put(j, _):
+            m = j // FIELDS * (2 * FIELDS) + core * FIELDS + j % FIELDS
+            rows = t_ref[pl.ds(pl.multiple_of(m * XROWS, 8), XROWS), :]
+            o_ref[m, 0:XROWS, :] = (rows + spare).astype(BF)
+            o_ref[m, XROWS:CHUNK, :] = whole
+            return 0
+
+        lax.fori_loop(0, WAVES // 2, put, 0)
 
 
 def operator_kernel(ids, wave_ref, table_ref, p_ref, t_ref, d_ref, sem):
@@ -189,14 +197,40 @@
 
 
 def atmosphere_kernel(
-    g_ref, sm_ref, sx_ref, se_ref, p_ref, o_ref, a_ref, x_ref, y_ref, s_ref, f_ref, t_ref
+    ids, g_ref, h_ref, sm_ref, sx_ref, se_ref, p_ref, o_ref, a_ref, x_ref, y_ref, s_ref, f_ref, t_ref
 ):
+    first = ids[0] % 2 == 0
     for lo in range(LO):
         lanes = slice(lo * 256, (lo + 1) * 256)
-        mix = jnp.concatenate([g_ref[f, 3 + lo] for f in range(FIELDS)], axis=1)
+        rows = jnp.concatenate([g_ref[lo // 2, f] for f in range(FIELDS)], axis=1)
+        x_ref[:, lanes] = lax.dot_general(sx_ref[lo % 2], rows, NT, preferred_element_type=F32)
+
+    nslot = BANDS * SLOTS
+    slot = lax.broadcasted_iota(jnp.int32, (1, nslot), 1)
+    south = x_ref[240:241, 0:nslot] + (slot % 256 // 8 * LAT - MARG).astype(F32)
+    low = x_ref[242:243, 0:nslot]
+    high = x_ref[244:245, 0:nslot]
+    for lo in range(LO):
+        r = lax.broadcasted_iota(jnp.int32, (256, 1), 0)
+        place = (r // 8 * LAT + lo * 8 + r % 8).astype(F32)
+        t_ref[lo * 256 : (lo + 1) * 256, :] = jnp.where(
+            place == south, low, jnp.where(place == south + 1.0, high, 0.0)
+        ).astype(BF)
+
+    for lo in range(LO):
+        lanes = slice(lo * 256, (lo + 1) * 256)
+        parts = []
+        for f in range(FIELDS):
+            if lo < 4:
+                own, other = g_ref[3 + lo % 2, f], h_ref[1 + lo % 2, f]
+                parts.append(jnp.where(first == (lo < 2), own, other))
+            else:
+                own, other = g_ref[2, f].astype(F32), h_ref[0, f].astype(F32)
+                lower = lax.broadcasted_iota(jnp.int32, own.shape, 1) < 64
+                even = pltpu.roll(jnp.where(first, own, other), 64, 1)
+                parts.append(jnp.where(lower, even, jnp.where(first, other, own)).astype(BF))
+        mix = jnp.concatenate(parts, axis=1)
         a_ref[:, lanes] = lax.dot_general(sm_ref[...], mix, NT, preferred_element_type=F32)
-        rows = jnp.concatenate([g_ref[f, lo // 2] for f in range(FIELDS)], axis=1)
-        x_ref[:, lanes] = lax.dot_general(sx_ref[lo % 2], rows, NT, preferred_element_type=F32)
 
     weight = x_ref[28 * 8 : 29 * 8, :]
     for l in range(0, LEVELS, 2):
@@ -238,17 +272,6 @@
 
     lax.fori_loop(0, STEPS, step, 0)
 
-    nslot = BANDS * SLOTS
-    slot = lax.broadcasted_iota(jnp.int32, (1, nslot), 1)
-    south = x_ref[240:241, 0:nslot] + (slot % 256 // 8 * LAT - MARG).astype(F32)
-    low = x_ref[242:243, 0:nslot]
-    high = x_ref[244:245, 0:nslot]
-    for lo in range(LO):
-        r = lax.broadcasted_iota(jnp.int32, (256, 1), 0)
-        place = (r // 8 * LAT + lo * 8 + r % 8).astype(F32)
-        t_ref[lo * 256 : (lo + 1) * 256, :] = jnp.where(
-            place == south, low, jnp.where(place == south + 1.0, high, 0.0)
-        ).astype(BF)
     flux = jnp.concatenate([f_ref[n].astype(BF) for n in range(NLAT // 128)], axis=1)
     at_slots = jnp.dot(flux, t_ref[...], preferred_element_type=F32) * (-ocean_step / math.sqrt(COLS))
     ends = jnp.concatenate(
@@ -435,10 +458,11 @@
         [pltpu.VMEM((lon, COLS), F32), pltpu.VMEM((2, 128, lon), F32)],
     )(ids, sea_coupling_matrix, angle_parts, own_sea, own_damp, *others)
 
-    got = got.reshape(BANDS, FIELDS, 8, 8, 128).transpose(1, 2, 0, 3, 4).reshape(FIELDS, 8, 256, 128)
+    got = got.reshape(BANDS, FIELDS, 5, 8, 128).transpose(2, 1, 0, 3, 4).reshape(5, FIELDS, 256, 128)
+    partner = lax.ppermute(got[2:], "band", [(i, i ^ 1) for i in range(BANDS)])
     out = call(
         atmosphere_kernel,
-        vmem(5),
+        smem(1) + vmem(6),
         shape((WAVES, OUT_ROWS, 128), BF),
         [
             pltpu.VMEM((NPAIR * 8, NLAT), F32),
@@ -448,7 +472,7 @@
             pltpu.VMEM((NLAT // 128, STEPS * 8, 128), F32),
             pltpu.VMEM((NLAT, BANDS * SLOTS), BF),
         ],
-    )(got, select_mix, select_x, select_end, operator)
+    )(ids, got, partner, select_mix, select_x, select_end, operator)
 
     back = lax.all_to_all(out, AXES, 0, 0, tiled=True)
     flux_in = back[:, :24].reshape(WAVES, 2, STEPS, 128).transpose(2, 1, 0, 3).reshape(STEPS, COLS, 128)

time: 134 us -> 139 us (1.037)
  waiting for transfers between devices: 35.3 us -> 38.9 us
    all_to_all x1, waiting for transfers between devices: 16.4 us -> 20 us  [per_device(): got = lax.all_to_all(chunks, AXES, 0, 0, tiled=True)]
    unnamed x20 -> x26, local copies, waits for them, and re-layouts: 0.76 us -> 2.55 us
    reshape x1, local copies, waits for them, and re-layouts: 1.9 us -> 0.34 us  [per_device(): got.reshape(BANDS, FIELDS, 5, 8, 128).transpose(2, 1, 0, 3, 4)]
  transfers between devices with their start and end apart: 7 -> 8, of which waited for: 3 -> 3; matrix products, arithmetic and copies ran while one was open for 4% -> 4% of each run, Pallas kernels for 12% -> 12%
where the time goes in v4:
time: 139 us; the launch traced here: 137 us
  Pallas kernels  55.4 us (40%)
  waiting for transfers between devices  38.9 us (28%)
  starting transfers between devices  29.3 us (21%)
  other arithmetic  6.59 us (5%)
  local copies, waits for them, and re-layouts  4.14 us (3%)
  between operations  1.53 us (1%)
    pallas_call x1, Pallas kernels, per_device(): call(atmosphere_kernel, smem(1) + vmem(6), shape((WAVES, OUT_ROWS, 128),...  23.1 us
    all_to_all x1, waiting for transfers between devices, per_device(): got = lax.all_to_all(chunks, AXES, 0, 0, tiled=True)  20 us
    ppermute x3, waiting for transfers between devices, per_device(): lax.ppermute(sent, 'lev', [(i, (i + d) % FIELDS) for i in range(FIELDS)])  18.9 us
    pallas_call x1, Pallas kernels, per_device(): call(ocean_kernel, smem(1) + vmem(6), (shape((SLOTS, lon), F32), shape((S...  11.4 us
    all_to_all x1, starting transfers between devices, per_device(): got = lax.all_to_all(chunks, AXES, 0, 0, tiled=True)  10.2 us
    pallas_call x1, Pallas kernels, per_device(): call(operator_kernel, smem(2) + [pl.BlockSpec(memory_space=pl.ANY)], shap...  8.87 us
    ppermute x3, starting transfers between devices, per_device(): lax.ppermute(sent, 'lev', [(i, (i + d) % FIELDS) for i in range(FIELDS)])  5.8 us
    ppermute x1, starting transfers between devices, per_device(): after = lax.ppermute(ocean_coef, 'band', down)  5.75 us
  transfers between devices with their start and end apart: 8, of which 3 were waited for; matrix products, arithmetic and copies ran while one was open for 4% of the time, Pallas kernels for 12%

profile of v4, /device:TPU:32, one launch (start us, length us, event | category | flops | bytes accessed | tf_op | source)
XLA Modules:
  0.0 137.0 jit_solution(8931181634999476947)
XLA Ops:
  1.3 0.6 pad_add_fusion.ids
  1.9 4.7 %shard_map.175 = bf16[128,40,128]{2,1,0:T(8,128)(2,1)} custom-call(s32[2]{0:T(128)} %pad_add_fusion.ids, s32[1]{0:T(128)S(6)} %copy.29.live_ref, f32[640,256]{1,0:T(8,128)} %bitcast.50, f32[480,256]{1,0:T(8,128)} %bitcast.52, f32[256,40]{1,0:T(8,128)} %bitcast.53, f32[1,40]{1,0:T(1,128)} %bitcast.54, f32[1,40]{1,0:T(1,128)} %k_ref.1, s32[1,32]{1,0:T(1,128)} %bitcast.55, ...), custom_call_target="tpu_custom_call" | custom-call | tf_op jit(solution)/shard_map/pallas_call | solution.py:394
  6.6 10.2 %all-to-all-start = ((bf16[128,40,128]{2,1,0:T(8,128)(2,1)}), bf16[128,40,128]{2,1,0:T(8,128)(2,1)S(1)}, u32[]{:S(2)}, u32[]{:S(2)}) async-start(bf16[128,40,128]{2,1,0:T(8,128)(2,1)} %shard_map.175), calls=%async_computation | async-start | bytes 2621440 | tf_op jit(solution)/shard_map/all_to_all | solution.py:411
  16.9 1.1 broadcast_and_fusion.1
  18.0 20.0 %all-to-all-done = bf16[128,40,128]{2,1,0:T(8,128)(2,1)S(1)} async-done(((bf16[128,40,128]{2,1,0:T(8,128)(2,1)}), bf16[128,40,128]{2,1,0:T(8,128)(2,1)S(1)}, u32[]{:S(2)}, u32[]{:S(2)}) %all-to-all-start) | async-done | bytes 1310752 | tf_op jit(solution)/shard_map/all_to_all | solution.py:411
  38.0 0.3 copy.28
  38.3 0.0 copy-start.1
  38.3 0.1 slice_bitcast_fusion
  38.4 0.4 collective-permute-start
  38.8 0.0 copy-start.5
  38.8 8.9 %shard_map.176.p_ref = bf16[1280,1280]{1,0:T(8,128)(2,1)} custom-call(s32[2]{0:T(128)} %pad_add_fusion.ids, s32[128]{0:T(128)} %wave_ref.1, bf16[4,32,5,8,1280]{4,3,2,1,0:T(8,128)(2,1)} %bitcast.42), custom_call_target="tpu_custom_call" | custom-call | tf_op jit(solution)/shard_map/pallas_call | solution.py:413
  47.7 0.0 copy-done.1
  47.7 0.0 copy-done.5
  47.7 0.9 add_convert_fusion.sx_ref
  48.6 1.4 %and_convert_fusion.sm_ref = bf16[960,512]{1,0:T(8,128)(2,1)} fusion(s32[512]{0:T(512)S(1)} %get-tuple-element.31, s32[512]{0:T(512)S(1)} %get-tuple-element.32, s32[960]{0:T(1024)S(1)} %get-tuple-element.29, s32[960]{0:T(1024)S(1)} %get-tuple-element.30), kind=kLoop, calls=%fused_computation.2 | loop fusion | flops 1966080 | bytes 994816 | tf_op jit(solution)/shard_map/convert_element_type | solution.py:426
  50.0 1.5 %fusion.se_ref = bf16[640,1024]{1,0:T(8,128)(2,1)} fusion(s32[1024]{0:T(1024)S(1)} %fusion.48), kind=kLoop, calls=%fused_computation.1 | loop fusion | flops 1310720 | bytes 1314816 | tf_op jit(solution)/shard_map/convert_element_type | solution.py:436
  51.4 0.0 collective-permute-done.h_ref
  51.5 1.0 copy-done.2
  52.4 23.1 %shard_map.177 = bf16[128,40,128]{2,1,0:T(8,128)(2,1)} custom-call(s32[2]{0:T(128)} %pad_add_fusion.ids, bf16[5,4,256,128]{3,2,1,0:T(8,128)(2,1)} %bitcast.44, bf16[3,4,256,128]{3,2,1,0:T(8,128)(2,1)} %copy-done.2, bf16[960,512]{1,0:T(8,128)(2,1)} %and_convert_fusion.sm_ref, bf16[2,256,512]{2,1,0:T(8,128)(2,1)} %add_convert_fusion.sx_ref, ...), custom_call_target="tpu_custom_call" | custom-call | tf_op jit(solution)/shard_map/pallas_call | solution.py:463
  75.6 0.0 copy-start.10
  75.6 5.1 %all-to-all-start.1 = ((bf16[128,40,128]{2,1,0:T(8,128)(2,1)}), bf16[128,40,128]{2,1,0:T(8,128)(2,1)S(1)}, u32[]{:S(2)}, u32[]{:S(2)}) async-start(bf16[128,40,128]{2,1,0:T(8,128)(2,1)} %shard_map.177), calls=%async_computation.1 | async-start | bytes 2621440 | tf_op jit(solution)/shard_map/all_to_all | solution.py:477
  80.7 0.0 copy-done.3
  80.7 0.0 copy-done.4
  80.8 1.6 %collective-permute-start.1 = (bf16[64,1440]{1,0:T(8,128)(2,1)S(1)}, bf16[64,1440]{1,0:T(8,128)(2,1)S(1)}, u32[]{:S(2)}, u32[]{:S(2)}) collective-permute-start(bf16[64,1440]{1,0:T(8,128)(2,1)S(1)} %pad_maximum_fusion), channel_id=1, source_target_pairs={{0,1},{1,2},{2,3},{3,0},{4,5},{5,6},{6,7},{7,4},{8,9},{9,10},{10,1... | collective-permute-start | bytes 552968 | tf_op jit(solution)/shard_map/ppermute | solution.py:447
  82.4 2.8 %collective-permute-start.2 = (bf16[64,1440]{1,0:T(8,128)(2,1)S(1)}, bf16[64,1440]{1,0:T(8,128)(2,1)S(1)}, u32[]{:S(2)}, u32[]{:S(2)}) collective-permute-start(bf16[64,1440]{1,0:T(8,128)(2,1)S(1)} %pad_maximum_fusion), channel_id=1, source_target_pairs={{0,2},{1,3},{2,0},{3,1},{4,6},{5,7},{6,4},{7,5},{8,10},{9,11},{10,... | collective-permute-start | bytes 552968 | tf_op jit(solution)/shard_map/ppermute | solution.py:447
  85.2 1.4 %collective-permute-start.3 = (bf16[64,1440]{1,0:T(8,128)(2,1)S(1)}, bf16[64,1440]{1,0:T(8,128)(2,1)S(1)}, u32[]{:S(2)}, u32[]{:S(2)}) collective-permute-start(bf16[64,1440]{1,0:T(8,128)(2,1)S(1)} %pad_maximum_fusion), channel_id=1, source_target_pairs={{0,3},{1,0},{2,1},{3,2},{4,7},{5,4},{6,5},{7,6},{8,11},{9,8},{10,9... | collective-permute-start | bytes 552968 | tf_op jit(solution)/shard_map/ppermute | solution.py:447
  86.6 0.0 copy-done.9
  86.6 1.1 sine_select_fusion.a_ref
  87.7 14.8 %collective-permute-done.1.o1 = bf16[64,1440]{1,0:T(8,128)(2,1)S(1)} collective-permute-done((bf16[64,1440]{1,0:T(8,128)(2,1)S(1)}, bf16[64,1440]{1,0:T(8,128)(2,1)S(1)}, u32[]{:S(2)}, u32[]{:S(2)}) %collective-permute-start.1) | collective-permute-done | bytes 184352 | tf_op jit(solution)/shard_map/ppermute | solution.py:447
  102.5 4.1 %collective-permute-done.2.o2 = bf16[64,1440]{1,0:T(8,128)(2,1)S(1)} collective-permute-done((bf16[64,1440]{1,0:T(8,128)(2,1)S(1)}, bf16[64,1440]{1,0:T(8,128)(2,1)S(1)}, u32[]{:S(2)}, u32[]{:S(2)}) %collective-permute-start.2) | collective-permute-done | bytes 184352 | tf_op jit(solution)/shard_map/ppermute | solution.py:447
  106.6 0.0 collective-permute-done.3.o3
  106.6 0.7 copy-done.7
  107.3 0.1 copy-done.8
  107.3 3.7 %shard_map.179 = (bf16[1440,256]{1,0:T(8,128)(2,1)}, bf16[256,1440]{1,0:T(8,128)(2,1)}, f32[1440,128]{1,0:T(8,128)}, f32[1440,128]{1,0:T(8,128)}, bf16[256,128]{1,0:T(8,128)(2,1)}) custom-call(s32[2]{0:T(128)} %pad_add_fusion.ids, f32[4,4]{1,0:T(4,128)} %c_ref.1, f32[160,128]{1,0:T(8,128)} %sine_select_fusion.a_ref, f32[32,1440]{1,0:T(8,128)} %bitcast.48, ...), custom_call_target="tpu_custom_call" | custom-call | tf_op jit(solution)/shard_map/pallas_call | solution.py:448
  111.0 0.0 all-to-all-done.1.b_ref
  111.1 0.1 slice.21
  111.1 0.2 copy.23
  111.3 0.8 copy-done
  112.1 1.0 copy.24
  113.1 11.4 %shard_map.180 = (f32[32,1440]{1,0:T(8,128)}, bf16[384,256]{1,0:T(8,128)(2,1)}) custom-call(s32[2]{0:T(128)} %pad_add_fusion.ids, bf16[12,256,128]{2,1,0:T(8,128)(2,1)} %bitcast.47, bf16[1440,256]{1,0:T(8,128)(2,1)} %get-tuple-element.10.zt_ref, bf16[256,1440]{1,0:T(8,128)(2,1)} %get-tuple-element.11.z_ref, bf16[256,128]{1,0:T(8,128)(2,1)} %get-tuple-element.12.c_ref, ...), custom_call_target="tpu_custom_call" | custom-call | tf_op jit(solution)/shard_map/pallas_call | solution.py:479
  124.5 2.0 %collective-permute-start.4 = (bf16[12,32,256]{2,1,0:T(8,128)(2,1)}, bf16[12,32,256]{2,1,0:T(8,128)(2,1)S(1)}, u32[]{:S(2)}, u32[]{:S(2)}) collective-permute-start(bf16[12,32,256]{2,1,0:T(8,128)(2,1)} %bitcast.58), channel_id=1, source_target_pairs={{0,4},{4,8},{8,12},{12,16},{16,20},{20,24},{24,28},{28,32},{32,36}... | collective-permute-start | bytes 589832 | tf_op jit(solution)/shard_map/ppermute | solution.py:501
  126.5 5.8 %collective-permute-start.5 = (bf16[12,32,256]{2,1,0:T(8,128)(2,1)}, bf16[12,32,256]{2,1,0:T(8,128)(2,1)S(1)}, u32[]{:S(2)}, u32[]{:S(2)}) collective-permute-start(bf16[12,32,256]{2,1,0:T(8,128)(2,1)} %bitcast.59), channel_id=1, source_target_pairs={{4,0},{8,4},{12,8},{16,12},{20,16},{24,20},{28,24},{32,28},{36,32}... | collective-permute-start | bytes 589832 | tf_op jit(solution)/shard_map/ppermute | solution.py:502
  132.3 0.0 copy-done.12
  132.3 3.6 %shard_map.178 = f32[640,256]{1,0:T(8,128)} custom-call(bf16[128,40,128]{2,1,0:T(8,128)(2,1)} %copy-done), custom_call_target="tpu_custom_call" | custom-call | tf_op jit(solution)/shard_map/pallas_call | solution.py:492
  135.9 0.0 collective-permute-done.4
  135.9 0.0 collective-permute-done.5
  135.9 0.0 copy-done.11
  135.9 1.1 convolution_bitcast_fusion
  (26 shorter events, 0.2 us)
Async XLA Ops:
  6.6 31.4 %all-to-all-start = ((bf16[128,40,128]{2,1,0:T(8,128)(2,1)}), bf16[128,40,128]{2,1,0:T(8,128)(2,1)S(1)}, u32[]{:S(2)}, u32[]{:S(2)}) async-start(bf16[128,40,128]{2,1,0:T(8,128)(2,1)} %shard_map.175), calls=%async_computation | async-start | bytes 2621440 | tf_op jit(solution)/shard_map/all_to_all | solution.py:411
  38.3 9.3 %copy-start.1 = (bf16[32,4,5,8,128]{4,3,0,1,2:T(8,128)(2,1)}, bf16[32,4,5,8,128]{4,3,0,1,2:T(8,128)(2,1)S(1)}, u32[]{:S(2)}) copy-start(bf16[32,4,5,8,128]{4,3,0,1,2:T(8,128)(2,1)S(1)} %copy.28) | copy-start | bytes 3932164
  38.4 13.1 %collective-permute-start = (bf16[3,4,256,128]{3,2,1,0:T(8,128)(2,1)S(1)}, bf16[3,4,256,128]{3,2,1,0:T(8,128)(2,1)S(1)}, u32[]{:S(2)}, u32[]{:S(2)}) collective-permute-start(bf16[3,4,256,128]{3,2,1,0:T(8,128)(2,1)S(1)} %slice_bitcast_fusion), channel_id=1, source_target_pairs={{0,4},{4,0},{8,12},{12,8},{16,20},{20,16},{24,28},{28,24},{32,36},... | collective-permute-start | bytes 2359304 | tf_op jit(solution)/shard_map/ppermute | solution.py:462
  38.8 8.9 %copy-start.5 = (pred[1,256,512]{2,1,0:T(8,128)(4,1)S(1)}, pred[1,256,512]{2,1,0:T(8,128)(4,1)}, u32[]{:S(2)}) copy-start(pred[1,256,512]{2,1,0:T(8,128)(4,1)} %get-tuple-element.26) | copy-start | bytes 393220
  51.5 1.0 copy-start.2
  75.5 5.2 %copy-start.3 = (f32[1,32,1440]{2,1,0:T(8,128)S(1)}, f32[1,32,1440]{2,1,0:T(8,128)}, u32[]{:S(2)}) copy-start(f32[1,32,1440]{2,1,0:T(8,128)} %param.23) | copy-start | bytes 552964
  75.6 5.2 %copy-start.4 = (f32[1,32,1440]{2,1,0:T(8,128)S(1)}, f32[1,32,1440]{2,1,0:T(8,128)}, u32[]{:S(2)}) copy-start(f32[1,32,1440]{2,1,0:T(8,128)} %param.24) | copy-start | bytes 552964
  75.6 11.1 %copy-start.9 = (s32[128]{0:T(128)S(1)}, s32[128]{0:T(128)}, u32[]{:S(2)}) copy-start(s32[128]{0:T(128)} %wave_ref.1) | copy-start | bytes 1540
  75.6 12.1 %copy-start.10 = (s32[2,40]{1,0:T(2,128)S(1)}, s32[2,40]{1,0:T(2,128)}, u32[]{:S(2)}) copy-start(s32[2,40]{1,0:T(2,128)} %param.29) | copy-start | bytes 964
  75.6 35.5 %all-to-all-start.1 = ((bf16[128,40,128]{2,1,0:T(8,128)(2,1)}), bf16[128,40,128]{2,1,0:T(8,128)(2,1)S(1)}, u32[]{:S(2)}, u32[]{:S(2)}) async-start(bf16[128,40,128]{2,1,0:T(8,128)(2,1)} %shard_map.177), calls=%async_computation.1 | async-start | bytes 2621440 | tf_op jit(solution)/shard_map/all_to_all | solution.py:477
  80.8 21.7 %collective-permute-start.1 = (bf16[64,1440]{1,0:T(8,128)(2,1)S(1)}, bf16[64,1440]{1,0:T(8,128)(2,1)S(1)}, u32[]{:S(2)}, u32[]{:S(2)}) collective-permute-start(bf16[64,1440]{1,0:T(8,128)(2,1)S(1)} %pad_maximum_fusion), channel_id=1, source_target_pairs={{0,1},{1,2},{2,3},{3,0},{4,5},{5,6},{6,7},{7,4},{8,9},{9,10},{10,1... | collective-permute-start | bytes 552968 | tf_op jit(solution)/shard_map/ppermute | solution.py:447
  82.4 24.2 %collective-permute-start.2 = (bf16[64,1440]{1,0:T(8,128)(2,1)S(1)}, bf16[64,1440]{1,0:T(8,128)(2,1)S(1)}, u32[]{:S(2)}, u32[]{:S(2)}) collective-permute-start(bf16[64,1440]{1,0:T(8,128)(2,1)S(1)} %pad_maximum_fusion), channel_id=1, source_target_pairs={{0,2},{1,3},{2,0},{3,1},{4,6},{5,7},{6,4},{7,5},{8,10},{9,11},{10,... | collective-permute-start | bytes 552968 | tf_op jit(solution)/shard_map/ppermute | solution.py:447
  85.2 21.4 %collective-permute-start.3 = (bf16[64,1440]{1,0:T(8,128)(2,1)S(1)}, bf16[64,1440]{1,0:T(8,128)(2,1)S(1)}, u32[]{:S(2)}, u32[]{:S(2)}) collective-permute-start(bf16[64,1440]{1,0:T(8,128)(2,1)S(1)} %pad_maximum_fusion), channel_id=1, source_target_pairs={{0,3},{1,0},{2,1},{3,2},{4,7},{5,4},{6,5},{7,6},{8,11},{9,8},{10,9... | collective-permute-start | bytes 552968 | tf_op jit(solution)/shard_map/ppermute | solution.py:447
  102.5 4.1 %copy-start.6 = (bf16[64,1440]{1,0:T(8,128)(2,1)}, bf16[64,1440]{1,0:T(8,128)(2,1)S(1)}, u32[]{:S(2)}) copy-start(bf16[64,1440]{1,0:T(8,128)(2,1)S(1)} %collective-permute-done.1.o1) | copy-start | bytes 552964
  106.6 0.7 copy-start.7
  106.6 0.7 copy-start.8
  111.1 1.1 copy-start
  113.1 19.2 %copy-start.12 = (f32[40]{0:T(128)S(1)}, f32[40]{0:T(128)}, u32[]{:S(2)}) copy-start(f32[40]{0:T(128)} %param.30) | copy-start | bytes 484
  124.5 11.4 %copy-start.11 = (bf16[384,256]{1,0:T(8,128)(2,1)S(1)}, bf16[384,256]{1,0:T(8,128)(2,1)}, u32[]{:S(2)}) copy-start(bf16[384,256]{1,0:T(8,128)(2,1)} %get-tuple-element.16) | copy-start | bytes 589828
  124.5 11.4 %collective-permute-start.4 = (bf16[12,32,256]{2,1,0:T(8,128)(2,1)}, bf16[12,32,256]{2,1,0:T(8,128)(2,1)S(1)}, u32[]{:S(2)}, u32[]{:S(2)}) collective-permute-start(bf16[12,32,256]{2,1,0:T(8,128)(2,1)} %bitcast.58), channel_id=1, source_target_pairs={{0,4},{4,8},{8,12},{12,16},{16,20},{20,24},{24,28},{28,32},{32,36}... | collective-permute-start | bytes 589832 | tf_op jit(solution)/shard_map/ppermute | solution.py:501
  126.5 9.4 %collective-permute-start.5 = (bf16[12,32,256]{2,1,0:T(8,128)(2,1)}, bf16[12,32,256]{2,1,0:T(8,128)(2,1)S(1)}, u32[]{:S(2)}, u32[]{:S(2)}) collective-permute-start(bf16[12,32,256]{2,1,0:T(8,128)(2,1)} %bitcast.59), channel_id=1, source_target_pairs={{4,0},{8,4},{12,8},{16,12},{20,16},{24,20},{28,24},{32,28},{36,32}... | collective-permute-start | bytes 589832 | tf_op jit(solution)/shard_map/ppermute | solution.py:502

commit v5 on v4

--- a/solution.py
+++ b/solution.py
@@ -47,6 +47,10 @@
     return hi, (v - hi.astype(F32)).astype(BF)
 
 
+def position():
+    return lax.axis_index("band"), lax.axis_index("lev")
+
+
 def split_columns():
     row = lax.broadcasted_iota(jnp.int32, (COLS, COLS), 0)
     col = lax.broadcasted_iota(jnp.int32, (COLS, COLS), 1)
@@ -74,7 +78,8 @@
     return arrays
 
 
-def pack_kernel(ids, live_ref, x_ref, s_ref, b_ref, w_ref, k_ref, south_ref, north_ref, q_ref, o_ref, d_ref, t_ref):
+def pack_kernel(live_ref, x_ref, s_ref, b_ref, w_ref, k_ref, south_ref, north_ref, q_ref, o_ref, d_ref, t_ref):
+    ids = position()
     spread = split_columns()
     base = 0
     for ref in (x_ref, s_ref):
@@ -129,10 +134,12 @@
             o_ref[m, XROWS:CHUNK, :] = whole
             return 0
 
-        lax.fori_loop(0, WAVES // 2, put, 0)
-
-
-def operator_kernel(ids, wave_ref, table_ref, p_ref, t_ref, d_ref, sem):
+        lax.fori_loop(0, WAVES // 2, put, 0, unroll=8)
+
+
+def operator_kernel(wave_ref, table_ref, p_ref, t_ref, d_ref, sem):
+    ids = position()
+
     def copy(lo):
         return pltpu.make_async_copy(table_ref.at[ids[1], :, lo], t_ref.at[lo], sem.at[lo])
 
@@ -155,7 +162,8 @@
         p_ref[lo * 256 : (lo + 1) * 256, :] = (p * scale).astype(BF)
 
 
-def tables_kernel(ids, c_ref, a_ref, own_s, own_d, o1, o2, o3, zt_ref, z_ref, so_ref, sr_ref, cp_ref, w_ref, h_ref):
+def tables_kernel(c_ref, a_ref, own_s, own_d, o1, o2, o3, zt_ref, z_ref, so_ref, sr_ref, cp_ref, w_ref, h_ref):
+    ids = position()
     lon = own_s.shape[1]
     fine = a_ref[0:80, :]
     for q in range(lon // 40):
@@ -197,9 +205,12 @@
 
 
 def atmosphere_kernel(
-    ids, g_ref, h_ref, sm_ref, sx_ref, se_ref, p_ref, o_ref, a_ref, x_ref, y_ref, s_ref, f_ref, t_ref
+    g_ref, h_ref, sx_ref, se_ref, p_ref, o_ref, a_ref, x_ref, y_ref, s_ref, f_ref, t_ref
 ):
-    first = ids[0] % 2 == 0
+    first = position()[0] % 2 == 0
+    eye = (
+        lax.broadcasted_iota(jnp.int32, (128, 128), 0) == lax.broadcasted_iota(jnp.int32, (128, 128), 1)
+    ).astype(F32).astype(BF)
     for lo in range(LO):
         lanes = slice(lo * 256, (lo + 1) * 256)
         rows = jnp.concatenate([g_ref[lo // 2, f] for f in range(FIELDS)], axis=1)
@@ -213,24 +224,33 @@
     for lo in range(LO):
         r = lax.broadcasted_iota(jnp.int32, (256, 1), 0)
         place = (r // 8 * LAT + lo * 8 + r % 8).astype(F32)
-        t_ref[lo * 256 : (lo + 1) * 256, :] = jnp.where(
-            place == south, low, jnp.where(place == south + 1.0, high, 0.0)
-        ).astype(BF)
+        for col in range(0, nslot, 128):
+            at, zero = (0, 144) if col % 256 == 0 else (112, 0)
+            lanes = slice(col, col + 128)
+            part = place[at : at + 144]
+            t_ref[lo * 256 + at : lo * 256 + at + 144, lanes] = jnp.where(
+                part == south[:, lanes],
+                low[:, lanes],
+                jnp.where(part == south[:, lanes] + 1.0, high[:, lanes], 0.0),
+            ).astype(BF)
+            t_ref[lo * 256 + zero : lo * 256 + zero + 112, lanes] = jnp.zeros((112, 128), BF)
 
     for lo in range(LO):
-        lanes = slice(lo * 256, (lo + 1) * 256)
-        parts = []
         for f in range(FIELDS):
             if lo < 4:
                 own, other = g_ref[3 + lo % 2, f], h_ref[1 + lo % 2, f]
-                parts.append(jnp.where(first == (lo < 2), own, other))
+                mix = jnp.where(first == (lo < 2), own, other)
             else:
                 own, other = g_ref[2, f].astype(F32), h_ref[0, f].astype(F32)
                 lower = lax.broadcasted_iota(jnp.int32, own.shape, 1) < 64
                 even = pltpu.roll(jnp.where(first, own, other), 64, 1)
-                parts.append(jnp.where(lower, even, jnp.where(first, other, own)).astype(BF))
-        mix = jnp.concatenate(parts, axis=1)
-        a_ref[:, lanes] = lax.dot_general(sm_ref[...], mix, NT, preferred_element_type=F32)
+                mix = jnp.where(lower, even, jnp.where(first, other, own)).astype(BF)
+            turned = lax.dot_general(eye, mix, NT, preferred_element_type=F32)
+            for half in range(2):
+                for c in range(2):
+                    a_ref[2 * lo + half, pl.ds(2 * f + c, NPAIR, stride=8), :] = turned[
+                        0:NPAIR, half * 128 : half * 128 + 128
+                    ]
 
     weight = x_ref[28 * 8 : 29 * 8, :]
     for l in range(0, LEVELS, 2):
@@ -249,7 +269,7 @@
         acc = [mixing_diagonal * v for v in mid]
         acc[LEVELS - 1] = acc[LEVELS - 1] + flux
         for i, (l, p) in enumerate(PAIRS):
-            a = a_ref[8 * i : 8 * i + 8, lanes]
+            a = a_ref[2 * n + half, 8 * i : 8 * i + 8, :]
             acc[l] = acc[l] + a * mid[p]
             acc[p] = acc[p] - a * mid[l]
         scale = x_ref[28 * 8 : 29 * 8, lanes]
@@ -296,10 +316,10 @@
 
 
 def ocean_kernel(
-    ids, f_ref, zt_ref, z_ref, c_ref, o0_ref, r_ref, so_ref, co_ref, o_ref, w_ref, p_ref, t_ref, h_ref
+    f_ref, zt_ref, z_ref, c_ref, o0_ref, r_ref, so_ref, co_ref, o_ref, w_ref, p_ref, t_ref, h_ref
 ):
     lon = o_ref.shape[0]
-    start = pl.multiple_of(ids[1] * SLOTS, SLOTS)
+    start = pl.multiple_of(position()[1] * SLOTS, SLOTS)
     o_ref[...] = o0_ref[...]
     scale = 1.0 / math.sqrt(lon)
 
@@ -334,7 +354,7 @@
         t_ref[pl.ds(pl.multiple_of(m * 16, 16), 16), :] = b_ref[m, 24:40, :].astype(F32)
         return 0
 
-    lax.fori_loop(0, WAVES, take, 0)
+    lax.fori_loop(0, WAVES, take, 0, unroll=8)
     for q in range(2):
         for h in range(8):
             v = t_ref[pl.ds(q * 8 + h, WAVES, stride=16), :].T
@@ -386,18 +406,15 @@
     air_second_share,
 ):
     band = lax.axis_index("band")
-    lev = lax.axis_index("lev")
-    ids = jnp.stack([band, lev]).astype(jnp.int32)
     lon = sea_boundary_values.shape[2]
     degree_count = associated_polynomial_table.shape[2]
 
     chunks = call(
         pack_kernel,
-        smem(2) + vmem(8),
+        smem(1) + vmem(8),
         shape((WAVES, CHUNK, 128), BF),
         [pltpu.VMEM((2, ITEMS * LAT, 128), F32), pltpu.VMEM((WAVES * XROWS, 128), F32)],
     )(
-        ids,
         patch_active_entries,
         air_fourier_coefficients.reshape(LEVELS * LAT, COLS),
         skin_heat_earlier.reshape(STEPS * LAT, COLS),
@@ -412,18 +429,16 @@
 
     operator = call(
         operator_kernel,
-        smem(2) + [pl.BlockSpec(memory_space=pl.ANY)],
+        smem(1) + [pl.BlockSpec(memory_space=pl.ANY)],
         shape((NLAT, NLAT), BF),
         [
             pltpu.VMEM((LO, BANDS, 8, degree_count), BF),
             pltpu.VMEM((NLAT, degree_count), BF),
             pltpu.SemaphoreType.DMA((LO,)),
         ],
-    )(ids, east_west_harmonic, associated_polynomial_table.reshape(FIELDS, BANDS, LO, 8, degree_count))
-
-    row = jnp.arange(NPAIR * 8, dtype=jnp.int32)[:, None]
+    )(east_west_harmonic, associated_polynomial_table.reshape(FIELDS, BANDS, LO, 8, degree_count))
+
     col = jnp.arange(FIELDS * 128, dtype=jnp.int32)[None, :]
-    select_mix = ((row // 8 == col % 128) & (row % 8 // 2 == col // 128)).astype(BF)
     row = jnp.arange(ITEMS * 8, dtype=jnp.int32)[:, None]
     item = row // 8
     same = (col % ITEMS == item) & (col // 128 == row % 8 // 2)
@@ -447,7 +462,7 @@
         others.append(lax.ppermute(sent, "lev", [(i, (i + d) % FIELDS) for i in range(FIELDS)]))
     zonal_t, zonal, ocean0, shrink, couple = call(
         tables_kernel,
-        smem(2) + vmem(6),
+        smem(1) + vmem(6),
         (
             shape((lon, COLS), BF),
             shape((COLS, lon), BF),
@@ -456,29 +471,29 @@
             shape((256, 128), BF),
         ),
         [pltpu.VMEM((lon, COLS), F32), pltpu.VMEM((2, 128, lon), F32)],
-    )(ids, sea_coupling_matrix, angle_parts, own_sea, own_damp, *others)
+    )(sea_coupling_matrix, angle_parts, own_sea, own_damp, *others)
 
     got = got.reshape(BANDS, FIELDS, 5, 8, 128).transpose(2, 1, 0, 3, 4).reshape(5, FIELDS, 256, 128)
     partner = lax.ppermute(got[2:], "band", [(i, i ^ 1) for i in range(BANDS)])
     out = call(
         atmosphere_kernel,
-        smem(1) + vmem(6),
+        vmem(5),
         shape((WAVES, OUT_ROWS, 128), BF),
         [
-            pltpu.VMEM((NPAIR * 8, NLAT), F32),
+            pltpu.VMEM((NLAT // 128, NPAIR * 8, 128), F32),
             pltpu.VMEM((ITEMS * 8, NLAT), F32),
             pltpu.VMEM((LO, 128, 256), F32),
             pltpu.VMEM((2, 128, NLAT), BF),
             pltpu.VMEM((NLAT // 128, STEPS * 8, 128), F32),
             pltpu.VMEM((NLAT, BANDS * SLOTS), BF),
         ],
-    )(ids, got, partner, select_mix, select_x, select_end, operator)
+    )(got, partner, select_x, select_end, operator)
 
     back = lax.all_to_all(out, AXES, 0, 0, tiled=True)
     flux_in = back[:, :24].reshape(WAVES, 2, STEPS, 128).transpose(2, 1, 0, 3).reshape(STEPS, COLS, 128)
     sea_end, ocean_coef = call(
         ocean_kernel,
-        smem(1) + vmem(6),
+        vmem(6),
         (shape((SLOTS, lon), F32), shape((STEPS * SLOTS, COLS), BF)),
         [
             pltpu.VMEM((lon, 128), F32),
@@ -487,7 +502,7 @@
             pltpu.VMEM((STEPS * SLOTS, COLS), F32),
             pltpu.VMEM((2, 128, COLS), F32),
         ],
-    )(ids, flux_in, zonal_t, zonal, couple, ocean0, shrink)
+    )(flux_in, zonal_t, zonal, couple, ocean0, shrink)
     ocean_coef = ocean_coef.reshape(STEPS, SLOTS, COLS)
     air_coefficients_end = call(
         unpack_kernel,

time: 139 us -> 127 us (0.914)
  the two profiles are of different devices: /device:TPU:32 before, /device:TPU:7 now
where the time goes in v5:
time: 127 us
  Pallas kernels  53.1 us (42%)
  waiting for transfers between devices  35.5 us (28%)
  starting transfers between devices  27.6 us (22%)
  local copies, waits for them, and re-layouts  4.12 us (3%)
  other arithmetic  3.95 us (3%)
  between operations  1.49 us (1%)
    pallas_call x1, Pallas kernels, per_device(): call(atmosphere_kernel, vmem(5), shape((WAVES, OUT_ROWS, 128), BF), [pltp...  22.2 us
    ppermute x3, waiting for transfers between devices, per_device(): lax.ppermute(sent, 'lev', [(i, (i + d) % FIELDS) for i in range(FIELDS)])  19.3 us
    all_to_all x1, waiting for transfers between devices, per_device(): got = lax.all_to_all(chunks, AXES, 0, 0, tiled=True)  11.7 us
    pallas_call x1, Pallas kernels, per_device(): call(ocean_kernel, vmem(6), (shape((SLOTS, lon), F32), shape((STEPS * SLO...  11.4 us
    all_to_all x1, starting transfers between devices, per_device(): got = lax.all_to_all(chunks, AXES, 0, 0, tiled=True)  10.8 us
    pallas_call x1, Pallas kernels, per_device(): call(operator_kernel, smem(1) + [pl.BlockSpec(memory_space=pl.ANY)], shap...  8.73 us
    all_to_all x1, starting transfers between devices, per_device(): back = lax.all_to_all(out, AXES, 0, 0, tiled=True)  5.37 us
    ppermute x3, starting transfers between devices, per_device(): lax.ppermute(sent, 'lev', [(i, (i + d) % FIELDS) for i in range(FIELDS)])  4.95 us
  transfers between devices with their start and end apart: 8, of which 4 were waited for; matrix products, arithmetic and copies ran while one was open for 3% of the time, Pallas kernels for 12%

profile of v5, /device:TPU:7, one launch (start us, length us, event | category | flops | bytes accessed | tf_op | source)
XLA Modules:
  0.0 126.8 jit_solution(8968316969777644829)
XLA Ops:
  1.3 4.1 %shard_map.175 = bf16[128,40,128]{2,1,0:T(8,128)(2,1)} custom-call(s32[1]{0:T(128)S(6)} %copy.29.live_ref, f32[640,256]{1,0:T(8,128)} %bitcast.48, f32[480,256]{1,0:T(8,128)} %bitcast.50, f32[256,40]{1,0:T(8,128)} %bitcast.51, f32[1,40]{1,0:T(1,128)} %bitcast.52, f32[1,40]{1,0:T(1,128)} %k_ref.1, s32[1,32]{1,0:T(1,128)} %bitcast.53, f32[1,32]{1,0:T(1,128)} %bitcast.54, ...), custom_call_target="tpu_custom_call" | custom-call | tf_op jit(solution)/shard_map/pallas_call | solution.py:412
  5.4 10.8 %all-to-all-start = ((bf16[128,40,128]{2,1,0:T(8,128)(2,1)}), bf16[128,40,128]{2,1,0:T(8,128)(2,1)S(1)}, u32[]{:S(2)}, u32[]{:S(2)}) async-start(bf16[128,40,128]{2,1,0:T(8,128)(2,1)} %shard_map.175), calls=%async_computation | async-start | bytes 2621440 | tf_op jit(solution)/shard_map/all_to_all | solution.py:428
  16.2 8.7 %shard_map.176.p_ref = bf16[1280,1280]{1,0:T(8,128)(2,1)} custom-call(s32[128]{0:T(128)} %wave_ref.1, bf16[4,32,5,8,1280]{4,3,2,1,0:T(8,128)(2,1)} %bitcast.40), custom_call_target="tpu_custom_call" | custom-call | tf_op jit(solution)/shard_map/pallas_call | solution.py:430
  25.0 11.7 %all-to-all-done = bf16[128,40,128]{2,1,0:T(8,128)(2,1)S(1)} async-done(((bf16[128,40,128]{2,1,0:T(8,128)(2,1)}), bf16[128,40,128]{2,1,0:T(8,128)(2,1)S(1)}, u32[]{:S(2)}, u32[]{:S(2)}) %all-to-all-start) | async-done | bytes 1310752 | tf_op jit(solution)/shard_map/all_to_all | solution.py:428
  36.7 0.3 copy.28
  37.1 0.0 copy-start.1
  37.1 0.1 slice_bitcast_fusion
  37.2 0.5 collective-permute-start
  37.7 0.4 broadcast_and_fusion.1
  38.1 0.9 add_convert_fusion.sx_ref
  39.0 0.0 copy-done.1
  39.0 1.5 %fusion.se_ref = bf16[640,1024]{1,0:T(8,128)(2,1)} fusion(s32[1024]{0:T(1024)S(1)} %fusion.41), kind=kLoop, calls=%fused_computation.1 | loop fusion | flops 1310720 | bytes 1314816 | tf_op jit(solution)/shard_map/convert_element_type | solution.py:451
  40.5 0.0 collective-permute-done.h_ref
  40.5 0.0 copy-start.2
  40.5 0.9 copy-done.2
  41.4 22.2 %shard_map.177 = bf16[128,40,128]{2,1,0:T(8,128)(2,1)} custom-call(bf16[5,4,256,128]{3,2,1,0:T(8,128)(2,1)} %bitcast.42, bf16[3,4,256,128]{3,2,1,0:T(8,128)(2,1)} %copy-done.2, bf16[2,256,512]{2,1,0:T(8,128)(2,1)} %add_convert_fusion.sx_ref, bf16[640,1024]{1,0:T(8,128)(2,1)} %fusion.se_ref, bf16[1280,1280]{1,0:T(8,128)(2,1)} %shard_map.176.p_ref), custom_call_target="tpu_custom_call" | custom-call | tf_op jit(solution)/shard_map/pallas_call | solution.py:478
  63.6 0.0 copy-start.3
  63.6 0.0 copy-start.4
  63.6 5.4 %all-to-all-start.1 = ((bf16[128,40,128]{2,1,0:T(8,128)(2,1)}), bf16[128,40,128]{2,1,0:T(8,128)(2,1)S(1)}, u32[]{:S(2)}, u32[]{:S(2)}) async-start(bf16[128,40,128]{2,1,0:T(8,128)(2,1)} %shard_map.177), calls=%async_computation.1 | async-start | bytes 2621440 | tf_op jit(solution)/shard_map/all_to_all | solution.py:492
  69.0 0.0 copy-done.3
  69.0 0.0 copy-done.4
  69.1 1.3 %collective-permute-start.1 = (bf16[64,1440]{1,0:T(8,128)(2,1)S(1)}, bf16[64,1440]{1,0:T(8,128)(2,1)S(1)}, u32[]{:S(2)}, u32[]{:S(2)}) collective-permute-start(bf16[64,1440]{1,0:T(8,128)(2,1)S(1)} %pad_maximum_fusion), channel_id=1, source_target_pairs={{0,1},{1,2},{2,3},{3,0},{4,5},{5,6},{6,7},{7,4},{8,9},{9,10},{10,1... | collective-permute-start | bytes 552968 | tf_op jit(solution)/shard_map/ppermute | solution.py:462
  70.4 2.5 %collective-permute-start.2 = (bf16[64,1440]{1,0:T(8,128)(2,1)S(1)}, bf16[64,1440]{1,0:T(8,128)(2,1)S(1)}, u32[]{:S(2)}, u32[]{:S(2)}) collective-permute-start(bf16[64,1440]{1,0:T(8,128)(2,1)S(1)} %pad_maximum_fusion), channel_id=1, source_target_pairs={{0,2},{1,3},{2,0},{3,1},{4,6},{5,7},{6,4},{7,5},{8,10},{9,11},{10,... | collective-permute-start | bytes 552968 | tf_op jit(solution)/shard_map/ppermute | solution.py:462
  72.9 1.1 collective-permute-start.3
  74.0 0.0 copy-done.8
  74.1 1.0 sine_select_fusion.a_ref
  75.1 0.0 copy-done.9
  75.1 15.1 %collective-permute-done.1.o1 = bf16[64,1440]{1,0:T(8,128)(2,1)S(1)} collective-permute-done((bf16[64,1440]{1,0:T(8,128)(2,1)S(1)}, bf16[64,1440]{1,0:T(8,128)(2,1)S(1)}, u32[]{:S(2)}, u32[]{:S(2)}) %collective-permute-start.1) | collective-permute-done | bytes 184352 | tf_op jit(solution)/shard_map/ppermute | solution.py:462
  90.2 4.2 %collective-permute-done.2.o2 = bf16[64,1440]{1,0:T(8,128)(2,1)S(1)} collective-permute-done((bf16[64,1440]{1,0:T(8,128)(2,1)S(1)}, bf16[64,1440]{1,0:T(8,128)(2,1)S(1)}, u32[]{:S(2)}, u32[]{:S(2)}) %collective-permute-start.2) | collective-permute-done | bytes 184352 | tf_op jit(solution)/shard_map/ppermute | solution.py:462
  94.5 0.0 collective-permute-done.3.o3
  94.5 0.0 copy-done.5
  94.5 0.7 copy-done.6
  95.1 0.1 copy-done.7
  95.2 3.7 %shard_map.179 = (bf16[1440,256]{1,0:T(8,128)(2,1)}, bf16[256,1440]{1,0:T(8,128)(2,1)}, f32[1440,128]{1,0:T(8,128)}, f32[1440,128]{1,0:T(8,128)}, bf16[256,128]{1,0:T(8,128)(2,1)}) custom-call(f32[4,4]{1,0:T(4,128)} %c_ref.1, f32[160,128]{1,0:T(8,128)} %sine_select_fusion.a_ref, f32[32,1440]{1,0:T(8,128)} %bitcast.46, f32[32,1440]{1,0:T(8,128)} %bitcast.47, ...), custom_call_target="tpu_custom_call" | custom-call | tf_op jit(solution)/shard_map/pallas_call | solution.py:463
  98.9 0.0 all-to-all-done.1.b_ref
  98.9 0.1 slice.21
  99.0 0.2 copy.23
  99.2 0.8 copy-done
  100.0 1.0 copy.24
  101.0 11.4 %shard_map.180 = (f32[32,1440]{1,0:T(8,128)}, bf16[384,256]{1,0:T(8,128)(2,1)}) custom-call(bf16[12,256,128]{2,1,0:T(8,128)(2,1)} %bitcast.45, bf16[1440,256]{1,0:T(8,128)(2,1)} %get-tuple-element.10.zt_ref, bf16[256,1440]{1,0:T(8,128)(2,1)} %get-tuple-element.11.z_ref, bf16[256,128]{1,0:T(8,128)(2,1)} %get-tuple-element.12.c_ref, ...), custom_call_target="tpu_custom_call" | custom-call | tf_op jit(solution)/shard_map/pallas_call | solution.py:494
  112.4 4.1 %collective-permute-start.4 = (bf16[12,32,256]{2,1,0:T(8,128)(2,1)}, bf16[12,32,256]{2,1,0:T(8,128)(2,1)S(1)}, u32[]{:S(2)}, u32[]{:S(2)}) collective-permute-start(bf16[12,32,256]{2,1,0:T(8,128)(2,1)} %bitcast.56), channel_id=1, source_target_pairs={{0,4},{4,8},{8,12},{12,16},{16,20},{20,24},{24,28},{28,32},{32,36}... | collective-permute-start | bytes 589832 | tf_op jit(solution)/shard_map/ppermute | solution.py:516
  116.5 1.9 %collective-permute-start.5 = (bf16[12,32,256]{2,1,0:T(8,128)(2,1)}, bf16[12,32,256]{2,1,0:T(8,128)(2,1)S(1)}, u32[]{:S(2)}, u32[]{:S(2)}) collective-permute-start(bf16[12,32,256]{2,1,0:T(8,128)(2,1)} %bitcast.57), channel_id=1, source_target_pairs={{4,0},{8,4},{12,8},{16,12},{20,16},{24,20},{28,24},{32,28},{36,32}... | collective-permute-start | bytes 589832 | tf_op jit(solution)/shard_map/ppermute | solution.py:517
  118.4 0.0 copy-done.11
  118.4 2.9 %shard_map.178 = f32[640,256]{1,0:T(8,128)} custom-call(bf16[128,40,128]{2,1,0:T(8,128)(2,1)} %copy-done), custom_call_target="tpu_custom_call" | custom-call | tf_op jit(solution)/shard_map/pallas_call | solution.py:507
  121.3 0.0 collective-permute-done.4
  121.3 4.4 %collective-permute-done.5 = bf16[12,32,256]{2,1,0:T(8,128)(2,1)S(1)} collective-permute-done((bf16[12,32,256]{2,1,0:T(8,128)(2,1)}, bf16[12,32,256]{2,1,0:T(8,128)(2,1)S(1)}, u32[]{:S(2)}, u32[]{:S(2)}) %collective-permute-start.5) | collective-permute-done | bytes 196640 | tf_op jit(solution)/shard_map/ppermute | solution.py:517
  125.8 0.0 copy-done.10
  125.8 1.0 convolution_bitcast_fusion
  (21 shorter events, 0.1 us)
Async XLA Ops:
  5.4 31.3 %all-to-all-start = ((bf16[128,40,128]{2,1,0:T(8,128)(2,1)}), bf16[128,40,128]{2,1,0:T(8,128)(2,1)S(1)}, u32[]{:S(2)}, u32[]{:S(2)}) async-start(bf16[128,40,128]{2,1,0:T(8,128)(2,1)} %shard_map.175), calls=%async_computation | async-start | bytes 2621440 | tf_op jit(solution)/shard_map/all_to_all | solution.py:428
  37.1 1.9 %copy-start.1 = (bf16[32,4,5,8,128]{4,3,0,1,2:T(8,128)(2,1)}, bf16[32,4,5,8,128]{4,3,0,1,2:T(8,128)(2,1)S(1)}, u32[]{:S(2)}) copy-start(bf16[32,4,5,8,128]{4,3,0,1,2:T(8,128)(2,1)S(1)} %copy.28) | copy-start | bytes 3932164
  37.2 3.3 %collective-permute-start = (bf16[3,4,256,128]{3,2,1,0:T(8,128)(2,1)S(1)}, bf16[3,4,256,128]{3,2,1,0:T(8,128)(2,1)S(1)}, u32[]{:S(2)}, u32[]{:S(2)}) collective-permute-start(bf16[3,4,256,128]{3,2,1,0:T(8,128)(2,1)S(1)} %slice_bitcast_fusion), channel_id=1, source_target_pairs={{0,4},{4,0},{8,12},{12,8},{16,20},{20,16},{24,28},{28,24},{32,36},... | collective-permute-start | bytes 2359304 | tf_op jit(solution)/shard_map/ppermute | solution.py:477
  40.5 0.9 copy-start.2
  63.6 5.4 %copy-start.3 = (f32[1,32,1440]{2,1,0:T(8,128)S(1)}, f32[1,32,1440]{2,1,0:T(8,128)}, u32[]{:S(2)}) copy-start(f32[1,32,1440]{2,1,0:T(8,128)} %param.23) | copy-start | bytes 552964
  63.6 5.4 %copy-start.4 = (f32[1,32,1440]{2,1,0:T(8,128)S(1)}, f32[1,32,1440]{2,1,0:T(8,128)}, u32[]{:S(2)}) copy-start(f32[1,32,1440]{2,1,0:T(8,128)} %param.24) | copy-start | bytes 552964
  63.6 10.5 %copy-start.8 = (s32[128]{0:T(128)S(1)}, s32[128]{0:T(128)}, u32[]{:S(2)}) copy-start(s32[128]{0:T(128)} %wave_ref.1) | copy-start | bytes 1540
  63.6 11.5 %copy-start.9 = (s32[2,40]{1,0:T(2,128)S(1)}, s32[2,40]{1,0:T(2,128)}, u32[]{:S(2)}) copy-start(s32[2,40]{1,0:T(2,128)} %param.29) | copy-start | bytes 964
  63.6 35.3 %all-to-all-start.1 = ((bf16[128,40,128]{2,1,0:T(8,128)(2,1)}), bf16[128,40,128]{2,1,0:T(8,128)(2,1)S(1)}, u32[]{:S(2)}, u32[]{:S(2)}) async-start(bf16[128,40,128]{2,1,0:T(8,128)(2,1)} %shard_map.177), calls=%async_computation.1 | async-start | bytes 2621440 | tf_op jit(solution)/shard_map/all_to_all | solution.py:492
  69.1 21.2 %collective-permute-start.1 = (bf16[64,1440]{1,0:T(8,128)(2,1)S(1)}, bf16[64,1440]{1,0:T(8,128)(2,1)S(1)}, u32[]{:S(2)}, u32[]{:S(2)}) collective-permute-start(bf16[64,1440]{1,0:T(8,128)(2,1)S(1)} %pad_maximum_fusion), channel_id=1, source_target_pairs={{0,1},{1,2},{2,3},{3,0},{4,5},{5,6},{6,7},{7,4},{8,9},{9,10},{10,1... | collective-permute-start | bytes 552968 | tf_op jit(solution)/shard_map/ppermute | solution.py:462
  70.4 24.1 %collective-permute-start.2 = (bf16[64,1440]{1,0:T(8,128)(2,1)S(1)}, bf16[64,1440]{1,0:T(8,128)(2,1)S(1)}, u32[]{:S(2)}, u32[]{:S(2)}) collective-permute-start(bf16[64,1440]{1,0:T(8,128)(2,1)S(1)} %pad_maximum_fusion), channel_id=1, source_target_pairs={{0,2},{1,3},{2,0},{3,1},{4,6},{5,7},{6,4},{7,5},{8,10},{9,11},{10,... | collective-permute-start | bytes 552968 | tf_op jit(solution)/shard_map/ppermute | solution.py:462
  72.9 21.6 %collective-permute-start.3 = (bf16[64,1440]{1,0:T(8,128)(2,1)S(1)}, bf16[64,1440]{1,0:T(8,128)(2,1)S(1)}, u32[]{:S(2)}, u32[]{:S(2)}) collective-permute-start(bf16[64,1440]{1,0:T(8,128)(2,1)S(1)} %pad_maximum_fusion), channel_id=1, source_target_pairs={{0,3},{1,0},{2,1},{3,2},{4,7},{5,4},{6,5},{7,6},{8,11},{9,8},{10,9... | collective-permute-start | bytes 552968 | tf_op jit(solution)/shard_map/ppermute | solution.py:462
  90.2 4.2 %copy-start.5 = (bf16[64,1440]{1,0:T(8,128)(2,1)}, bf16[64,1440]{1,0:T(8,128)(2,1)S(1)}, u32[]{:S(2)}) copy-start(bf16[64,1440]{1,0:T(8,128)(2,1)S(1)} %collective-permute-done.1.o1) | copy-start | bytes 552964
  94.5 0.7 copy-start.6
  94.5 0.7 copy-start.7
  98.9 1.1 copy-start
  101.0 17.4 %copy-start.11 = (f32[40]{0:T(128)S(1)}, f32[40]{0:T(128)}, u32[]{:S(2)}) copy-start(f32[40]{0:T(128)} %param.30) | copy-start | bytes 484
  112.4 13.4 %copy-start.10 = (bf16[384,256]{1,0:T(8,128)(2,1)S(1)}, bf16[384,256]{1,0:T(8,128)(2,1)}, u32[]{:S(2)}) copy-start(bf16[384,256]{1,0:T(8,128)(2,1)} %get-tuple-element.16) | copy-start | bytes 589828
  112.4 9.0 %collective-permute-start.4 = (bf16[12,32,256]{2,1,0:T(8,128)(2,1)}, bf16[12,32,256]{2,1,0:T(8,128)(2,1)S(1)}, u32[]{:S(2)}, u32[]{:S(2)}) collective-permute-start(bf16[12,32,256]{2,1,0:T(8,128)(2,1)} %bitcast.56), channel_id=1, source_target_pairs={{0,4},{4,8},{8,12},{12,16},{16,20},{20,24},{24,28},{28,32},{32,36}... | collective-permute-start | bytes 589832 | tf_op jit(solution)/shard_map/ppermute | solution.py:516
  116.5 9.3 %collective-permute-start.5 = (bf16[12,32,256]{2,1,0:T(8,128)(2,1)}, bf16[12,32,256]{2,1,0:T(8,128)(2,1)S(1)}, u32[]{:S(2)}, u32[]{:S(2)}) collective-permute-start(bf16[12,32,256]{2,1,0:T(8,128)(2,1)} %bitcast.57), channel_id=1, source_target_pairs={{4,0},{8,4},{12,8},{16,12},{20,16},{24,20},{28,24},{32,28},{36,32}... | collective-permute-start | bytes 589832 | tf_op jit(solution)/shard_map/ppermute | solution.py:517

commit v6 on v5

--- a/solution.py
+++ b/solution.py
@@ -205,8 +205,15 @@
 
 
 def atmosphere_kernel(
-    g_ref, h_ref, sx_ref, se_ref, p_ref, o_ref, a_ref, x_ref, y_ref, s_ref, f_ref, t_ref
+    g_ref, h_any, sx_ref, se_any, p_any, o_ref,
+    a_ref, x_ref, y_ref, s_ref, f_ref, t_ref, h_ref, se_ref, p_ref, sem,
 ):
+    copies = [
+        pltpu.make_async_copy(src, dst, sem.at[i])
+        for i, (src, dst) in enumerate(((h_any, h_ref), (p_any, p_ref), (se_any, se_ref)))
+    ]
+    for copy in copies:
+        copy.start()
     first = position()[0] % 2 == 0
     eye = (
         lax.broadcasted_iota(jnp.int32, (128, 128), 0) == lax.broadcasted_iota(jnp.int32, (128, 128), 1)
@@ -235,6 +242,7 @@
             ).astype(BF)
             t_ref[lo * 256 + zero : lo * 256 + zero + 112, lanes] = jnp.zeros((112, 128), BF)
 
+    copies[0].wait()
     for lo in range(LO):
         for f in range(FIELDS):
             if lo < 4:
@@ -252,6 +260,8 @@
                         0:NPAIR, half * 128 : half * 128 + 128
                     ]
 
+    copies[1].wait()
+    copies[2].wait()
     weight = x_ref[28 * 8 : 29 * 8, :]
     for l in range(0, LEVELS, 2):
         pair = x_ref[8 * l : 8 * l + 16, :].reshape(2, 8, NLAT) * weight[None]
@@ -316,24 +326,34 @@
 
 
 def ocean_kernel(
-    f_ref, zt_ref, z_ref, c_ref, o0_ref, r_ref, so_ref, co_ref, o_ref, w_ref, p_ref, t_ref, h_ref
+    f_ref, zt_ref, z_any, c_ref, o0_any, r_any, so_ref, co_ref,
+    o_ref, w_ref, p_ref, t_ref, h_ref, z_ref, r_ref, sem,
 ):
     lon = o_ref.shape[0]
     start = pl.multiple_of(position()[1] * SLOTS, SLOTS)
-    o_ref[...] = o0_ref[...]
+    copies = [
+        pltpu.make_async_copy(src, dst, sem.at[i])
+        for i, (src, dst) in enumerate(((o0_any, o_ref), (r_any, r_ref), (z_any, z_ref)))
+    ]
+    for copy in copies:
+        copy.start()
+
+    def push(j, slot):
+        pair = jnp.concatenate([f_ref[2 * j], f_ref[2 * j + 1]], axis=1)
+        p_ref[slot] = jnp.dot(zt_ref[...], pair, preferred_element_type=F32)
+
     scale = 1.0 / math.sqrt(lon)
 
     def two_steps(j, _):
-        pair = jnp.concatenate([f_ref[2 * j], f_ref[2 * j + 1]], axis=1)
-        p_ref[...] = jnp.dot(zt_ref[...], pair, preferred_element_type=F32)
         for i in range(2):
             coarse = o_ref[...].astype(BF)
             pull = jnp.dot(
                 jnp.concatenate([coarse, coarse], axis=1), c_ref[...], preferred_element_type=F32
             )
-            updated = (o_ref[...] + (pull + p_ref[:, i * 128 : (i + 1) * 128])) * r_ref[...]
+            updated = (o_ref[...] + (pull + p_ref[j % 2, :, i * 128 : (i + 1) * 128])) * r_ref[...]
             o_ref[...] = updated
             w_ref[:, i * 128 : (i + 1) * 128] = updated.astype(BF)
+        push(jnp.minimum(j + 1, STEPS // 2 - 1), (j + 1) % 2)
         coef = jnp.dot(z_ref[...], w_ref[...], preferred_element_type=F32) * scale
         for i in range(2):
             h_ref[i] = coef[:, i * 128 : (i + 1) * 128].T
@@ -341,6 +361,9 @@
             t_ref[pl.ds(at, SLOTS), :] = h_ref[i, pl.ds(start, SLOTS), :]
         return 0
 
+    push(0, 0)
+    for copy in copies:
+        copy.wait()
     lax.fori_loop(0, STEPS // 2, two_steps, 0)
     co_ref[...] = jnp.dot(t_ref[...].astype(BF), join_columns(), preferred_element_type=F32).astype(BF)
     for x in range(0, lon, 128):
@@ -349,9 +372,13 @@
         so_ref[:, x : x + w] = h_ref[0, pl.ds(start, SLOTS), 0:w]
 
 
-def unpack_kernel(b_ref, o_ref, t_ref, v_ref):
+def unpack_kernel(b_any, o_ref, t_ref, v_ref, b_ref, sem):
+    copy = pltpu.make_async_copy(b_any.at[:, 24:40, :], b_ref, sem)
+    copy.start()
+    copy.wait()
+
     def take(m, _):
-        t_ref[pl.ds(pl.multiple_of(m * 16, 16), 16), :] = b_ref[m, 24:40, :].astype(F32)
+        t_ref[pl.ds(pl.multiple_of(m * 16, 16), 16), :] = b_ref[m].astype(F32)
         return 0
 
     lax.fori_loop(0, WAVES, take, 0, unroll=8)
@@ -370,6 +397,10 @@
     return [pl.BlockSpec(memory_space=pltpu.VMEM)] * n
 
 
+def anywhere(n):
+    return [pl.BlockSpec(memory_space=pl.ANY)] * n
+
+
 def smem(n):
     return [pl.BlockSpec(memory_space=pltpu.SMEM)] * n
 
@@ -386,6 +417,23 @@
 
 def shape(dims, kind):
     return jax.ShapeDtypeStruct(dims, kind)
+
+
+def state_selection():
+    col = jnp.arange(FIELDS * 128, dtype=jnp.int32)[None, :]
+    row = jnp.arange(ITEMS * 8, dtype=jnp.int32)[:, None]
+    item = row // 8
+    same = (col % ITEMS == item) & (col // 128 == row % 8 // 2)
+    same_c = (col % 64 // ITEMS == row % 2) | (item == 28) | (item == 29)
+    return jnp.stack([same & same_c & (col % 128 // 64 == q) for q in range(2)]).astype(BF)
+
+
+def end_selection():
+    row = jnp.arange(LO * 128, dtype=jnp.int32)[:, None]
+    col = jnp.arange(2 * FIELDS * 128, dtype=jnp.int32)[None, :]
+    lo = col // 512 * 4 + col % 128 // 32
+    at = lo * 128 + col % LEVELS * 8 + col % 512 // 128 * 2 + col % 32 // LEVELS
+    return (row == at).astype(BF)
 
 
 def per_device(
@@ -438,17 +486,8 @@
         ],
     )(east_west_harmonic, associated_polynomial_table.reshape(FIELDS, BANDS, LO, 8, degree_count))
 
-    col = jnp.arange(FIELDS * 128, dtype=jnp.int32)[None, :]
-    row = jnp.arange(ITEMS * 8, dtype=jnp.int32)[:, None]
-    item = row // 8
-    same = (col % ITEMS == item) & (col // 128 == row % 8 // 2)
-    same_c = (col % 64 // ITEMS == row % 2) | (item == 28) | (item == 29)
-    select_x = jnp.stack([same & same_c & (col % 128 // 64 == q) for q in range(2)]).astype(BF)
-    row = jnp.arange(LO * 128, dtype=jnp.int32)[:, None]
-    col = jnp.arange(2 * FIELDS * 128, dtype=jnp.int32)[None, :]
-    lo = col // 512 * 4 + col % 128 // 32
-    at = lo * 128 + col % LEVELS * 8 + col % 512 // 128 * 2 + col % 32 // LEVELS
-    select_end = (row == at).astype(BF)
+    select_x = state_selection()
+    select_end = end_selection()
 
     part = jnp.arange(160, dtype=jnp.int32)[:, None]
     longitude = jnp.where(part < 80, part % 40, part % 40 * 40)
@@ -477,7 +516,7 @@
     partner = lax.ppermute(got[2:], "band", [(i, i ^ 1) for i in range(BANDS)])
     out = call(
         atmosphere_kernel,
-        vmem(5),
+        vmem(1) + anywhere(1) + vmem(1) + anywhere(2),
         shape((WAVES, OUT_ROWS, 128), BF),
         [
             pltpu.VMEM((NLAT // 128, NPAIR * 8, 128), F32),
@@ -486,6 +525,10 @@
             pltpu.VMEM((2, 128, NLAT), BF),
             pltpu.VMEM((NLAT // 128, STEPS * 8, 128), F32),
             pltpu.VMEM((NLAT, BANDS * SLOTS), BF),
+            pltpu.VMEM((3, FIELDS, 256, 128), BF),
+            pltpu.VMEM((LO * 128, 1024), BF),
+            pltpu.VMEM((NLAT, NLAT), BF),
+            pltpu.SemaphoreType.DMA((3,)),
         ],
     )(got, partner, select_x, select_end, operator)
 
@@ -493,22 +536,30 @@
     flux_in = back[:, :24].reshape(WAVES, 2, STEPS, 128).transpose(2, 1, 0, 3).reshape(STEPS, COLS, 128)
     sea_end, ocean_coef = call(
         ocean_kernel,
-        vmem(6),
+        vmem(2) + anywhere(1) + vmem(1) + anywhere(2),
         (shape((SLOTS, lon), F32), shape((STEPS * SLOTS, COLS), BF)),
         [
             pltpu.VMEM((lon, 128), F32),
             pltpu.VMEM((lon, COLS), BF),
-            pltpu.VMEM((lon, COLS), F32),
+            pltpu.VMEM((2, lon, COLS), F32),
             pltpu.VMEM((STEPS * SLOTS, COLS), F32),
             pltpu.VMEM((2, 128, COLS), F32),
+            pltpu.VMEM((COLS, lon), BF),
+            pltpu.VMEM((lon, 128), F32),
+            pltpu.SemaphoreType.DMA((3,)),
         ],
     )(flux_in, zonal_t, zonal, couple, ocean0, shrink)
     ocean_coef = ocean_coef.reshape(STEPS, SLOTS, COLS)
     air_coefficients_end = call(
         unpack_kernel,
-        vmem(1),
+        anywhere(1),
         shape((LEVELS * LAT, COLS), F32),
-        [pltpu.VMEM((WAVES * 16, 128), F32), pltpu.VMEM((2, LEVELS * LAT, 128), F32)],
+        [
+            pltpu.VMEM((WAVES * 16, 128), F32),
+            pltpu.VMEM((2, LEVELS * LAT, 128), F32),
+            pltpu.VMEM((WAVES, 16, 128), BF),
+            pltpu.SemaphoreType.DMA,
+        ],
     )(back).reshape(1, LEVELS, LAT, COLS)
 
     up = [(i, i + 1) for i in range(BANDS - 1)]

time: 127 us -> 126 us (level)
  Pallas kernels: 53.1 us -> 51.6 us
    pallas_call x3, Pallas kernels: 36.5 us -> 35 us  [the longest x1 20.9 us: per_device(): call(atmosphere_kernel, vmem(1) + anywhere(1) + vmem(1) + anywhere(2), sh...]
where the time goes in v6:
time: 126 us
  Pallas kernels  51.6 us (41%)
  waiting for transfers between devices  35.8 us (28%)
  starting transfers between devices  27.7 us (22%)
  local copies, waits for them, and re-layouts  4.13 us (3%)
  other arithmetic  3.95 us (3%)
  between operations  1.55 us (1%)
    pallas_call x1, Pallas kernels, per_device(): call(atmosphere_kernel, vmem(1) + anywhere(1) + vmem(1) + anywhere(2), sh...  20.9 us
    ppermute x3, waiting for transfers between devices, per_device(): lax.ppermute(sent, 'lev', [(i, (i + d) % FIELDS) for i in range(FIELDS)])  19.3 us
    all_to_all x1, waiting for transfers between devices, per_device(): got = lax.all_to_all(chunks, AXES, 0, 0, tiled=True)  11.7 us
    pallas_call x1, Pallas kernels, per_device(): call(ocean_kernel, vmem(2) + anywhere(1) + vmem(1) + anywhere(2), (shape(...  11.4 us
    all_to_all x1, starting transfers between devices, per_device(): got = lax.all_to_all(chunks, AXES, 0, 0, tiled=True)  10.8 us
    pallas_call x1, Pallas kernels, per_device(): call(operator_kernel, smem(1) + [pl.BlockSpec(memory_space=pl.ANY)], shap...  8.73 us
    all_to_all x1, starting transfers between devices, per_device(): back = lax.all_to_all(out, AXES, 0, 0, tiled=True)  5.38 us
    ppermute x3, starting transfers between devices, per_device(): lax.ppermute(sent, 'lev', [(i, (i + d) % FIELDS) for i in range(FIELDS)])  4.95 us
  transfers between devices with their start and end apart: 8, of which 4 were waited for; matrix products, arithmetic and copies ran while one was open for 3% of the time, Pallas kernels for 12%

profile of v6, /device:TPU:7, one launch (start us, length us, event | category | flops | bytes accessed | tf_op | source)
XLA Modules:
  0.0 125.7 jit_solution(8862665606897555220)
XLA Ops:
  1.3 4.1 %shard_map.175 = bf16[128,40,128]{2,1,0:T(8,128)(2,1)} custom-call(s32[1]{0:T(128)S(6)} %copy.29.live_ref, f32[640,256]{1,0:T(8,128)} %bitcast.48, f32[480,256]{1,0:T(8,128)} %bitcast.50, f32[256,40]{1,0:T(8,128)} %bitcast.51, f32[1,40]{1,0:T(1,128)} %bitcast.52, f32[1,40]{1,0:T(1,128)} %k_ref.1, s32[1,32]{1,0:T(1,128)} %bitcast.53, f32[1,32]{1,0:T(1,128)} %bitcast.54, ...), custom_call_target="tpu_custom_call" | custom-call | tf_op jit(solution)/shard_map/pallas_call | solution.py:460
  5.4 10.8 %all-to-all-start = ((bf16[128,40,128]{2,1,0:T(8,128)(2,1)}), bf16[128,40,128]{2,1,0:T(8,128)(2,1)S(1)}, u32[]{:S(2)}, u32[]{:S(2)}) async-start(bf16[128,40,128]{2,1,0:T(8,128)(2,1)} %shard_map.175), calls=%async_computation | async-start | bytes 2621440 | tf_op jit(solution)/shard_map/all_to_all | solution.py:476
  16.2 8.7 %shard_map.176.p_any = bf16[1280,1280]{1,0:T(8,128)(2,1)} custom-call(s32[128]{0:T(128)} %wave_ref.1, bf16[4,32,5,8,1280]{4,3,2,1,0:T(8,128)(2,1)} %bitcast.40), custom_call_target="tpu_custom_call" | custom-call | tf_op jit(solution)/shard_map/pallas_call | solution.py:478
  25.0 11.7 %all-to-all-done = bf16[128,40,128]{2,1,0:T(8,128)(2,1)S(1)} async-done(((bf16[128,40,128]{2,1,0:T(8,128)(2,1)}), bf16[128,40,128]{2,1,0:T(8,128)(2,1)S(1)}, u32[]{:S(2)}, u32[]{:S(2)}) %all-to-all-start) | async-done | bytes 1310752 | tf_op jit(solution)/shard_map/all_to_all | solution.py:476
  36.7 0.3 copy.28
  37.1 0.0 copy-start.1
  37.1 0.1 slice_bitcast_fusion
  37.2 0.5 collective-permute-start
  37.7 0.4 broadcast_and_fusion.1
  38.1 0.9 add_convert_fusion.sx_ref
  39.0 0.0 copy-done.1
  39.0 1.5 %fusion.se_any = bf16[640,1024]{1,0:T(8,128)(2,1)} fusion(s32[1024]{0:T(1024)S(1)} %fusion.41), kind=kLoop, calls=%fused_computation.1 | loop fusion | flops 1310720 | bytes 1314816 | tf_op jit(solution)/shard_map/convert_element_type | solution.py:436
  40.5 0.0 collective-permute-done.h_any
  40.5 0.9 copy-done.2
  41.4 20.9 %shard_map.177 = bf16[128,40,128]{2,1,0:T(8,128)(2,1)} custom-call(bf16[5,4,256,128]{3,2,1,0:T(8,128)(2,1)} %bitcast.42, bf16[3,4,256,128]{3,2,1,0:T(8,128)(2,1)} %copy-done.2, bf16[2,256,512]{2,1,0:T(8,128)(2,1)} %add_convert_fusion.sx_ref, bf16[640,1024]{1,0:T(8,128)(2,1)} %fusion.se_any, bf16[1280,1280]{1,0:T(8,128)(2,1)} %shard_map.176.p_any), custom_call_target="tpu_custom_call" | custom-call | tf_op jit(solution)/shard_map/pallas_call | solution.py:517
  62.4 0.0 copy-start.3
  62.4 0.0 copy-start.4
  62.4 0.0 copy-start.8
  62.4 0.0 copy-start.9
  62.4 5.4 %all-to-all-start.1 = ((bf16[128,40,128]{2,1,0:T(8,128)(2,1)}), bf16[128,40,128]{2,1,0:T(8,128)(2,1)S(1)}, u32[]{:S(2)}, u32[]{:S(2)}) async-start(bf16[128,40,128]{2,1,0:T(8,128)(2,1)} %shard_map.177), calls=%async_computation.1 | async-start | bytes 2621440 | tf_op jit(solution)/shard_map/all_to_all | solution.py:535
  67.8 0.0 copy-done.3
  67.8 0.0 copy-done.4
  67.9 1.3 %collective-permute-start.1 = (bf16[64,1440]{1,0:T(8,128)(2,1)S(1)}, bf16[64,1440]{1,0:T(8,128)(2,1)S(1)}, u32[]{:S(2)}, u32[]{:S(2)}) collective-permute-start(bf16[64,1440]{1,0:T(8,128)(2,1)S(1)} %pad_maximum_fusion), channel_id=1, source_target_pairs={{0,1},{1,2},{2,3},{3,0},{4,5},{5,6},{6,7},{7,4},{8,9},{9,10},{10,1... | collective-permute-start | bytes 552968 | tf_op jit(solution)/shard_map/ppermute | solution.py:501
  69.2 2.5 %collective-permute-start.2 = (bf16[64,1440]{1,0:T(8,128)(2,1)S(1)}, bf16[64,1440]{1,0:T(8,128)(2,1)S(1)}, u32[]{:S(2)}, u32[]{:S(2)}) collective-permute-start(bf16[64,1440]{1,0:T(8,128)(2,1)S(1)} %pad_maximum_fusion), channel_id=1, source_target_pairs={{0,2},{1,3},{2,0},{3,1},{4,6},{5,7},{6,4},{7,5},{8,10},{9,11},{10,... | collective-permute-start | bytes 552968 | tf_op jit(solution)/shard_map/ppermute | solution.py:501
  71.7 1.1 collective-permute-start.3
  72.9 0.0 copy-done.8
  72.9 1.0 sine_select_fusion.a_ref
  73.9 0.0 copy-done.9
  73.9 15.1 %collective-permute-done.1.o1 = bf16[64,1440]{1,0:T(8,128)(2,1)S(1)} collective-permute-done((bf16[64,1440]{1,0:T(8,128)(2,1)S(1)}, bf16[64,1440]{1,0:T(8,128)(2,1)S(1)}, u32[]{:S(2)}, u32[]{:S(2)}) %collective-permute-start.1) | collective-permute-done | bytes 184352 | tf_op jit(solution)/shard_map/ppermute | solution.py:501
  89.1 4.2 %collective-permute-done.2.o2 = bf16[64,1440]{1,0:T(8,128)(2,1)S(1)} collective-permute-done((bf16[64,1440]{1,0:T(8,128)(2,1)S(1)}, bf16[64,1440]{1,0:T(8,128)(2,1)S(1)}, u32[]{:S(2)}, u32[]{:S(2)}) %collective-permute-start.2) | collective-permute-done | bytes 184352 | tf_op jit(solution)/shard_map/ppermute | solution.py:501
  93.3 0.0 collective-permute-done.3.o3
  93.3 0.7 copy-done.6
  94.0 0.1 copy-done.7
  94.0 3.7 %shard_map.179 = (bf16[1440,256]{1,0:T(8,128)(2,1)}, bf16[256,1440]{1,0:T(8,128)(2,1)}, f32[1440,128]{1,0:T(8,128)}, f32[1440,128]{1,0:T(8,128)}, bf16[256,128]{1,0:T(8,128)(2,1)}) custom-call(f32[4,4]{1,0:T(4,128)} %c_ref.1, f32[160,128]{1,0:T(8,128)} %sine_select_fusion.a_ref, f32[32,1440]{1,0:T(8,128)} %bitcast.46, f32[32,1440]{1,0:T(8,128)} %bitcast.47, ...), custom_call_target="tpu_custom_call" | custom-call | tf_op jit(solution)/shard_map/pallas_call | solution.py:502
  97.7 0.0 all-to-all-done.1.b_any
  97.7 0.1 slice.21
  97.8 0.2 copy.23
  98.0 0.8 copy-done
  98.8 1.0 copy.24
  99.8 11.4 %shard_map.180 = (f32[32,1440]{1,0:T(8,128)}, bf16[384,256]{1,0:T(8,128)(2,1)}) custom-call(bf16[12,256,128]{2,1,0:T(8,128)(2,1)} %bitcast.45, bf16[1440,256]{1,0:T(8,128)(2,1)} %get-tuple-element.10.zt_ref, bf16[256,1440]{1,0:T(8,128)(2,1)} %get-tuple-element.11.z_any, bf16[256,128]{1,0:T(8,128)(2,1)} %get-tuple-element.12.c_ref, ...), custom_call_target="tpu_custom_call" | custom-call | tf_op jit(solution)/shard_map/pallas_call | solution.py:537
  111.2 0.0 copy-start.10
  111.3 4.1 %collective-permute-start.4 = (bf16[12,32,256]{2,1,0:T(8,128)(2,1)}, bf16[12,32,256]{2,1,0:T(8,128)(2,1)S(1)}, u32[]{:S(2)}, u32[]{:S(2)}) collective-permute-start(bf16[12,32,256]{2,1,0:T(8,128)(2,1)} %bitcast.56), channel_id=1, source_target_pairs={{0,4},{4,8},{8,12},{12,16},{16,20},{20,24},{24,28},{28,32},{32,36}... | collective-permute-start | bytes 589832 | tf_op jit(solution)/shard_map/ppermute | solution.py:567
  115.4 1.9 %collective-permute-start.5 = (bf16[12,32,256]{2,1,0:T(8,128)(2,1)}, bf16[12,32,256]{2,1,0:T(8,128)(2,1)S(1)}, u32[]{:S(2)}, u32[]{:S(2)}) collective-permute-start(bf16[12,32,256]{2,1,0:T(8,128)(2,1)} %bitcast.57), channel_id=1, source_target_pairs={{4,0},{8,4},{12,8},{16,12},{20,16},{24,20},{28,24},{32,28},{36,32}... | collective-permute-start | bytes 589832 | tf_op jit(solution)/shard_map/ppermute | solution.py:568
  117.3 2.7 %shard_map.178 = f32[640,256]{1,0:T(8,128)} custom-call(bf16[128,40,128]{2,1,0:T(8,128)(2,1)} %copy-done), custom_call_target="tpu_custom_call" | custom-call | tf_op jit(solution)/shard_map/pallas_call | solution.py:553
  120.0 0.0 collective-permute-done.4
  120.0 4.7 %collective-permute-done.5 = bf16[12,32,256]{2,1,0:T(8,128)(2,1)S(1)} collective-permute-done((bf16[12,32,256]{2,1,0:T(8,128)(2,1)}, bf16[12,32,256]{2,1,0:T(8,128)(2,1)S(1)}, u32[]{:S(2)}, u32[]{:S(2)}) %collective-permute-start.5) | collective-permute-done | bytes 196640 | tf_op jit(solution)/shard_map/ppermute | solution.py:568
  124.7 0.0 copy-done.10
  124.7 1.1 convolution_bitcast_fusion
  (21 shorter events, 0.1 us)
Async XLA Ops:
  5.4 31.3 %all-to-all-start = ((bf16[128,40,128]{2,1,0:T(8,128)(2,1)}), bf16[128,40,128]{2,1,0:T(8,128)(2,1)S(1)}, u32[]{:S(2)}, u32[]{:S(2)}) async-start(bf16[128,40,128]{2,1,0:T(8,128)(2,1)} %shard_map.175), calls=%async_computation | async-start | bytes 2621440 | tf_op jit(solution)/shard_map/all_to_all | solution.py:476
  37.1 1.9 %copy-start.1 = (bf16[32,4,5,8,128]{4,3,0,1,2:T(8,128)(2,1)}, bf16[32,4,5,8,128]{4,3,0,1,2:T(8,128)(2,1)S(1)}, u32[]{:S(2)}) copy-start(bf16[32,4,5,8,128]{4,3,0,1,2:T(8,128)(2,1)S(1)} %copy.28) | copy-start | bytes 3932164
  37.2 3.3 %collective-permute-start = (bf16[3,4,256,128]{3,2,1,0:T(8,128)(2,1)S(1)}, bf16[3,4,256,128]{3,2,1,0:T(8,128)(2,1)S(1)}, u32[]{:S(2)}, u32[]{:S(2)}) collective-permute-start(bf16[3,4,256,128]{3,2,1,0:T(8,128)(2,1)S(1)} %slice_bitcast_fusion), channel_id=1, source_target_pairs={{0,4},{4,0},{8,12},{12,8},{16,20},{20,16},{24,28},{28,24},{32,36},... | collective-permute-start | bytes 2359304 | tf_op jit(solution)/shard_map/ppermute | solution.py:516
  40.5 0.9 copy-start.2
  62.4 5.4 %copy-start.3 = (f32[1,32,1440]{2,1,0:T(8,128)S(1)}, f32[1,32,1440]{2,1,0:T(8,128)}, u32[]{:S(2)}) copy-start(f32[1,32,1440]{2,1,0:T(8,128)} %param.23) | copy-start | bytes 552964
  62.4 5.4 %copy-start.4 = (f32[1,32,1440]{2,1,0:T(8,128)S(1)}, f32[1,32,1440]{2,1,0:T(8,128)}, u32[]{:S(2)}) copy-start(f32[1,32,1440]{2,1,0:T(8,128)} %param.24) | copy-start | bytes 552964
  62.4 10.5 %copy-start.8 = (s32[128]{0:T(128)S(1)}, s32[128]{0:T(128)}, u32[]{:S(2)}) copy-start(s32[128]{0:T(128)} %wave_ref.1) | copy-start | bytes 1540
  62.4 11.5 %copy-start.9 = (s32[2,40]{1,0:T(2,128)S(1)}, s32[2,40]{1,0:T(2,128)}, u32[]{:S(2)}) copy-start(s32[2,40]{1,0:T(2,128)} %param.29) | copy-start | bytes 964
  62.4 35.3 %all-to-all-start.1 = ((bf16[128,40,128]{2,1,0:T(8,128)(2,1)}), bf16[128,40,128]{2,1,0:T(8,128)(2,1)S(1)}, u32[]{:S(2)}, u32[]{:S(2)}) async-start(bf16[128,40,128]{2,1,0:T(8,128)(2,1)} %shard_map.177), calls=%async_computation.1 | async-start | bytes 2621440 | tf_op jit(solution)/shard_map/all_to_all | solution.py:535
  67.9 21.2 %collective-permute-start.1 = (bf16[64,1440]{1,0:T(8,128)(2,1)S(1)}, bf16[64,1440]{1,0:T(8,128)(2,1)S(1)}, u32[]{:S(2)}, u32[]{:S(2)}) collective-permute-start(bf16[64,1440]{1,0:T(8,128)(2,1)S(1)} %pad_maximum_fusion), channel_id=1, source_target_pairs={{0,1},{1,2},{2,3},{3,0},{4,5},{5,6},{6,7},{7,4},{8,9},{9,10},{10,1... | collective-permute-start | bytes 552968 | tf_op jit(solution)/shard_map/ppermute | solution.py:501
  69.2 24.1 %collective-permute-start.2 = (bf16[64,1440]{1,0:T(8,128)(2,1)S(1)}, bf16[64,1440]{1,0:T(8,128)(2,1)S(1)}, u32[]{:S(2)}, u32[]{:S(2)}) collective-permute-start(bf16[64,1440]{1,0:T(8,128)(2,1)S(1)} %pad_maximum_fusion), channel_id=1, source_target_pairs={{0,2},{1,3},{2,0},{3,1},{4,6},{5,7},{6,4},{7,5},{8,10},{9,11},{10,... | collective-permute-start | bytes 552968 | tf_op jit(solution)/shard_map/ppermute | solution.py:501
  71.7 21.6 %collective-permute-start.3 = (bf16[64,1440]{1,0:T(8,128)(2,1)S(1)}, bf16[64,1440]{1,0:T(8,128)(2,1)S(1)}, u32[]{:S(2)}, u32[]{:S(2)}) collective-permute-start(bf16[64,1440]{1,0:T(8,128)(2,1)S(1)} %pad_maximum_fusion), channel_id=1, source_target_pairs={{0,3},{1,0},{2,1},{3,2},{4,7},{5,4},{6,5},{7,6},{8,11},{9,8},{10,9... | collective-permute-start | bytes 552968 | tf_op jit(solution)/shard_map/ppermute | solution.py:501
  89.1 4.2 %copy-start.5 = (bf16[64,1440]{1,0:T(8,128)(2,1)}, bf16[64,1440]{1,0:T(8,128)(2,1)S(1)}, u32[]{:S(2)}) copy-start(bf16[64,1440]{1,0:T(8,128)(2,1)S(1)} %collective-permute-done.1.o1) | copy-start | bytes 552964
  93.3 0.7 copy-start.6
  93.3 0.7 copy-start.7
  97.7 1.1 copy-start
  99.8 17.5 %copy-start.11 = (f32[40]{0:T(128)S(1)}, f32[40]{0:T(128)}, u32[]{:S(2)}) copy-start(f32[40]{0:T(128)} %param.30) | copy-start | bytes 484
  111.2 13.4 %copy-start.10 = (bf16[384,256]{1,0:T(8,128)(2,1)S(1)}, bf16[384,256]{1,0:T(8,128)(2,1)}, u32[]{:S(2)}) copy-start(bf16[384,256]{1,0:T(8,128)(2,1)} %get-tuple-element.16) | copy-start | bytes 589828
  111.3 8.7 %collective-permute-start.4 = (bf16[12,32,256]{2,1,0:T(8,128)(2,1)}, bf16[12,32,256]{2,1,0:T(8,128)(2,1)S(1)}, u32[]{:S(2)}, u32[]{:S(2)}) collective-permute-start(bf16[12,32,256]{2,1,0:T(8,128)(2,1)} %bitcast.56), channel_id=1, source_target_pairs={{0,4},{4,8},{8,12},{12,16},{16,20},{20,24},{24,28},{28,32},{32,36}... | collective-permute-start | bytes 589832 | tf_op jit(solution)/shard_map/ppermute | solution.py:567
  115.4 9.3 %collective-permute-start.5 = (bf16[12,32,256]{2,1,0:T(8,128)(2,1)}, bf16[12,32,256]{2,1,0:T(8,128)(2,1)S(1)}, u32[]{:S(2)}, u32[]{:S(2)}) collective-permute-start(bf16[12,32,256]{2,1,0:T(8,128)(2,1)} %bitcast.57), channel_id=1, source_target_pairs={{4,0},{8,4},{12,8},{16,12},{20,16},{24,20},{28,24},{32,28},{36,32}... | collective-permute-start | bytes 589832 | tf_op jit(solution)/shard_map/ppermute | solution.py:568
